TPU v7x, 256 devices: a whole 4x4x8 slice. The times are simulated.
256 devices in a mesh: subj: 16 (over z, core), vox: 16 (over y, x).
Axes of the slice: x: 4, y: 4, z: 8, core: 2. Of those that a mesh axis runs over, the one named last changes fastest.
Arguments:
- data: bfloat16 [32, 240, 65536], P('subj', None, 'vox'), may hold values from -40 to 40, as said below
- shared_start: bfloat16 [128, 240], replicated, may hold values from -6 to 6
Outputs:
- projections: float32 [32, 128, 240], P('subj')
- response: float32 [128, 240], replicated
Inputs may be any that keep to these rules, and one draw needn't show every extreme that they name: `data`: real-valued recordings.
All inputs are finite; a program needn't handle non-finite values.
Results may differ from a plain program's by a relative error of at most 0.00035.
The roundings to bfloat16 on the way count: a program that leaves them out, or rounds other values in their place, can miss the bound.
Values may be sent and summed in bfloat16 or wider, within the bound.
No kernel may reach another device: no remote copies, remote signals or barrier semaphores. Data moves between devices by JAX's collectives and lax.ppermute only.
A program may use at most 64 MiB of HBM per device.

v0:
```python
import jax
import jax.numpy as jnp
from jax import lax
from jax.sharding import PartitionSpec as P

ITERS = 3
OUTER = 2


def from_everyone(shard, axis):
    peers = lax.axis_size(axis)
    return lax.all_to_all(
        jnp.broadcast_to(shard[None], (peers, *shard.shape)), axis, 0, 0, tiled=True
    )


def taken_together(shard, axis):
    everything = from_everyone(shard, axis)
    return jnp.sum(everything, axis=0)


def in_order(pieces, dim):
    pieces = jnp.moveaxis(pieces, 0, dim)
    shape = pieces.shape
    return pieces.reshape(*shape[:dim], shape[dim] * shape[dim + 1], *shape[dim + 2 :])


def one_gather(arrays, axis, dims):
    ravelled = jnp.concatenate([a.reshape(-1) for a in arrays])
    lines, at, gathered = (lax.all_gather(ravelled, axis), 0, [])
    for a, dim in zip(arrays, dims):
        pieces = lines[:, at : at + a.size].reshape(-1, *a.shape)
        gathered.append(in_order(pieces, dim))
        at += a.size
    return tuple(gathered)


def rows_for(lines, peers):
    spare = -lines.shape[0] % peers
    if not spare:
        return lines
    return jnp.concatenate([lines, jnp.zeros((spare, *lines.shape[1:]), lines.dtype)])


def gathered_copies(shard, axis, dim):
    return in_order(from_everyone(shard, axis), dim)


def split_up(shard, dim, peers):
    shape = shard.shape
    pieces = shard.reshape(*shape[:dim], peers, shape[dim] // peers, *shape[dim + 1 :])
    return jnp.moveaxis(pieces, dim, 0)


def sent_and_summed(shard, axis, dim):
    peers = lax.axis_size(axis)
    pieces = lax.all_to_all(split_up(shard, dim, peers), axis, 0, 0, tiled=True)
    return jnp.sum(pieces, axis=0)


def total_of(shard, axes):
    lines = shard.reshape(-1, shard.shape[-1])
    padded = rows_for(lines, lax.axis_size(axes))
    whole = gathered_copies(sent_and_summed(padded, axes, 0), axes, 0)
    return lax.slice_in_dim(whole, 0, len(lines)).reshape(shard.shape)


def polar_factor(first, squares):
    features = first.shape[1]
    identity = jnp.broadcast_to(jnp.eye(features, dtype=jnp.float32), first.shape)
    factor = identity
    for count in range(ITERS):
        inner = jnp.einsum("sik,sij->skj", factor, first, precision=lax.Precision.HIGHEST)
        gram = (
            jnp.einsum("skj,sjl->skl", inner, factor, precision=lax.Precision.HIGHEST)
            / squares[:, None, None]
        )
        factor = jnp.einsum(
            "sik,skj->sij", factor, 1.5 * identity - 0.5 * gram, precision=lax.Precision.HIGHEST
        )
    return factor


def from_frames(frame_gram, shared):
    subjects = frame_gram.shape[0] * lax.axis_size("subj")
    frames = frame_gram.shape[1]
    width = frames // lax.axis_size("vox")
    start = lax.axis_index("vox") * width
    shared_wide = shared.astype(jnp.float32)
    left = jnp.einsum("kt,stu->sku", shared_wide, frame_gram, precision=lax.Precision.HIGHEST)
    first = jnp.einsum("sku,ju->skj", left, shared_wide, precision=lax.Precision.HIGHEST)
    squares = jnp.trace(first, axis1=1, axis2=2) + 1e-06
    factor = polar_factor(first, squares)
    left_share = lax.dynamic_slice_in_dim(left, start, width, 2)
    share = (
        jnp.einsum("sik,sit->skt", factor, left_share, precision=lax.Precision.HIGHEST)
        / jnp.sqrt(squares)[:, None, None]
    )
    total = taken_together(jnp.sum(share, axis=0), "subj") / jnp.float32(subjects)
    projections, response = one_gather((share, total), "vox", (2, 1))
    return (projections, response)


def local(data, shared_start):
    shared = shared_start
    projections = None
    response = None
    frame_gram = total_of(
        jnp.einsum("stv,suv->stu", data, data, preferred_element_type=jnp.float32), "vox"
    )
    for outer in range(OUTER):
        projections, response = from_frames(frame_gram, shared)
        shared = response.astype(jnp.bfloat16)
    return (projections, response)


def solution(mesh):
    placed = (P("subj", None, "vox"), P())
    return jax.shard_map(
        local, mesh=mesh, in_specs=placed, out_specs=(P("subj", None, None), P()), check_vma=False
    )
```

profile of v0, /device:TPU:2, one launch (start us, length us, event | category | flops | bytes accessed | tf_op | source)
XLA Modules:
  0.0 129.6 jit_solution(2602082858228522722)
XLA Ops:
  0.6 4.5 %fusion.39 = f32[2,240,240]{2,1,0:T(8,128)S(1)} fusion(bf16[2,240,4096]{2,1,0:T(8,128)(2,1)} %param.2), kind=kOutput, calls=%fused_computation.59 | convolution fusion | flops 943718400 | bytes 4392960 | tf_op jit(solution)/shard_map/stv,suv->stu/dot_general | solution.py:109
  5.2 17.4 %all_to_all.20 = f32[16,30,240]{2,1,0:T(8,128)S(1)} all-to-all(f32[16,30,240]{2,1,0:T(8,128)S(1)} %reshape_reshape.6), channel_id=1, replica_groups=mesh['subj'=16,'vox'=16] {'vox'}, dimensions={0} | all-to-all | bytes 921600 | tf_op jit(solution)/shard_map/all_to_all | solution.py:57
  22.7 0.8 broadcast_in_dim.67
  23.6 4.8 %all-to-all-start.1 = ((f32[16,30,240]{2,1,0:T(8,128)}), f32[16,30,240]{2,1,0:T(8,128)S(1)}, u32[]{:S(2)}, u32[]{:S(2)}) async-start(f32[16,30,240]{2,1,0:T(8,128)} %broadcast_in_dim.67), calls=%async_computation.1 | async-start | bytes 1048576 | tf_op jit(solution)/shard_map/all_to_all | solution.py:12
  28.5 9.1 %all-to-all-done.1 = f32[16,30,240]{2,1,0:T(8,128)S(1)} async-done(((f32[16,30,240]{2,1,0:T(8,128)}), f32[16,30,240]{2,1,0:T(8,128)S(1)}, u32[]{:S(2)}, u32[]{:S(2)}) %all-to-all-start.1) | async-done | bytes 460832 | tf_op jit(solution)/shard_map/all_to_all | solution.py:12
  37.7 0.6 fusion.27
  38.3 0.5 select_reduce_fusion.1
  38.8 0.4 fusion.24
  39.2 0.3 fusion.11
  39.7 0.4 fusion.40
  40.7 0.4 fusion.42
  41.9 0.7 broadcast_in_dim.70
  42.5 8.6 %all-to-all-start.2 = ((f32[16,128,15]{1,2,0:T(8,128)}), f32[16,128,15]{1,2,0:T(8,128)S(1)}, u32[]{:S(2)}, u32[]{:S(2)}) async-start(f32[16,128,15]{1,2,0:T(8,128)} %broadcast_in_dim.70), calls=%async_computation.2 | async-start | bytes 262144 | tf_op jit(solution)/shard_map/all_to_all | solution.py:12
  51.5 8.3 %all-to-all-done.2 = f32[16,128,15]{1,2,0:T(8,128)S(1)} async-done(((f32[16,128,15]{1,2,0:T(8,128)}), f32[16,128,15]{1,2,0:T(8,128)S(1)}, u32[]{:S(2)}, u32[]{:S(2)}) %all-to-all-start.2) | async-done | bytes 122912 | tf_op jit(solution)/shard_map/all_to_all | solution.py:12
  60.2 22.3 %all-gather.2 = bf16[16,1,5760]{2,1,0:T(2,128)(2,1)S(1)} all-gather(bf16[1,1,5760]{2,1,0:T(2,128)(2,1)S(1)} %reshape.59), channel_id=2, replica_groups=mesh['subj'=16,'vox'=16] {'vox'}, dimensions={0}, use_global_device_ids=true | all-gather | bytes 195840 | tf_op jit(solution)/shard_map/all_gather | solution.py:30
  82.5 1.0 convert_element_type.33
  83.8 0.6 fusion.44
  84.5 0.5 select_reduce_fusion
  84.9 0.4 fusion.19
  85.3 0.3 fusion.5
  85.9 0.4 fusion.45
  86.8 0.4 fusion.47
  88.0 0.7 broadcast_in_dim.71
  88.7 3.5 %all-to-all-start.3 = ((f32[16,128,15]{1,2,0:T(8,128)}), f32[16,128,15]{1,2,0:T(8,128)S(1)}, u32[]{:S(2)}, u32[]{:S(2)}) async-start(f32[16,128,15]{1,2,0:T(8,128)} %broadcast_in_dim.71), calls=%async_computation.3 | async-start | bytes 262144 | tf_op jit(solution)/shard_map/all_to_all | solution.py:12
  92.5 8.3 %all-to-all-done.3 = f32[16,128,15]{1,2,0:T(8,128)S(1)} async-done(((f32[16,128,15]{1,2,0:T(8,128)}), f32[16,128,15]{1,2,0:T(8,128)S(1)}, u32[]{:S(2)}, u32[]{:S(2)}) %all-to-all-start.3) | async-done | bytes 122912 | tf_op jit(solution)/shard_map/all_to_all | solution.py:12
  101.2 22.8 %all-gather.3 = f32[16,1,5760]{2,1,0:T(1,128)S(1)} all-gather(f32[1,1,5760]{2,1,0:T(1,128)S(1)} %reshape.61), channel_id=3, replica_groups=mesh['subj'=16,'vox'=16] {'vox'}, dimensions={0}, use_global_device_ids=true | all-gather | bytes 391680 | tf_op jit(solution)/shard_map/all_gather | solution.py:30
  124.1 0.9 reshape.55
  125.0 0.3 copy.40
  125.3 0.7 reshape.56
  126.0 2.2 %reshape.53 = f32[16,2,128,15]{3,2,1,0:T(8,128)S(1)} reshape(f32[16,3840]{1,0:T(8,128)S(1)} %slice.13) | data formatting | bytes 491520 | tf_op jit(solution)/shard_map/reshape | solution.py:32
  128.2 0.6 copy.39
  128.9 0.7 copy.41
  (45 shorter events, 5.2 us)
Async XLA Ops:
  0.6 37.0 %copy-start = (bf16[128,240]{0,1:T(8,128)(2,1)S(1)}, bf16[128,240]{0,1:T(8,128)(2,1)}, u32[]{:S(2)}) copy-start(bf16[128,240]{0,1:T(8,128)(2,1)} %param.3) | copy-start | bytes 184324
  23.6 14.0 %all-to-all-start.1 = ((f32[16,30,240]{2,1,0:T(8,128)}), f32[16,30,240]{2,1,0:T(8,128)S(1)}, u32[]{:S(2)}, u32[]{:S(2)}) async-start(f32[16,30,240]{2,1,0:T(8,128)} %broadcast_in_dim.67), calls=%async_computation.1 | async-start | bytes 1048576 | tf_op jit(solution)/shard_map/all_to_all | solution.py:12
  42.5 17.2 %all-to-all-start.2 = ((f32[16,128,15]{1,2,0:T(8,128)}), f32[16,128,15]{1,2,0:T(8,128)S(1)}, u32[]{:S(2)}, u32[]{:S(2)}) async-start(f32[16,128,15]{1,2,0:T(8,128)} %broadcast_in_dim.70), calls=%async_computation.2 | async-start | bytes 262144 | tf_op jit(solution)/shard_map/all_to_all | solution.py:12
  88.7 12.1 %all-to-all-start.3 = ((f32[16,128,15]{1,2,0:T(8,128)}), f32[16,128,15]{1,2,0:T(8,128)S(1)}, u32[]{:S(2)}, u32[]{:S(2)}) async-start(f32[16,128,15]{1,2,0:T(8,128)} %broadcast_in_dim.71), calls=%async_computation.3 | async-start | bytes 262144 | tf_op jit(solution)/shard_map/all_to_all | solution.py:12
where the time goes:
time: 130 us
  blocking collectives  62.5 us (48%)
  waiting for transfers between devices  25.7 us (20%)
  starting transfers between devices  16.9 us (13%)
  matrix products  12.7 us (10%)
  local copies, waits for them, and re-layouts  10.6 us (8%)
    all_gather x2, blocking collectives, one_gather(): lines, at, gathered = (lax.all_gather(ravelled, axis), 0, [])  45.1 us
    all_to_all x3, waiting for transfers between devices, from_everyone(): lax.all_to_all(jnp.broadcast_to(shard[None], (peers, *shard.shape)), axis...  25.7 us
    all_to_all x1, blocking collectives, sent_and_summed(): pieces = lax.all_to_all(split_up(shard, dim, peers), axis, 0, 0, tiled=True)  17.4 us
    all_to_all x3, starting transfers between devices, from_everyone(): lax.all_to_all(jnp.broadcast_to(shard[None], (peers, *shard.shape)), axis...  16.9 us
    dot_general x1, matrix products, local(): jnp.einsum('stv,suv->stu', data, data, preferred_element_type=jnp.float32)  4.53 us
    reshape x2, local copies, waits for them, and re-layouts, one_gather(): pieces = lines[:, at:at + a.size].reshape(-1, *a.shape)  3.14 us
  transfers between devices with their start and end apart: 3, of which 3 were waited for; matrix products, arithmetic and copies ran while one was open for 1% of the time, Pallas kernels for 0%

commit v1 on v0

v1 whole, which is shorter than its diff:
```python
import jax
import jax.numpy as jnp
from jax import lax
from jax.experimental import pallas as pl
from jax.experimental.pallas import tpu as pltpu
from jax.sharding import PartitionSpec as P

ITERS = 3
OUTER = 2
LANES = 128
HIGHEST = lax.Precision.HIGHEST


def padded(frames):
    return -(-frames // (2 * LANES)) * 2 * LANES


def positions(size):
    rows = lax.broadcasted_iota(jnp.int32, (size, size), 0)
    cols = lax.broadcasted_iota(jnp.int32, (size, size), 1)
    return rows, cols


def gram_kernel(data_ref, packed_ref, sums_ref):
    step = pl.program_id(0)
    frames = data_ref.shape[1]
    size = packed_ref.shape[1]

    @pl.when(step == 0)
    def _():
        sums_ref[...] = jnp.zeros_like(sums_ref)

    for subject in range(2):
        block = data_ref[subject]
        sums_ref[subject] += lax.dot_general(
            block, block, (((1,), (1,)), ((), ())), preferred_element_type=jnp.float32
        )

    @pl.when(step == pl.num_programs(0) - 1)
    def _():
        rows, cols = positions(frames)
        first, second = sums_ref[0], sums_ref[1]
        mixed = jnp.where(rows >= cols, first, second)
        diagonal = jnp.sum(jnp.where(rows == cols, second, 0.0), axis=1, keepdims=True)
        packed_ref[...] = jnp.zeros_like(packed_ref)
        packed_ref[0:frames, 0:frames] = mixed
        packed_ref[0:frames, frames : frames + 1] = diagonal


def packed_grams(data, size):
    subjects, frames, voxels = data.shape
    tile = 1024
    return pl.pallas_call(
        gram_kernel,
        grid=(voxels // tile,),
        in_specs=[pl.BlockSpec((subjects, frames, tile), lambda i: (0, 0, i))],
        out_specs=pl.BlockSpec((size, size), lambda i: (0, 0)),
        out_shape=jax.ShapeDtypeStruct((size, size), jnp.float32),
        scratch_shapes=[pltpu.VMEM((subjects, frames, frames), jnp.float32)],
        name="grams",
    )(data)


def in_three(x):
    high = x.astype(jnp.bfloat16)
    rest = x - high.astype(jnp.float32)
    middle = rest.astype(jnp.bfloat16)
    low = (rest - middle.astype(jnp.float32)).astype(jnp.bfloat16)
    return high, middle, low


def exact_right(x, y, dims):
    return sum(
        lax.dot_general(part, y, (dims, ((), ())), preferred_element_type=jnp.float32)
        for part in in_three(x)
    )


def exact_left(x, y, dims):
    return sum(
        lax.dot_general(x, part, (dims, ((), ())), preferred_element_type=jnp.float32)
        for part in in_three(y)
    )


def times(a, b):
    return jnp.dot(a, b, precision=HIGHEST, preferred_element_type=jnp.float32)


def refit(gram, shared):
    crossed = exact_right(gram, shared, ((1,), (0,)))
    first = exact_left(shared, crossed, ((0,), (0,)))
    features = first.shape[0]
    rows, cols = positions(features)
    eye = (rows == cols).astype(jnp.float32)
    square = jnp.sum(first * eye) + 1e-06
    current = first / square
    result = crossed / jnp.sqrt(square)
    for count in range(ITERS):
        step = 1.5 * eye - 0.5 * current
        result = times(result, step)
        if count < ITERS - 1:
            current = times(times(current, step), step)
    return result


def refit_body(frames, last, place_ref, packed_ref, shared_ref, share_ref, *refs):
    total_ref, wide_ref = refs[-2:]
    size = packed_ref.shape[0]
    rows, cols = positions(size)
    packed = packed_ref[...]
    diagonal = packed[:, frames : frames + 1]
    packed = jnp.where(cols < frames, packed, 0.0)
    flipped = packed.T
    grams = (
        jnp.where(rows >= cols, packed, flipped),
        jnp.where(rows == cols, diagonal, jnp.where(rows < cols, packed, flipped)),
    )
    wide_ref[...] = jnp.zeros_like(wide_ref)
    wide_ref[0:frames, :] = shared_ref[0:frames, :]
    shared = wide_ref[...]
    results = [refit(gram, shared) for gram in grams]
    if last:
        for subject in range(2):
            refs[0][subject] = results[subject][0:frames, :]
    total_ref[...] = results[0] + results[1]
    width = share_ref.shape[1]
    share = total_ref[pl.ds(pl.multiple_of(place_ref[0] * width, width), width), :]
    for peer in range(share_ref.shape[0]):
        share_ref[peer] = share


def refits(packed, shared, place, frames, peers, last):
    size = packed.shape[0]
    features = shared.shape[1]
    width = size // peers
    out = [jax.ShapeDtypeStruct((peers, width, features), jnp.float32)]
    if last:
        out.append(jax.ShapeDtypeStruct((2, frames, features), jnp.float32))

    def kernel(*refs):
        return refit_body(frames, last, *refs)

    return pl.pallas_call(
        kernel,
        in_specs=[
            pl.BlockSpec(memory_space=pltpu.SMEM),
            pl.BlockSpec(memory_space=pltpu.VMEM),
            pl.BlockSpec(memory_space=pltpu.VMEM),
        ],
        out_specs=[pl.BlockSpec(memory_space=pltpu.VMEM)] * len(out),
        out_shape=out,
        scratch_shapes=[
            pltpu.VMEM((size, features), jnp.float32),
            pltpu.VMEM((size, features), jnp.bfloat16),
        ],
        name="refits_last" if last else "refits",
    )(place, packed, shared)


def exchanged(pieces, axis):
    return lax.all_to_all(pieces, axis, 0, 0, tiled=True)


def to_everyone(shard, peers):
    return jnp.broadcast_to(shard[None], (peers, *shard.shape))


def local(data, shared_start):
    frames = data.shape[1]
    peers = lax.axis_size("vox")
    subjects = data.shape[0] * lax.axis_size("subj")
    size = padded(frames)
    place = lax.axis_index("vox").astype(jnp.int32).reshape(1)
    pieces = packed_grams(data, size).reshape(peers, size // peers, size)
    share = jnp.sum(exchanged(pieces, "vox"), axis=0)
    packed = exchanged(to_everyone(share, peers), "vox").reshape(size, size)
    shared = shared_start.T
    for outer in range(OUTER):
        last = outer == OUTER - 1
        out = refits(packed, shared, place, frames, peers, last)
        total = jnp.sum(exchanged(out[0], "subj"), axis=0) / jnp.float32(subjects)
        if not last:
            total = total.astype(jnp.bfloat16)
        shared = exchanged(to_everyone(total, peers), "vox").reshape(size, -1)
    projections = jnp.swapaxes(out[1], 1, 2)
    return (projections, shared[:frames].T)


def solution(mesh):
    placed = (P("subj", None, "vox"), P())
    return jax.shard_map(
        local, mesh=mesh, in_specs=placed, out_specs=(P("subj", None, None), P()), check_vma=False
    )
```

time: 130 us -> 98.5 us (0.76)
  the two profiles are of different devices: /device:TPU:2 before, /device:TPU:1 now
where the time goes in v1:
time: 98.5 us; the launch traced here: 97.9 us
  blocking collectives  69.2 us (70%)
  Pallas kernels  14.9 us (15%)
  waiting for transfers between devices  7.5 us (8%)
  starting transfers between devices  3.53 us (4%)
  local copies, waits for them, and re-layouts  2.09 us (2%)
    all_to_all x5, blocking collectives, exchanged(): return lax.all_to_all(pieces, axis, 0, 0, tiled=True)  69.2 us
    pallas_call x2, Pallas kernels, refits(): pl.pallas_call(kernel, in_specs=[pl.BlockSpec(memory_space=pltpu.SMEM), p...  10.2 us
    all_to_all x1, waiting for transfers between devices, exchanged(): return lax.all_to_all(pieces, axis, 0, 0, tiled=True)  7.5 us
    pallas_call x1, Pallas kernels, packed_grams(): pl.pallas_call(gram_kernel, grid=(voxels // tile,), in_specs=[pl.BlockSpe...  4.69 us
    all_to_all x1, starting transfers between devices, exchanged(): return lax.all_to_all(pieces, axis, 0, 0, tiled=True)  3.53 us
  transfers between devices with their start and end apart: 1, of which 1 were waited for; matrix products, arithmetic and copies ran while one was open for 0% of the time, Pallas kernels for 0%

profile of v1, /device:TPU:1, one launch (start us, length us, event | category | flops | bytes accessed | tf_op | source)
XLA Modules:
  0.0 97.9 jit_solution(12635390471508995784)
XLA Ops:
  0.6 4.7 %grams.1 = f32[256,256]{1,0:T(8,128)} custom-call(bf16[2,240,4096]{2,1,0:T(8,128)(2,1)} %data_ref.1), custom_call_target="tpu_custom_call" | custom-call | tf_op jit(solution)/shard_map/grams/pallas_call | solution.py:53
  5.3 15.1 %all_to_all.30 = f32[16,16,256]{2,1,0:T(8,128)S(1)} all-to-all(f32[16,16,256]{2,1,0:T(8,128)} %bitcast.11), channel_id=1, replica_groups=mesh['subj'=16,'vox'=16] {'vox'}, dimensions={0} | all-to-all | bytes 524288 | tf_op jit(solution)/shard_map/all_to_all | solution.py:162
  20.5 0.7 broadcast_in_dim.6
  21.2 3.5 %all-to-all-start.1 = ((f32[16,16,256]{2,1,0:T(8,128)}), f32[16,16,256]{2,1,0:T(8,128)S(1)}, u32[]{:S(2)}, u32[]{:S(2)}) async-start(f32[16,16,256]{2,1,0:T(8,128)} %broadcast_in_dim.6), calls=%async_computation.1 | async-start | bytes 524288 | tf_op jit(solution)/shard_map/all_to_all | solution.py:162
  24.7 7.5 %all-to-all-done.1 = f32[16,16,256]{2,1,0:T(8,128)S(1)} async-done(((f32[16,16,256]{2,1,0:T(8,128)}), f32[16,16,256]{2,1,0:T(8,128)S(1)}, u32[]{:S(2)}, u32[]{:S(2)}) %all-to-all-start.1) | async-done | bytes 262176 | tf_op jit(solution)/shard_map/all_to_all | solution.py:162
  32.2 0.0 copy-start
  32.2 0.7 copy-done
  32.9 5.1 %refits.1 = f32[16,16,128]{2,1,0:T(8,128)} custom-call(s32[1]{0:T(128)} %bitcast.refs_0_, f32[256,256]{1,0:T(8,128)} %bitcast.9, bf16[240,128]{1,0:T(8,128)(2,1)} %bitcast.14), custom_call_target="tpu_custom_call" | custom-call | tf_op jit(solution)/shard_map/refits/pallas_call | solution.py:144
  38.0 20.6 %all_to_all.31 = f32[16,16,128]{2,1,0:T(8,128)S(1)} all-to-all(f32[16,16,128]{2,1,0:T(8,128)} %refits.1), channel_id=1, replica_groups=mesh['subj'=16,'vox'=16] {'subj'}, dimensions={0} | all-to-all | bytes 262144 | tf_op jit(solution)/shard_map/all_to_all | solution.py:162
  58.7 10.1 %all_to_all.32 = bf16[16,16,128]{2,1,0:T(8,128)(2,1)} all-to-all(bf16[16,16,128]{2,1,0:T(8,128)(2,1)S(1)} %broadcast_in_dim.7), channel_id=1, replica_groups=mesh['subj'=16,'vox'=16] {'vox'}, dimensions={0} | all-to-all | bytes 131072 | tf_op jit(solution)/shard_map/all_to_all | solution.py:162
  68.8 5.1 %refits_last.1 = (f32[16,16,128]{2,1,0:T(8,128)}, f32[2,240,128]{2,1,0:T(8,128)}) custom-call(s32[1]{0:T(128)} %bitcast.refs_0_, f32[256,256]{1,0:T(8,128)} %bitcast.10, bf16[256,128]{1,0:T(8,128)(2,1)} %bitcast.12), custom_call_target="tpu_custom_call" | custom-call | tf_op jit(solution)/shard_map/refits_last/pallas_call | solution.py:144
  73.8 13.2 %all_to_all.33 = f32[16,16,128]{2,1,0:T(8,128)S(1)} all-to-all(f32[16,16,128]{2,1,0:T(8,128)} %get-tuple-element.5), channel_id=1, replica_groups=mesh['subj'=16,'vox'=16] {'subj'}, dimensions={0} | all-to-all | bytes 262144 | tf_op jit(solution)/shard_map/all_to_all | solution.py:162
  87.1 10.2 %all_to_all.34 = f32[16,16,128]{2,1,0:T(8,128)S(1)} all-to-all(f32[16,16,128]{2,1,0:T(8,128)S(1)} %broadcast_in_dim.8), channel_id=1, replica_groups=mesh['subj'=16,'vox'=16] {'vox'}, dimensions={0} | all-to-all | bytes 262144 | tf_op jit(solution)/shard_map/all_to_all | solution.py:162
  97.3 0.7 slice.8
  (7 shorter events, 0.1 us)
Async XLA Ops:
  21.2 11.0 %all-to-all-start.1 = ((f32[16,16,256]{2,1,0:T(8,128)}), f32[16,16,256]{2,1,0:T(8,128)S(1)}, u32[]{:S(2)}, u32[]{:S(2)}) async-start(f32[16,16,256]{2,1,0:T(8,128)} %broadcast_in_dim.6), calls=%async_computation.1 | async-start | bytes 524288 | tf_op jit(solution)/shard_map/all_to_all | solution.py:162
  32.2 0.7 copy-start

commit v2 on v1

v2 whole, which is shorter than its diff:
```python
import jax
import jax.numpy as jnp
from jax import lax
from jax.experimental import pallas as pl
from jax.experimental.pallas import tpu as pltpu
from jax.sharding import PartitionSpec as P

ITERS = 3
OUTER = 2
LANES = 128
VMEM = pl.BlockSpec(memory_space=pltpu.VMEM)
SMEM = pl.BlockSpec(memory_space=pltpu.SMEM)


def padded(frames):
    return -(-frames // (2 * LANES)) * 2 * LANES


def positions(size):
    rows = lax.broadcasted_iota(jnp.int32, (size, size), 0)
    cols = lax.broadcasted_iota(jnp.int32, (size, size), 1)
    return rows, cols


def gram_kernel(data_ref, start_ref, packed_ref, shared_ref, sums_ref):
    step = pl.program_id(0)
    frames = data_ref.shape[1]

    @pl.when(step == 0)
    def _():
        sums_ref[...] = jnp.zeros_like(sums_ref)
        shared_ref[...] = jnp.zeros_like(shared_ref)
        shared_ref[:, 0:frames] = start_ref[...].T

    for subject in range(2):
        block = data_ref[subject]
        sums_ref[subject] += lax.dot_general(
            block, block, (((1,), (1,)), ((), ())), preferred_element_type=jnp.float32
        )

    @pl.when(step == pl.num_programs(0) - 1)
    def _():
        rows, cols = positions(frames)
        first, second = sums_ref[0], sums_ref[1]
        mixed = jnp.where(rows >= cols, first, second)
        diagonal = jnp.sum(jnp.where(rows == cols, second, 0.0), axis=1, keepdims=True)
        packed_ref[...] = jnp.zeros_like(packed_ref)
        packed_ref[0:frames, 0:frames] = mixed
        packed_ref[0:frames, frames : frames + 1] = diagonal


def packed_grams(data, start, size):
    subjects, frames, voxels = data.shape
    features = start.shape[1]
    tile = 1024
    return pl.pallas_call(
        gram_kernel,
        grid=(voxels // tile,),
        in_specs=[pl.BlockSpec((subjects, frames, tile), lambda i: (0, 0, i)), VMEM],
        out_specs=[VMEM, VMEM],
        out_shape=[
            pltpu.VMEM((size, size), jnp.float32),
            pltpu.VMEM((features, size), jnp.bfloat16),
        ],
        scratch_shapes=[pltpu.VMEM((subjects, frames, frames), jnp.float32)],
        name="grams",
    )(data, start)


def parts_of(x, count):
    parts = []
    for part in range(count):
        parts.append(x.astype(jnp.bfloat16))
        if part < count - 1:
            x = x - parts[-1].astype(jnp.float32)
    return parts


def product(a, b, dims=((1,), (0,))):
    return lax.dot_general(a, b, (dims, ((), ())), preferred_element_type=jnp.float32)


def times(a, b):
    width = b.shape[1]
    a_both = jnp.concatenate(parts_of(a, 2), axis=1)
    high, low = parts_of(b, 2)
    if 2 * width <= 2 * LANES:
        wide = jnp.concatenate([high, low], axis=1)
        out = product(a_both, jnp.concatenate([wide, wide], axis=0))
        return out[:, :width] + out[:, width:]
    out = product(a_both, jnp.concatenate([high, high], axis=0))
    return out + product(a_both, jnp.concatenate([low, low], axis=0))


def refit(gram, shared, count):
    crossed = sum(product(shared, part) for part in parts_of(gram, count))
    square = jnp.sum(crossed * shared.astype(jnp.float32)) + 1e-06
    first = sum(product(shared, part, ((1,), (1,))) for part in parts_of(crossed, count))
    current = first * (1.0 / square)
    result = crossed * (1.0 / jnp.sqrt(square))
    for step in range(ITERS):
        if step < ITERS - 1:
            half = 1.5 * current - 0.5 * times(current, current)
        result = 1.5 * result - 0.5 * times(current, result)
        if step < ITERS - 1:
            current = 1.5 * half - 0.5 * times(half, current)
    return result


def refit_kernel(frames, last, place_ref, packed_ref, shared_ref, share_ref, *refs):
    total_ref = refs[-1]
    size = total_ref.shape[1]
    rows, cols = positions(size)
    packed = packed_ref[...]
    diagonal = packed[:, frames : frames + 1]
    packed = jnp.where(cols < frames, packed, 0.0)
    flipped = packed.T
    grams = (
        jnp.where(rows >= cols, packed, flipped),
        jnp.where(rows == cols, diagonal, jnp.where(rows < cols, packed, flipped)),
    )
    shared = shared_ref[...]
    results = [refit(gram, shared, 2 if last else 3) for gram in grams]
    if last:
        for subject in range(2):
            refs[0][subject] = results[subject]
    total_ref[...] = results[0] + results[1]
    width = share_ref.shape[1]
    share = total_ref[pl.ds(pl.multiple_of(place_ref[0] * width, width), width), :]
    for peer in range(share_ref.shape[0]):
        share_ref[peer] = share


def refits(packed, shared, place, frames, peers, last):
    features, size = shared.shape
    out = [pltpu.VMEM((peers, features // peers, size), jnp.float32)]
    if last:
        out.append(pltpu.VMEM((2, features, size), jnp.float32))

    def kernel(*refs):
        return refit_kernel(frames, last, *refs)

    return pl.pallas_call(
        kernel,
        in_specs=[SMEM, VMEM, VMEM],
        out_specs=[VMEM] * len(out),
        out_shape=out,
        scratch_shapes=[pltpu.VMEM((features, size), jnp.float32)],
        name="refits_last" if last else "refits",
    )(place, in_vmem(packed), in_vmem(shared))


def in_vmem(x):
    return pltpu.with_memory_space_constraint(x, pltpu.VMEM)


def exchanged(pieces, axis):
    return lax.all_to_all(pieces, axis, 0, 0, tiled=True)


def to_everyone(shard, peers):
    return jnp.broadcast_to(shard[None], (peers, *shard.shape))


def local(data, shared_start):
    frames = data.shape[1]
    peers = lax.axis_size("vox")
    subjects = data.shape[0] * lax.axis_size("subj")
    size = padded(frames)
    place = lax.axis_index("vox").astype(jnp.int32).reshape(1)
    packed, shared = packed_grams(data, shared_start.T, size)
    packed, place = lax.optimization_barrier((packed, place))
    share = jnp.sum(exchanged(packed.reshape(peers, size // peers, size), "vox"), axis=0)
    packed = exchanged(to_everyone(share, peers), "vox").reshape(size, size)
    for outer in range(OUTER):
        last = outer == OUTER - 1
        out = refits(packed, shared, place, frames, peers, last)
        total = jnp.sum(exchanged(out[0], "subj"), axis=0) / jnp.float32(subjects)
        if not last:
            total = total.astype(jnp.bfloat16)
        shared = exchanged(to_everyone(total, peers), "vox").reshape(-1, size)
    return (out[1][:, :, :frames], shared[:, :frames])


def solution(mesh):
    placed = (P("subj", None, "vox"), P())
    return jax.shard_map(
        local, mesh=mesh, in_specs=placed, out_specs=(P("subj", None, None), P()), check_vma=False
    )
```

time: 98.5 us -> 89.8 us (0.912)
  Pallas kernels: 14.9 us -> 8.41 us
  blocking collectives: 69.2 us -> 67.9 us
    pallas_call x2, Pallas kernels: 10.2 us -> 4.36 us  [refits(): pl.pallas_call(kernel, in_specs=[SMEM, VMEM, VMEM], out_specs=[VMEM] * le...]
    all_to_all x5, blocking collectives: 69.2 us -> 67.9 us  [exchanged(): return lax.all_to_all(pieces, axis, 0, 0, tiled=True)]
  transfers between devices with their start and end apart: 1 -> 1, of which waited for: 1 -> 1; matrix products, arithmetic and copies ran while one was open for 0% -> 1% of each run, Pallas kernels for 0% -> 0%
where the time goes in v2:
time: 89.8 us; the launch traced here: 89.4 us
  blocking collectives  67.9 us (76%)
  Pallas kernels  8.41 us (9%)
  waiting for transfers between devices  6.52 us (7%)
  starting transfers between devices  3.51 us (4%)
  local copies, waits for them, and re-layouts  2.25 us (3%)
    all_to_all x5, blocking collectives, exchanged(): return lax.all_to_all(pieces, axis, 0, 0, tiled=True)  67.9 us
    all_to_all x1, waiting for transfers between devices, exchanged(): return lax.all_to_all(pieces, axis, 0, 0, tiled=True)  6.52 us
    pallas_call x2, Pallas kernels, refits(): pl.pallas_call(kernel, in_specs=[SMEM, VMEM, VMEM], out_specs=[VMEM] * le...  4.36 us
    pallas_call x1, Pallas kernels, packed_grams(): pl.pallas_call(gram_kernel, grid=(voxels // tile,), in_specs=[pl.BlockSpe...  4.05 us
    all_to_all x1, starting transfers between devices, exchanged(): return lax.all_to_all(pieces, axis, 0, 0, tiled=True)  3.51 us
  transfers between devices with their start and end apart: 1, of which 1 were waited for; matrix products, arithmetic and copies ran while one was open for 1% of the time, Pallas kernels for 0%

profile of v2, /device:TPU:1, one launch (start us, length us, event | category | flops | bytes accessed | tf_op | source)
XLA Modules:
  0.0 89.4 jit_solution(4666810015196210961)
XLA Ops:
  0.6 4.1 %grams.1 = (f32[256,256]{1,0:T(8,128)S(1)}, bf16[128,256]{1,0:T(8,128)(2,1)S(1)}) custom-call(bf16[2,240,4096]{2,1,0:T(8,128)(2,1)} %data_ref.1, bf16[240,128]{1,0:T(8,128)(2,1)} %bitcast.14), custom_call_target="tpu_custom_call" | custom-call | tf_op jit(solution)/shard_map/grams/pallas_call | solution.py:56
  4.7 14.9 %all_to_all.30 = f32[16,16,256]{2,1,0:T(8,128)S(1)} all-to-all(f32[16,16,256]{2,1,0:T(8,128)S(1)} %bitcast.12), channel_id=1, replica_groups=mesh['subj'=16,'vox'=16] {'vox'}, dimensions={0} | all-to-all | bytes 524288 | tf_op jit(solution)/shard_map/all_to_all | solution.py:158
  19.7 10.5 %all_to_all.31 = f32[16,16,256]{2,1,0:T(8,128)S(1)} all-to-all(f32[16,16,256]{2,1,0:T(8,128)S(1)} %broadcast_in_dim.6), channel_id=1, replica_groups=mesh['subj'=16,'vox'=16] {'vox'}, dimensions={0} | all-to-all | bytes 524288 | tf_op jit(solution)/shard_map/all_to_all | solution.py:158
  30.1 2.2 %refits.1 = f32[16,8,256]{2,1,0:T(8,128)S(1)} custom-call(s32[1]{0:T(128)} %bitcast.1.refs_0_, f32[256,256]{1,0:T(8,128)S(1)} %bitcast.8, bf16[128,256]{1,0:T(8,128)(2,1)S(1)} %get-tuple-element.11.refs_2_), custom_call_target="tpu_custom_call" | custom-call | tf_op jit(solution)/shard_map/refits/pallas_call | solution.py:143
  32.4 20.4 %all_to_all.32 = f32[16,8,256]{2,1,0:T(8,128)S(1)} all-to-all(f32[16,8,256]{2,1,0:T(8,128)S(1)} %refits.1), channel_id=1, replica_groups=mesh['subj'=16,'vox'=16] {'subj'}, dimensions={0} | all-to-all | bytes 262144 | tf_op jit(solution)/shard_map/all_to_all | solution.py:158
  52.8 9.1 %all_to_all.33 = bf16[16,8,256]{2,1,0:T(8,128)(2,1)S(1)} all-to-all(bf16[16,8,256]{2,1,0:T(8,128)(2,1)S(1)} %broadcast_in_dim.7), channel_id=1, replica_groups=mesh['subj'=16,'vox'=16] {'vox'}, dimensions={0} | all-to-all | bytes 131072 | tf_op jit(solution)/shard_map/all_to_all | solution.py:158
  61.9 2.1 %refits_last.1 = (f32[16,8,256]{2,1,0:T(8,128)S(1)}, f32[2,128,256]{2,1,0:T(8,128)S(1)}) custom-call(s32[1]{0:T(128)} %bitcast.1.refs_0_, f32[256,256]{1,0:T(8,128)S(1)} %bitcast.9, bf16[128,256]{1,0:T(8,128)(2,1)S(1)} %bitcast.10), custom_call_target="tpu_custom_call" | custom-call | tf_op jit(solution)/shard_map/refits_last/pallas_call | solution.py:143
  64.1 13.0 %all_to_all.34 = f32[16,8,256]{2,1,0:T(8,128)S(1)} all-to-all(f32[16,8,256]{2,1,0:T(8,128)S(1)} %get-tuple-element.13), channel_id=1, replica_groups=mesh['subj'=16,'vox'=16] {'subj'}, dimensions={0} | all-to-all | bytes 262144 | tf_op jit(solution)/shard_map/all_to_all | solution.py:158
  77.1 0.6 broadcast_in_dim.8
  77.7 3.5 %all-to-all-start.5 = ((f32[16,8,256]{2,1,0:T(8,128)}), f32[16,8,256]{2,1,0:T(8,128)S(1)}, u32[]{:S(2)}, u32[]{:S(2)}) async-start(f32[16,8,256]{2,1,0:T(8,128)} %broadcast_in_dim.8), calls=%async_computation.5 | async-start | bytes 262144 | tf_op jit(solution)/shard_map/all_to_all | solution.py:158
  81.3 0.8 copy.6
  82.1 6.5 %all-to-all-done.5 = f32[16,8,256]{2,1,0:T(8,128)S(1)} async-done(((f32[16,8,256]{2,1,0:T(8,128)}), f32[16,8,256]{2,1,0:T(8,128)S(1)}, u32[]{:S(2)}, u32[]{:S(2)}) %all-to-all-start.5) | async-done | bytes 131104 | tf_op jit(solution)/shard_map/all_to_all | solution.py:158
  88.6 0.7 copy.7
  (7 shorter events, 0.1 us)
Async XLA Ops:
  77.7 10.9 %all-to-all-start.5 = ((f32[16,8,256]{2,1,0:T(8,128)}), f32[16,8,256]{2,1,0:T(8,128)S(1)}, u32[]{:S(2)}, u32[]{:S(2)}) async-start(f32[16,8,256]{2,1,0:T(8,128)} %broadcast_in_dim.8), calls=%async_computation.5 | async-start | bytes 262144 | tf_op jit(solution)/shard_map/all_to_all | solution.py:158

commit v3 on v2

--- a/solution.py
+++ b/solution.py
@@ -3,10 +3,9 @@
 from jax import lax
 from jax.experimental import pallas as pl
 from jax.experimental.pallas import tpu as pltpu
-from jax.sharding import PartitionSpec as P
+from jax.sharding import Mesh, PartitionSpec as P
 
 ITERS = 3
-OUTER = 2
 LANES = 128
 VMEM = pl.BlockSpec(memory_space=pltpu.VMEM)
 SMEM = pl.BlockSpec(memory_space=pltpu.SMEM)
@@ -52,7 +51,7 @@
 def packed_grams(data, start, size):
     subjects, frames, voxels = data.shape
     features = start.shape[1]
-    tile = 1024
+    tile = 2048
     return pl.pallas_call(
         gram_kernel,
         grid=(voxels // tile,),
@@ -107,9 +106,11 @@
     return result
 
 
-def refit_kernel(frames, last, place_ref, packed_ref, shared_ref, share_ref, *refs):
-    total_ref = refs[-1]
+def refit_kernel(frames, last, place_ref, packed_ref, *refs):
+    shared_refs, refs = refs[: 1 if not last else 4], refs[1 if not last else 4 :]
+    keep_ref, give_ref, total_ref = refs[0], refs[1], refs[-1]
     size = total_ref.shape[1]
+    width = keep_ref.shape[0]
     rows, cols = positions(size)
     packed = packed_ref[...]
     diagonal = packed[:, frames : frames + 1]
@@ -119,35 +120,65 @@
         jnp.where(rows >= cols, packed, flipped),
         jnp.where(rows == cols, diagonal, jnp.where(rows < cols, packed, flipped)),
     )
-    shared = shared_ref[...]
+    if last:
+        shared_ref = refs[-2]
+        for piece, piece_ref in enumerate(shared_refs):
+            shared_ref[block(place_ref, piece, width), :] = piece_ref[...]
+        shared = shared_ref[...]
+    else:
+        shared = shared_refs[0][...]
     results = [refit(gram, shared, 2 if last else 3) for gram in grams]
     if last:
         for subject in range(2):
-            refs[0][subject] = results[subject]
+            refs[2][subject] = results[subject]
     total_ref[...] = results[0] + results[1]
-    width = share_ref.shape[1]
-    share = total_ref[pl.ds(pl.multiple_of(place_ref[0] * width, width), width), :]
-    for peer in range(share_ref.shape[0]):
-        share_ref[peer] = share
-
-
-def refits(packed, shared, place, frames, peers, last):
-    features, size = shared.shape
-    out = [pltpu.VMEM((peers, features // peers, size), jnp.float32)]
+    keep_ref[...] = total_ref[block(place_ref, 0, width), :]
+    give_ref[...] = total_ref[block(place_ref, 1, width), :]
+
+
+def block(place_ref, piece, width):
+    return pl.ds(pl.multiple_of(place_ref[piece] * width, width), width)
+
+
+def refits(packed, shared, place, frames, features, last):
+    size = packed.shape[1]
+    quarter = pltpu.VMEM((features // 4, size), jnp.float32)
+    out = [quarter, quarter]
+    scratch = [pltpu.VMEM((features, size), jnp.float32)]
     if last:
         out.append(pltpu.VMEM((2, features, size), jnp.float32))
+        scratch.insert(0, pltpu.VMEM((features, size), jnp.bfloat16))
 
     def kernel(*refs):
         return refit_kernel(frames, last, *refs)
 
     return pl.pallas_call(
         kernel,
-        in_specs=[SMEM, VMEM, VMEM],
+        in_specs=[SMEM] + [VMEM] * (1 + len(shared)),
         out_specs=[VMEM] * len(out),
         out_shape=out,
-        scratch_shapes=[pltpu.VMEM((features, size), jnp.float32)],
+        scratch_shapes=scratch,
         name="refits_last" if last else "refits",
-    )(place, in_vmem(packed), in_vmem(shared))
+    )(place, *(in_vmem(x) for x in (packed, *shared)))
+
+
+def whole_kernel(place_ref, *refs):
+    pieces, out_ref, whole_ref = refs[:4], refs[4], refs[5]
+    for piece, piece_ref in enumerate(pieces):
+        whole_ref[block(place_ref, piece, piece_ref.shape[0]), :] = piece_ref[...]
+    out_ref[...] = whole_ref[...].T[0 : out_ref.shape[0], :]
+
+
+def whole(pieces, place, frames):
+    width, size = pieces[0].shape
+    return pl.pallas_call(
+        whole_kernel,
+        in_specs=[SMEM] + [VMEM] * 4,
+        out_specs=VMEM,
+        out_shape=jax.ShapeDtypeStruct((frames, 4 * width), jnp.float32),
+        scratch_shapes=[pltpu.VMEM((4 * width, size), jnp.float32)],
+        name="whole",
+    )(place, *(in_vmem(x) for x in pieces))
 
 
 def in_vmem(x):
@@ -162,28 +193,56 @@
     return jnp.broadcast_to(shard[None], (peers, *shard.shape))
 
 
+def swapped(x, core, across):
+    cores, chips = lax.axis_size("core"), lax.axis_size("x")
+    pairs = []
+    for c in range(cores):
+        for i in range(chips):
+            to = (c ^ core) * chips + (i ^ across)
+            pairs.append((c * chips + i, to))
+    return lax.ppermute(x, ("core", "x"), pairs)
+
+
+def all_summed(keep, give, dtype, scale, held=None):
+    chip = keep + swapped(give, 1, 0)
+    pieces = exchanged(to_everyone(chip, lax.axis_size("z")), "z")
+    total = (jnp.sum(pieces, axis=0) * scale).astype(dtype)
+    if held is not None:
+        total, held = lax.optimization_barrier((total, held))
+    return (total, swapped(total, 1, 0), swapped(total, 0, 1), swapped(total, 1, 1)), held
+
+
 def local(data, shared_start):
     frames = data.shape[1]
-    peers = lax.axis_size("vox")
-    subjects = data.shape[0] * lax.axis_size("subj")
+    features = shared_start.shape[0]
+    peers = lax.axis_size(("y", "x"))
+    subjects = data.shape[0] * lax.axis_size(("z", "core"))
     size = padded(frames)
-    place = lax.axis_index("vox").astype(jnp.int32).reshape(1)
+    core = lax.axis_index("core").astype(jnp.int32)
+    side = 2 * (lax.axis_index("x").astype(jnp.int32) % 2)
+    place = jnp.stack([side + core, side + 1 - core, 2 - side + core, 3 - side - core])
     packed, shared = packed_grams(data, shared_start.T, size)
     packed, place = lax.optimization_barrier((packed, place))
-    share = jnp.sum(exchanged(packed.reshape(peers, size // peers, size), "vox"), axis=0)
-    packed = exchanged(to_everyone(share, peers), "vox").reshape(size, size)
-    for outer in range(OUTER):
-        last = outer == OUTER - 1
-        out = refits(packed, shared, place, frames, peers, last)
-        total = jnp.sum(exchanged(out[0], "subj"), axis=0) / jnp.float32(subjects)
-        if not last:
-            total = total.astype(jnp.bfloat16)
-        shared = exchanged(to_everyone(total, peers), "vox").reshape(-1, size)
-    return (out[1][:, :, :frames], shared[:, :frames])
+    share = jnp.sum(exchanged(packed.reshape(peers, size // peers, size), ("y", "x")), axis=0)
+    packed = exchanged(to_everyone(share, peers), ("y", "x")).reshape(size, size)
+    keep, give = refits(packed, (shared,), place, frames, features, False)
+    pieces, _ = all_summed(keep, give, jnp.bfloat16, 1.0 / subjects)
+    keep, give, projections = refits(packed, pieces, place, frames, features, True)
+    pieces, projections = all_summed(keep, give, jnp.float32, 1.0 / subjects, projections)
+    response = whole(pieces, place, frames)
+    return (projections[:, :, :frames], response.T)
 
 
 def solution(mesh):
-    placed = (P("subj", None, "vox"), P())
+    sizes = dict(mesh.shape)
+    cores, across = 2, 4
+    shape = (sizes["subj"] // cores, cores, sizes["vox"] // across, across)
+    chips = Mesh(mesh.devices.reshape(shape), ("z", "core", "y", "x"))
+    placed = (P(("z", "core"), None, ("y", "x")), P())
     return jax.shard_map(
-        local, mesh=mesh, in_specs=placed, out_specs=(P("subj", None, None), P()), check_vma=False
+        local,
+        mesh=chips,
+        in_specs=placed,
+        out_specs=(P(("z", "core"), None, None), P()),
+        check_vma=False,
     )

time: 89.8 us -> 86.3 us (0.961)
  blocking collectives: 67.9 us -> 59.3 us
  starting transfers between devices: 3.51 us -> 9.77 us
  waiting for transfers between devices: 6.52 us -> 4.38 us
  Pallas kernels: 8.41 us -> 10.3 us
  local copies, waits for them, and re-layouts: 2.25 us -> 0.89 us
    ppermute x0 -> x8, starting transfers between devices: none -> 9.77 us  [swapped(): return lax.ppermute(x, ('core', 'x'), pairs)]
    all_to_all x5 -> x4, blocking collectives: 67.9 us -> 59.3 us  [exchanged(): return lax.all_to_all(pieces, axis, 0, 0, tiled=True)]
    all_to_all x1 -> x0, waiting for transfers between devices: 6.52 us -> none  [exchanged(): return lax.all_to_all(pieces, axis, 0, 0, tiled=True)]
    ppermute x0 -> x8, waiting for transfers between devices: none -> 4.38 us  [swapped(): return lax.ppermute(x, ('core', 'x'), pairs)]
    all_to_all x1 -> x0, starting transfers between devices: 3.51 us -> none  [exchanged(): return lax.all_to_all(pieces, axis, 0, 0, tiled=True)]
    pallas_call x2 -> x3, Pallas kernels: 4.36 us -> 7.1 us  [the longest x2 5.67 us: refits(): pl.pallas_call(kernel, in_specs=[SMEM] + [VMEM] * (1 + len(shared)), out_...]
  transfers between devices with their start and end apart: 1 -> 8, of which waited for: 1 -> 6; matrix products, arithmetic and copies ran while one was open for 1% -> 1% of each run, Pallas kernels for 0% -> 0%
where the time goes in v3:
time: 86.3 us; the launch traced here: 86 us
  blocking collectives  59.3 us (69%)
  Pallas kernels  10.3 us (12%)
  starting transfers between devices  9.77 us (11%)
  waiting for transfers between devices  4.38 us (5%)
  local copies, waits for them, and re-layouts  0.89 us (1%)
    all_to_all x4, blocking collectives, exchanged(): return lax.all_to_all(pieces, axis, 0, 0, tiled=True)  59.3 us
    ppermute x8, starting transfers between devices, swapped(): return lax.ppermute(x, ('core', 'x'), pairs)  9.77 us
    pallas_call x2, Pallas kernels, refits(): pl.pallas_call(kernel, in_specs=[SMEM] + [VMEM] * (1 + len(shared)), out_...  5.67 us
    ppermute x8, waiting for transfers between devices, swapped(): return lax.ppermute(x, ('core', 'x'), pairs)  4.38 us
    pallas_call x1, Pallas kernels, packed_grams(): pl.pallas_call(gram_kernel, grid=(voxels // tile,), in_specs=[pl.BlockSpe...  3.17 us
  transfers between devices with their start and end apart: 8, of which 6 were waited for; matrix products, arithmetic and copies ran while one was open for 1% of the time, Pallas kernels for 0%

profile of v3, /device:TPU:1, one launch (start us, length us, event | category | flops | bytes accessed | tf_op | source)
XLA Modules:
  0.0 86.0 jit_solution(14971090454254043510)
XLA Ops:
  0.7 3.2 %grams.1 = (f32[256,256]{1,0:T(8,128)S(1)}, bf16[128,256]{1,0:T(8,128)(2,1)S(1)}) custom-call(bf16[2,240,4096]{2,1,0:T(8,128)(2,1)} %data_ref.1, bf16[240,128]{1,0:T(8,128)(2,1)} %bitcast.14), custom_call_target="tpu_custom_call" | custom-call | tf_op jit(solution)/shard_map/grams/pallas_call | solution.py:55
  3.8 0.6 pad_add_fusion.refs_0_.place_ref
  4.4 14.9 %all_to_all.20 = f32[16,16,256]{2,1,0:T(8,128)S(1)} all-to-all(f32[16,16,256]{2,1,0:T(8,128)S(1)} %bitcast.12), channel_id=1, replica_groups=mesh['z'=8,'core'=2,'y'=4,'x'=4] {'y','x'}, dimensions={0} | all-to-all | bytes 524288 | tf_op jit(solution)/shard_map/all_to_all | solution.py:189
  19.4 10.5 %all_to_all.21 = f32[16,16,256]{2,1,0:T(8,128)S(1)} all-to-all(f32[16,16,256]{2,1,0:T(8,128)S(1)} %broadcast_in_dim.6), channel_id=1, replica_groups=mesh['z'=8,'core'=2,'y'=4,'x'=4] {'y','x'}, dimensions={0} | all-to-all | bytes 524288 | tf_op jit(solution)/shard_map/all_to_all | solution.py:189
  29.8 2.9 %refits.1 = (f32[32,256]{1,0:T(8,128)S(1)}, f32[32,256]{1,0:T(8,128)S(1)}) custom-call(s32[4]{0:T(128)} %pad_add_fusion.refs_0_.place_ref, f32[256,256]{1,0:T(8,128)S(1)} %bitcast.9, bf16[128,256]{1,0:T(8,128)(2,1)S(1)} %get-tuple-element.16.refs_2_), custom_call_target="tpu_custom_call" | custom-call | tf_op jit(solution)/shard_map/refits/pallas_call | solution.py:155
  32.7 3.3 %collective-permute-start = (f32[32,256]{1,0:T(8,128)S(1)}, f32[32,256]{1,0:T(8,128)S(1)}, u32[]{:S(2)}, u32[]{:S(2)}) collective-permute-start(f32[32,256]{1,0:T(8,128)S(1)} %get-tuple-element.18), channel_id=1, source_target_pairs={{0,16},{1,17},{2,18},{3,19},{16,0},{17,1},{18,2},{19,3},{4,20},{5,... | collective-permute-start | bytes 98312 | tf_op jit(solution)/shard_map/ppermute | solution.py:203
  36.1 0.9 collective-permute-done
  37.0 19.2 %all_to_all.22 = f32[8,32,256]{2,1,0:T(8,128)S(1)} all-to-all(f32[8,32,256]{2,1,0:T(8,128)S(1)} %broadcast_in_dim.7), channel_id=1, replica_groups=mesh['z'=8,'core'=2,'y'=4,'x'=4] {'z'}, dimensions={0} | all-to-all | bytes 524288 | tf_op jit(solution)/shard_map/all_to_all | solution.py:189
  56.2 1.9 %collective-permute-start.3 = (bf16[32,256]{1,0:T(8,128)(2,1)S(1)}, bf16[32,256]{1,0:T(8,128)(2,1)S(1)}, u32[]{:S(2)}, u32[]{:S(2)}) collective-permute-start(bf16[32,256]{1,0:T(8,128)(2,1)S(1)} %multiply_convert_fusion.refs_2_), channel_id=1, source_target_pairs={{0,17},{1,16},{2,19},{3,18},{16,1},{17,0},{18,3},{19,2},{4,21},{5,... | collective-permute-start | bytes 49160 | tf_op jit(solution)/shard_map/ppermute | solution.py:203
  58.1 1.2 %collective-permute-start.2 = (bf16[32,256]{1,0:T(8,128)(2,1)S(1)}, bf16[32,256]{1,0:T(8,128)(2,1)S(1)}, u32[]{:S(2)}, u32[]{:S(2)}) collective-permute-start(bf16[32,256]{1,0:T(8,128)(2,1)S(1)} %multiply_convert_fusion.refs_2_), channel_id=1, source_target_pairs={{0,1},{1,0},{2,3},{3,2},{16,17},{17,16},{18,19},{19,18},{4,5},{5,4... | collective-permute-start | bytes 49160 | tf_op jit(solution)/shard_map/ppermute | solution.py:203
  59.3 0.0 collective-permute-start.1
  59.3 0.2 collective-permute-done.3.refs_5_
  59.5 1.2 %collective-permute-done.2.refs_4_ = bf16[32,256]{1,0:T(8,128)(2,1)S(1)} collective-permute-done((bf16[32,256]{1,0:T(8,128)(2,1)S(1)}, bf16[32,256]{1,0:T(8,128)(2,1)S(1)}, u32[]{:S(2)}, u32[]{:S(2)}) %collective-permute-start.2) | collective-permute-done | bytes 16416 | tf_op jit(solution)/shard_map/ppermute | solution.py:203
  60.7 0.0 collective-permute-done.1.refs_3_
  60.7 2.8 %refits_last.1 = (f32[32,256]{1,0:T(8,128)S(1)}, f32[32,256]{1,0:T(8,128)S(1)}, f32[2,128,256]{2,1,0:T(8,128)S(1)}) custom-call(s32[4]{0:T(128)} %pad_add_fusion.refs_0_.place_ref, f32[256,256]{1,0:T(8,128)S(1)} %bitcast.10, bf16[32,256]{1,0:T(8,128)(2,1)S(1)} %multiply_convert_fusion.refs_2_, bf16[32,256]{1,0:T(8,128)(2,1)S(1)} %collective-permute-done.1.refs_3_, ...), custom_call_target="tpu_custom_call" | custom-call | tf_op jit(solution)/shard_map/refits_last/pallas_call | solution.py:155
  63.5 1.2 %collective-permute-start.4 = (f32[32,256]{1,0:T(8,128)S(1)}, f32[32,256]{1,0:T(8,128)S(1)}, u32[]{:S(2)}, u32[]{:S(2)}) collective-permute-start(f32[32,256]{1,0:T(8,128)S(1)} %get-tuple-element.20), channel_id=1, source_target_pairs={{0,16},{1,17},{2,18},{3,19},{16,0},{17,1},{18,2},{19,3},{4,20},{5,... | collective-permute-start | bytes 98312 | tf_op jit(solution)/shard_map/ppermute | solution.py:203
  64.6 0.9 collective-permute-done.4
  65.5 14.8 %all_to_all.23 = f32[8,32,256]{2,1,0:T(8,128)S(1)} all-to-all(f32[8,32,256]{2,1,0:T(8,128)S(1)} %broadcast_in_dim.8), channel_id=1, replica_groups=mesh['z'=8,'core'=2,'y'=4,'x'=4] {'z'}, dimensions={0} | all-to-all | bytes 524288 | tf_op jit(solution)/shard_map/all_to_all | solution.py:189
  80.3 0.9 %collective-permute-start.7 = (f32[32,256]{1,0:T(8,128)S(1)}, f32[32,256]{1,0:T(8,128)S(1)}, u32[]{:S(2)}, u32[]{:S(2)}) collective-permute-start(f32[32,256]{1,0:T(8,128)S(1)} %broadcast_multiply_fusion.refs_0_), channel_id=1, source_target_pairs={{0,17},{1,16},{2,19},{3,18},{16,1},{17,0},{18,3},{19,2},{4,21},{5,... | collective-permute-start | bytes 98312 | tf_op jit(solution)/shard_map/ppermute | solution.py:203
  81.2 1.0 %collective-permute-start.6 = (f32[32,256]{1,0:T(8,128)S(1)}, f32[32,256]{1,0:T(8,128)S(1)}, u32[]{:S(2)}, u32[]{:S(2)}) collective-permute-start(f32[32,256]{1,0:T(8,128)S(1)} %broadcast_multiply_fusion.refs_0_), channel_id=1, source_target_pairs={{0,1},{1,0},{2,3},{3,2},{16,17},{17,16},{18,19},{19,18},{4,5},{5,4... | collective-permute-start | bytes 98312 | tf_op jit(solution)/shard_map/ppermute | solution.py:203
  82.2 0.3 collective-permute-start.5
  82.5 0.8 copy.5
  83.4 0.7 collective-permute-done.7.refs_3_
  84.1 0.5 collective-permute-done.6.refs_2_
  84.6 0.0 collective-permute-done.5.refs_1_
  84.6 1.4 %whole.1 = f32[240,128]{1,0:T(8,128)} custom-call(s32[4]{0:T(128)} %pad_add_fusion.refs_0_.place_ref, f32[32,256]{1,0:T(8,128)S(1)} %broadcast_multiply_fusion.refs_0_, f32[32,256]{1,0:T(8,128)S(1)} %collective-permute-done.5.refs_1_, f32[32,256]{1,0:T(8,128)S(1)} %collective-permute-done.6.refs_2_, f32[32,256]{1,0:T(8,128)S(1)} %collective-permute-done.7.refs_3_), custom_call_target="tpu_custom_call" | custom-call | tf_op jit(solution)/shard_map/whole/pallas_call | solution.py:174
  (10 shorter events, 0.1 us)
Async XLA Ops:
  32.7 4.2 %collective-permute-start = (f32[32,256]{1,0:T(8,128)S(1)}, f32[32,256]{1,0:T(8,128)S(1)}, u32[]{:S(2)}, u32[]{:S(2)}) collective-permute-start(f32[32,256]{1,0:T(8,128)S(1)} %get-tuple-element.18), channel_id=1, source_target_pairs={{0,16},{1,17},{2,18},{3,19},{16,0},{17,1},{18,2},{19,3},{4,20},{5,... | collective-permute-start | bytes 98312 | tf_op jit(solution)/shard_map/ppermute | solution.py:203
  56.2 3.3 %collective-permute-start.3 = (bf16[32,256]{1,0:T(8,128)(2,1)S(1)}, bf16[32,256]{1,0:T(8,128)(2,1)S(1)}, u32[]{:S(2)}, u32[]{:S(2)}) collective-permute-start(bf16[32,256]{1,0:T(8,128)(2,1)S(1)} %multiply_convert_fusion.refs_2_), channel_id=1, source_target_pairs={{0,17},{1,16},{2,19},{3,18},{16,1},{17,0},{18,3},{19,2},{4,21},{5,... | collective-permute-start | bytes 49160 | tf_op jit(solution)/shard_map/ppermute | solution.py:203
  58.1 2.6 %collective-permute-start.2 = (bf16[32,256]{1,0:T(8,128)(2,1)S(1)}, bf16[32,256]{1,0:T(8,128)(2,1)S(1)}, u32[]{:S(2)}, u32[]{:S(2)}) collective-permute-start(bf16[32,256]{1,0:T(8,128)(2,1)S(1)} %multiply_convert_fusion.refs_2_), channel_id=1, source_target_pairs={{0,1},{1,0},{2,3},{3,2},{16,17},{17,16},{18,19},{19,18},{4,5},{5,4... | collective-permute-start | bytes 49160 | tf_op jit(solution)/shard_map/ppermute | solution.py:203
  59.3 1.4 %collective-permute-start.1 = (bf16[32,256]{1,0:T(8,128)(2,1)S(1)}, bf16[32,256]{1,0:T(8,128)(2,1)S(1)}, u32[]{:S(2)}, u32[]{:S(2)}) collective-permute-start(bf16[32,256]{1,0:T(8,128)(2,1)S(1)} %multiply_convert_fusion.refs_2_), channel_id=1, source_target_pairs={{0,16},{1,17},{2,18},{3,19},{16,0},{17,1},{18,2},{19,3},{4,20},{5,... | collective-permute-start | bytes 49160 | tf_op jit(solution)/shard_map/ppermute | solution.py:203
  63.5 2.0 %collective-permute-start.4 = (f32[32,256]{1,0:T(8,128)S(1)}, f32[32,256]{1,0:T(8,128)S(1)}, u32[]{:S(2)}, u32[]{:S(2)}) collective-permute-start(f32[32,256]{1,0:T(8,128)S(1)} %get-tuple-element.20), channel_id=1, source_target_pairs={{0,16},{1,17},{2,18},{3,19},{16,0},{17,1},{18,2},{19,3},{4,20},{5,... | collective-permute-start | bytes 98312 | tf_op jit(solution)/shard_map/ppermute | solution.py:203
  80.3 3.8 %collective-permute-start.7 = (f32[32,256]{1,0:T(8,128)S(1)}, f32[32,256]{1,0:T(8,128)S(1)}, u32[]{:S(2)}, u32[]{:S(2)}) collective-permute-start(f32[32,256]{1,0:T(8,128)S(1)} %broadcast_multiply_fusion.refs_0_), channel_id=1, source_target_pairs={{0,17},{1,16},{2,19},{3,18},{16,1},{17,0},{18,3},{19,2},{4,21},{5,... | collective-permute-start | bytes 98312 | tf_op jit(solution)/shard_map/ppermute | solution.py:203
  81.2 3.4 %collective-permute-start.6 = (f32[32,256]{1,0:T(8,128)S(1)}, f32[32,256]{1,0:T(8,128)S(1)}, u32[]{:S(2)}, u32[]{:S(2)}) collective-permute-start(f32[32,256]{1,0:T(8,128)S(1)} %broadcast_multiply_fusion.refs_0_), channel_id=1, source_target_pairs={{0,1},{1,0},{2,3},{3,2},{16,17},{17,16},{18,19},{19,18},{4,5},{5,4... | collective-permute-start | bytes 98312 | tf_op jit(solution)/shard_map/ppermute | solution.py:203
  82.2 2.4 %collective-permute-start.5 = (f32[32,256]{1,0:T(8,128)S(1)}, f32[32,256]{1,0:T(8,128)S(1)}, u32[]{:S(2)}, u32[]{:S(2)}) collective-permute-start(f32[32,256]{1,0:T(8,128)S(1)} %broadcast_multiply_fusion.refs_0_), channel_id=1, source_target_pairs={{0,16},{1,17},{2,18},{3,19},{16,0},{17,1},{18,2},{19,3},{4,20},{5,... | collective-permute-start | bytes 98312 | tf_op jit(solution)/shard_map/ppermute | solution.py:203

commit v4 on v3

--- a/solution.py
+++ b/solution.py
@@ -8,7 +8,6 @@
 ITERS = 3
 LANES = 128
 VMEM = pl.BlockSpec(memory_space=pltpu.VMEM)
-SMEM = pl.BlockSpec(memory_space=pltpu.SMEM)
 
 
 def padded(frames):
@@ -106,7 +105,7 @@
     return result
 
 
-def refit_kernel(frames, last, place_ref, packed_ref, *refs):
+def refit_kernel(frames, last, packed_ref, *refs):
     shared_refs, refs = refs[: 1 if not last else 4], refs[1 if not last else 4 :]
     keep_ref, give_ref, total_ref = refs[0], refs[1], refs[-1]
     size = total_ref.shape[1]
@@ -123,7 +122,7 @@
     if last:
         shared_ref = refs[-2]
         for piece, piece_ref in enumerate(shared_refs):
-            shared_ref[block(place_ref, piece, width), :] = piece_ref[...]
+            shared_ref[block(piece, width), :] = piece_ref[...]
         shared = shared_ref[...]
     else:
         shared = shared_refs[0][...]
@@ -132,15 +131,18 @@
         for subject in range(2):
             refs[2][subject] = results[subject]
     total_ref[...] = results[0] + results[1]
-    keep_ref[...] = total_ref[block(place_ref, 0, width), :]
-    give_ref[...] = total_ref[block(place_ref, 1, width), :]
-
-
-def block(place_ref, piece, width):
-    return pl.ds(pl.multiple_of(place_ref[piece] * width, width), width)
-
-
-def refits(packed, shared, place, frames, features, last):
+    keep_ref[...] = total_ref[block(0, width), :]
+    give_ref[...] = total_ref[block(1, width), :]
+
+
+def block(piece, width):
+    core, side = lax.axis_index("core"), lax.axis_index("x") % 2
+    core = 1 - core if piece % 2 else core
+    side = 1 - side if piece // 2 else side
+    return pl.ds(pl.multiple_of((2 * side + core) * width, width), width)
+
+
+def refits(packed, shared, frames, features, last):
     size = packed.shape[1]
     quarter = pltpu.VMEM((features // 4, size), jnp.float32)
     out = [quarter, quarter]
@@ -154,31 +156,31 @@
 
     return pl.pallas_call(
         kernel,
-        in_specs=[SMEM] + [VMEM] * (1 + len(shared)),
+        in_specs=[VMEM] * (1 + len(shared)),
         out_specs=[VMEM] * len(out),
         out_shape=out,
         scratch_shapes=scratch,
         name="refits_last" if last else "refits",
-    )(place, *(in_vmem(x) for x in (packed, *shared)))
-
-
-def whole_kernel(place_ref, *refs):
+    )(*(in_vmem(x) for x in (packed, *shared)))
+
+
+def whole_kernel(*refs):
     pieces, out_ref, whole_ref = refs[:4], refs[4], refs[5]
     for piece, piece_ref in enumerate(pieces):
-        whole_ref[block(place_ref, piece, piece_ref.shape[0]), :] = piece_ref[...]
+        whole_ref[block(piece, piece_ref.shape[0]), :] = piece_ref[...]
     out_ref[...] = whole_ref[...].T[0 : out_ref.shape[0], :]
 
 
-def whole(pieces, place, frames):
+def whole(pieces, frames):
     width, size = pieces[0].shape
     return pl.pallas_call(
         whole_kernel,
-        in_specs=[SMEM] + [VMEM] * 4,
+        in_specs=[VMEM] * 4,
         out_specs=VMEM,
         out_shape=jax.ShapeDtypeStruct((frames, 4 * width), jnp.float32),
         scratch_shapes=[pltpu.VMEM((4 * width, size), jnp.float32)],
         name="whole",
-    )(place, *(in_vmem(x) for x in pieces))
+    )(*(in_vmem(x) for x in pieces))
 
 
 def in_vmem(x):
@@ -218,18 +220,14 @@
     peers = lax.axis_size(("y", "x"))
     subjects = data.shape[0] * lax.axis_size(("z", "core"))
     size = padded(frames)
-    core = lax.axis_index("core").astype(jnp.int32)
-    side = 2 * (lax.axis_index("x").astype(jnp.int32) % 2)
-    place = jnp.stack([side + core, side + 1 - core, 2 - side + core, 3 - side - core])
     packed, shared = packed_grams(data, shared_start.T, size)
-    packed, place = lax.optimization_barrier((packed, place))
     share = jnp.sum(exchanged(packed.reshape(peers, size // peers, size), ("y", "x")), axis=0)
     packed = exchanged(to_everyone(share, peers), ("y", "x")).reshape(size, size)
-    keep, give = refits(packed, (shared,), place, frames, features, False)
+    keep, give = refits(packed, (shared,), frames, features, False)
     pieces, _ = all_summed(keep, give, jnp.bfloat16, 1.0 / subjects)
-    keep, give, projections = refits(packed, pieces, place, frames, features, True)
+    keep, give, projections = refits(packed, pieces, frames, features, True)
     pieces, projections = all_summed(keep, give, jnp.float32, 1.0 / subjects, projections)
-    response = whole(pieces, place, frames)
+    response = whole(pieces, frames)
     return (projections[:, :, :frames], response.T)
 
 

time: 86.3 us -> 83.7 us (0.970)
  Pallas kernels: 10.3 us -> 8.29 us
    pallas_call x3, Pallas kernels: 7.1 us -> 5.12 us  [the longest x2 4.35 us: refits(): pl.pallas_call(kernel, in_specs=[VMEM] * (1 + len(shared)), out_specs=[VM...]
where the time goes in v4:
time: 83.7 us; the launch traced here: 83.4 us
  blocking collectives  59.3 us (71%)
  starting transfers between devices  9.78 us (12%)
  Pallas kernels  8.29 us (10%)
  waiting for transfers between devices  4.39 us (5%)
  local copies, waits for them, and re-layouts  0.89 us (1%)
    all_to_all x4, blocking collectives, exchanged(): return lax.all_to_all(pieces, axis, 0, 0, tiled=True)  59.3 us
    ppermute x8, starting transfers between devices, swapped(): return lax.ppermute(x, ('core', 'x'), pairs)  9.78 us
    ppermute x8, waiting for transfers between devices, swapped(): return lax.ppermute(x, ('core', 'x'), pairs)  4.39 us
    pallas_call x2, Pallas kernels, refits(): pl.pallas_call(kernel, in_specs=[VMEM] * (1 + len(shared)), out_specs=[VM...  4.35 us
    pallas_call x1, Pallas kernels, packed_grams(): pl.pallas_call(gram_kernel, grid=(voxels // tile,), in_specs=[pl.BlockSpe...  3.17 us
  transfers between devices with their start and end apart: 8, of which 6 were waited for; matrix products, arithmetic and copies ran while one was open for 1% of the time, Pallas kernels for 0%

profile of v4, /device:TPU:1, one launch (start us, length us, event | category | flops | bytes accessed | tf_op | source)
XLA Modules:
  0.0 83.4 jit_solution(10534870976854431005)
XLA Ops:
  0.6 3.2 %grams.1 = (f32[256,256]{1,0:T(8,128)S(1)}, bf16[128,256]{1,0:T(8,128)(2,1)S(1)}) custom-call(bf16[2,240,4096]{2,1,0:T(8,128)(2,1)} %data_ref.1, bf16[240,128]{1,0:T(8,128)(2,1)} %bitcast.10), custom_call_target="tpu_custom_call" | custom-call | tf_op jit(solution)/shard_map/grams/pallas_call | solution.py:54
  3.8 14.9 %all_to_all.20 = f32[16,16,256]{2,1,0:T(8,128)S(1)} all-to-all(f32[16,16,256]{2,1,0:T(8,128)S(1)} %bitcast.8), channel_id=1, replica_groups=mesh['z'=8,'core'=2,'y'=4,'x'=4] {'y','x'}, dimensions={0} | all-to-all | bytes 524288 | tf_op jit(solution)/shard_map/all_to_all | solution.py:191
  18.8 10.5 %all_to_all.21 = f32[16,16,256]{2,1,0:T(8,128)S(1)} all-to-all(f32[16,16,256]{2,1,0:T(8,128)S(1)} %broadcast_in_dim.6), channel_id=1, replica_groups=mesh['z'=8,'core'=2,'y'=4,'x'=4] {'y','x'}, dimensions={0} | all-to-all | bytes 524288 | tf_op jit(solution)/shard_map/all_to_all | solution.py:191
  29.2 2.2 %refits.1 = (f32[32,256]{1,0:T(8,128)S(1)}, f32[32,256]{1,0:T(8,128)S(1)}) custom-call(f32[256,256]{1,0:T(8,128)S(1)} %bitcast.5, bf16[128,256]{1,0:T(8,128)(2,1)S(1)} %get-tuple-element.12.refs_1_), custom_call_target="tpu_custom_call" | custom-call | tf_op jit(solution)/shard_map/refits/pallas_call | solution.py:157
  31.5 3.3 %collective-permute-start = (f32[32,256]{1,0:T(8,128)S(1)}, f32[32,256]{1,0:T(8,128)S(1)}, u32[]{:S(2)}, u32[]{:S(2)}) collective-permute-start(f32[32,256]{1,0:T(8,128)S(1)} %get-tuple-element.14), channel_id=1, source_target_pairs={{0,16},{1,17},{2,18},{3,19},{16,0},{17,1},{18,2},{19,3},{4,20},{5,... | collective-permute-start | bytes 98312 | tf_op jit(solution)/shard_map/ppermute | solution.py:205
  34.8 0.9 %collective-permute-done = f32[32,256]{1,0:T(8,128)S(1)} collective-permute-done((f32[32,256]{1,0:T(8,128)S(1)}, f32[32,256]{1,0:T(8,128)S(1)}, u32[]{:S(2)}, u32[]{:S(2)}) %collective-permute-start) | collective-permute-done | bytes 32800 | tf_op jit(solution)/shard_map/ppermute | solution.py:205
  35.7 19.2 %all_to_all.22 = f32[8,32,256]{2,1,0:T(8,128)S(1)} all-to-all(f32[8,32,256]{2,1,0:T(8,128)S(1)} %broadcast_in_dim.7), channel_id=1, replica_groups=mesh['z'=8,'core'=2,'y'=4,'x'=4] {'z'}, dimensions={0} | all-to-all | bytes 524288 | tf_op jit(solution)/shard_map/all_to_all | solution.py:191
  54.9 1.9 %collective-permute-start.3 = (bf16[32,256]{1,0:T(8,128)(2,1)S(1)}, bf16[32,256]{1,0:T(8,128)(2,1)S(1)}, u32[]{:S(2)}, u32[]{:S(2)}) collective-permute-start(bf16[32,256]{1,0:T(8,128)(2,1)S(1)} %multiply_convert_fusion.refs_1_), channel_id=1, source_target_pairs={{0,17},{1,16},{2,19},{3,18},{16,1},{17,0},{18,3},{19,2},{4,21},{5,... | collective-permute-start | bytes 49160 | tf_op jit(solution)/shard_map/ppermute | solution.py:205
  56.8 1.2 %collective-permute-start.2 = (bf16[32,256]{1,0:T(8,128)(2,1)S(1)}, bf16[32,256]{1,0:T(8,128)(2,1)S(1)}, u32[]{:S(2)}, u32[]{:S(2)}) collective-permute-start(bf16[32,256]{1,0:T(8,128)(2,1)S(1)} %multiply_convert_fusion.refs_1_), channel_id=1, source_target_pairs={{0,1},{1,0},{2,3},{3,2},{16,17},{17,16},{18,19},{19,18},{4,5},{5,4... | collective-permute-start | bytes 49160 | tf_op jit(solution)/shard_map/ppermute | solution.py:205
  58.0 0.0 collective-permute-start.1
  58.0 0.2 collective-permute-done.3.refs_4_
  58.2 1.2 %collective-permute-done.2.refs_3_ = bf16[32,256]{1,0:T(8,128)(2,1)S(1)} collective-permute-done((bf16[32,256]{1,0:T(8,128)(2,1)S(1)}, bf16[32,256]{1,0:T(8,128)(2,1)S(1)}, u32[]{:S(2)}, u32[]{:S(2)}) %collective-permute-start.2) | collective-permute-done | bytes 16416 | tf_op jit(solution)/shard_map/ppermute | solution.py:205
  59.4 0.0 collective-permute-done.1.refs_2_
  59.4 2.1 %refits_last.1 = (f32[32,256]{1,0:T(8,128)S(1)}, f32[32,256]{1,0:T(8,128)S(1)}, f32[2,128,256]{2,1,0:T(8,128)S(1)}) custom-call(f32[256,256]{1,0:T(8,128)S(1)} %bitcast.6, bf16[32,256]{1,0:T(8,128)(2,1)S(1)} %multiply_convert_fusion.refs_1_, bf16[32,256]{1,0:T(8,128)(2,1)S(1)} %collective-permute-done.1.refs_2_, ...), custom_call_target="tpu_custom_call" | custom-call | tf_op jit(solution)/shard_map/refits_last/pallas_call | solution.py:157
  61.5 1.2 %collective-permute-start.4 = (f32[32,256]{1,0:T(8,128)S(1)}, f32[32,256]{1,0:T(8,128)S(1)}, u32[]{:S(2)}, u32[]{:S(2)}) collective-permute-start(f32[32,256]{1,0:T(8,128)S(1)} %get-tuple-element.16), channel_id=1, source_target_pairs={{0,16},{1,17},{2,18},{3,19},{16,0},{17,1},{18,2},{19,3},{4,20},{5,... | collective-permute-start | bytes 98312 | tf_op jit(solution)/shard_map/ppermute | solution.py:205
  62.7 0.9 %collective-permute-done.4 = f32[32,256]{1,0:T(8,128)S(1)} collective-permute-done((f32[32,256]{1,0:T(8,128)S(1)}, f32[32,256]{1,0:T(8,128)S(1)}, u32[]{:S(2)}, u32[]{:S(2)}) %collective-permute-start.4) | collective-permute-done | bytes 32800 | tf_op jit(solution)/shard_map/ppermute | solution.py:205
  63.6 14.8 %all_to_all.23 = f32[8,32,256]{2,1,0:T(8,128)S(1)} all-to-all(f32[8,32,256]{2,1,0:T(8,128)S(1)} %broadcast_in_dim.8), channel_id=1, replica_groups=mesh['z'=8,'core'=2,'y'=4,'x'=4] {'z'}, dimensions={0} | all-to-all | bytes 524288 | tf_op jit(solution)/shard_map/all_to_all | solution.py:191
  78.4 0.9 %collective-permute-start.7 = (f32[32,256]{1,0:T(8,128)S(1)}, f32[32,256]{1,0:T(8,128)S(1)}, u32[]{:S(2)}, u32[]{:S(2)}) collective-permute-start(f32[32,256]{1,0:T(8,128)S(1)} %broadcast_multiply_fusion.refs_0_), channel_id=1, source_target_pairs={{0,17},{1,16},{2,19},{3,18},{16,1},{17,0},{18,3},{19,2},{4,21},{5,... | collective-permute-start | bytes 98312 | tf_op jit(solution)/shard_map/ppermute | solution.py:205
  79.3 1.0 %collective-permute-start.6 = (f32[32,256]{1,0:T(8,128)S(1)}, f32[32,256]{1,0:T(8,128)S(1)}, u32[]{:S(2)}, u32[]{:S(2)}) collective-permute-start(f32[32,256]{1,0:T(8,128)S(1)} %broadcast_multiply_fusion.refs_0_), channel_id=1, source_target_pairs={{0,1},{1,0},{2,3},{3,2},{16,17},{17,16},{18,19},{19,18},{4,5},{5,4... | collective-permute-start | bytes 98312 | tf_op jit(solution)/shard_map/ppermute | solution.py:205
  80.3 0.3 collective-permute-start.5
  80.6 0.8 copy.5
  81.4 0.7 collective-permute-done.7.refs_3_
  82.1 0.5 collective-permute-done.6.refs_2_
  82.7 0.0 collective-permute-done.5.refs_1_
  82.7 0.8 whole.1
  (10 shorter events, 0.1 us)
Async XLA Ops:
  31.5 4.2 %collective-permute-start = (f32[32,256]{1,0:T(8,128)S(1)}, f32[32,256]{1,0:T(8,128)S(1)}, u32[]{:S(2)}, u32[]{:S(2)}) collective-permute-start(f32[32,256]{1,0:T(8,128)S(1)} %get-tuple-element.14), channel_id=1, source_target_pairs={{0,16},{1,17},{2,18},{3,19},{16,0},{17,1},{18,2},{19,3},{4,20},{5,... | collective-permute-start | bytes 98312 | tf_op jit(solution)/shard_map/ppermute | solution.py:205
  54.9 3.3 %collective-permute-start.3 = (bf16[32,256]{1,0:T(8,128)(2,1)S(1)}, bf16[32,256]{1,0:T(8,128)(2,1)S(1)}, u32[]{:S(2)}, u32[]{:S(2)}) collective-permute-start(bf16[32,256]{1,0:T(8,128)(2,1)S(1)} %multiply_convert_fusion.refs_1_), channel_id=1, source_target_pairs={{0,17},{1,16},{2,19},{3,18},{16,1},{17,0},{18,3},{19,2},{4,21},{5,... | collective-permute-start | bytes 49160 | tf_op jit(solution)/shard_map/ppermute | solution.py:205
  56.8 2.6 %collective-permute-start.2 = (bf16[32,256]{1,0:T(8,128)(2,1)S(1)}, bf16[32,256]{1,0:T(8,128)(2,1)S(1)}, u32[]{:S(2)}, u32[]{:S(2)}) collective-permute-start(bf16[32,256]{1,0:T(8,128)(2,1)S(1)} %multiply_convert_fusion.refs_1_), channel_id=1, source_target_pairs={{0,1},{1,0},{2,3},{3,2},{16,17},{17,16},{18,19},{19,18},{4,5},{5,4... | collective-permute-start | bytes 49160 | tf_op jit(solution)/shard_map/ppermute | solution.py:205
  58.0 1.4 %collective-permute-start.1 = (bf16[32,256]{1,0:T(8,128)(2,1)S(1)}, bf16[32,256]{1,0:T(8,128)(2,1)S(1)}, u32[]{:S(2)}, u32[]{:S(2)}) collective-permute-start(bf16[32,256]{1,0:T(8,128)(2,1)S(1)} %multiply_convert_fusion.refs_1_), channel_id=1, source_target_pairs={{0,16},{1,17},{2,18},{3,19},{16,0},{17,1},{18,2},{19,3},{4,20},{5,... | collective-permute-start | bytes 49160 | tf_op jit(solution)/shard_map/ppermute | solution.py:205
  61.5 2.0 %collective-permute-start.4 = (f32[32,256]{1,0:T(8,128)S(1)}, f32[32,256]{1,0:T(8,128)S(1)}, u32[]{:S(2)}, u32[]{:S(2)}) collective-permute-start(f32[32,256]{1,0:T(8,128)S(1)} %get-tuple-element.16), channel_id=1, source_target_pairs={{0,16},{1,17},{2,18},{3,19},{16,0},{17,1},{18,2},{19,3},{4,20},{5,... | collective-permute-start | bytes 98312 | tf_op jit(solution)/shard_map/ppermute | solution.py:205
  78.4 3.8 %collective-permute-start.7 = (f32[32,256]{1,0:T(8,128)S(1)}, f32[32,256]{1,0:T(8,128)S(1)}, u32[]{:S(2)}, u32[]{:S(2)}) collective-permute-start(f32[32,256]{1,0:T(8,128)S(1)} %broadcast_multiply_fusion.refs_0_), channel_id=1, source_target_pairs={{0,17},{1,16},{2,19},{3,18},{16,1},{17,0},{18,3},{19,2},{4,21},{5,... | collective-permute-start | bytes 98312 | tf_op jit(solution)/shard_map/ppermute | solution.py:205
  79.3 3.4 %collective-permute-start.6 = (f32[32,256]{1,0:T(8,128)S(1)}, f32[32,256]{1,0:T(8,128)S(1)}, u32[]{:S(2)}, u32[]{:S(2)}) collective-permute-start(f32[32,256]{1,0:T(8,128)S(1)} %broadcast_multiply_fusion.refs_0_), channel_id=1, source_target_pairs={{0,1},{1,0},{2,3},{3,2},{16,17},{17,16},{18,19},{19,18},{4,5},{5,4... | collective-permute-start | bytes 98312 | tf_op jit(solution)/shard_map/ppermute | solution.py:205
  80.3 2.4 %collective-permute-start.5 = (f32[32,256]{1,0:T(8,128)S(1)}, f32[32,256]{1,0:T(8,128)S(1)}, u32[]{:S(2)}, u32[]{:S(2)}) collective-permute-start(f32[32,256]{1,0:T(8,128)S(1)} %broadcast_multiply_fusion.refs_0_), channel_id=1, source_target_pairs={{0,16},{1,17},{2,18},{3,19},{16,0},{17,1},{18,2},{19,3},{4,20},{5,... | collective-permute-start | bytes 98312 | tf_op jit(solution)/shard_map/ppermute | solution.py:205

commit v5 on v4

v5 whole, which is shorter than its diff:
```python
import functools

import jax
import jax.numpy as jnp
from jax import lax
from jax.experimental import pallas as pl
from jax.experimental.pallas import tpu as pltpu
from jax.sharding import Mesh, PartitionSpec as P

ITERS = 3
LANES = 128
VMEM = pl.BlockSpec(memory_space=pltpu.VMEM)


def padded(frames):
    return -(-frames // (2 * LANES)) * 2 * LANES


def positions(size):
    rows = lax.broadcasted_iota(jnp.int32, (size, size), 0)
    cols = lax.broadcasted_iota(jnp.int32, (size, size), 1)
    return rows, cols


def gram_kernel(data_ref, start_ref, packed_ref, shared_ref, sums_ref):
    step = pl.program_id(0)
    frames = data_ref.shape[1]

    @pl.when(step == 0)
    def _():
        sums_ref[...] = jnp.zeros_like(sums_ref)
        shared_ref[...] = jnp.zeros_like(shared_ref)
        shared_ref[:, 0:frames] = start_ref[...].T

    for subject in range(2):
        block = data_ref[subject]
        sums_ref[subject] += lax.dot_general(
            block, block, (((1,), (1,)), ((), ())), preferred_element_type=jnp.float32
        )

    @pl.when(step == pl.num_programs(0) - 1)
    def _():
        rows, cols = positions(frames)
        first, second = sums_ref[0], sums_ref[1]
        mixed = jnp.where(rows >= cols, first, second)
        diagonal = jnp.sum(jnp.where(rows == cols, second, 0.0), axis=1, keepdims=True)
        packed_ref[...] = jnp.zeros_like(packed_ref)
        packed_ref[0:frames, 0:frames] = mixed
        packed_ref[0:frames, frames : frames + 1] = diagonal


def packed_grams(data, start, size):
    subjects, frames, voxels = data.shape
    features = start.shape[1]
    tile = 2048
    return pl.pallas_call(
        gram_kernel,
        grid=(voxels // tile,),
        in_specs=[pl.BlockSpec((subjects, frames, tile), lambda i: (0, 0, i)), VMEM],
        out_specs=[VMEM, VMEM],
        out_shape=[
            pltpu.VMEM((size, size), jnp.float32),
            pltpu.VMEM((features, size), jnp.bfloat16),
        ],
        scratch_shapes=[pltpu.VMEM((subjects, frames, frames), jnp.float32)],
        name="grams",
    )(data, start)


def parts_of(x, count):
    parts = []
    for part in range(count):
        parts.append(x.astype(jnp.bfloat16))
        if part < count - 1:
            x = x - parts[-1].astype(jnp.float32)
    return parts


def product(a, b, dims=((1,), (0,))):
    return lax.dot_general(a, b, (dims, ((), ())), preferred_element_type=jnp.float32)


def halves(matrices):
    return [parts_of(matrix, 2) for matrix in matrices]


def times(a, b):
    high, low = b
    wide = jnp.concatenate([high, low], axis=1)
    out = product(jnp.concatenate(a, axis=1), jnp.concatenate([wide, wide], axis=0))
    return out[:, : high.shape[1]] + out[:, high.shape[1] :]


def unpacked(packed, frames):
    rows, cols = positions(packed.shape[0])
    diagonal = packed[:, frames : frames + 1]
    packed = jnp.where(cols < frames, packed, 0.0)
    flipped = packed.T
    return (
        jnp.where(rows >= cols, packed, flipped),
        jnp.where(rows == cols, diagonal, jnp.where(rows < cols, packed, flipped)),
    )


def refit(grams, shared):
    crossed = [sum(product(shared, part) for part in parts) for parts in grams]
    wide = shared.astype(jnp.float32)
    squares = [jnp.sum(cross * wide) + 1e-06 for cross in crossed]
    split = halves(crossed)
    both = [product(shared, jnp.concatenate(parts, axis=0), ((1,), (1,))) for parts in split]
    features = shared.shape[0]
    current = [
        (pair[:, :features] + pair[:, features:]) * (1.0 / square)
        for pair, square in zip(both, squares)
    ]
    taken, gain = None, 1.0
    for step in range(ITERS - 1):
        parts = halves(current)
        squared = [times(part, part) for part in parts]
        if step > 0:
            moved = [times(own, part) for own, part in zip(halves(taken), parts)]
        half = [1.5 * x - 0.5 * y for x, y in zip(current, squared)]
        cubed = [times(own, part) for own, part in zip(halves(half), parts)]
        if step > 0:
            taken = [1.5 * d + 0.5 * gain * x - 0.5 * y for d, x, y in zip(taken, current, moved)]
        else:
            taken = [0.5 * gain * x for x in current]
        gain *= 1.5
        current = [1.5 * x - 0.5 * y for x, y in zip(half, cubed)]
    moved = [against(own, part) for own, part in zip(halves(taken), split)]
    before = [gain * cross - part for cross, part in zip(crossed, moved)]
    return before, current, [1.0 / jnp.sqrt(square) for square in squares]


def against(a, b):
    high, low = b
    stacked = jnp.concatenate([high, high], axis=0)
    return product(jnp.concatenate(a, axis=1), stacked) + product(a[0], low)


def shares(keep_ref, give_ref, before_ref, current_ref, before, scales):
    width = keep_ref.shape[0]
    ahead, factor = [], []
    for piece in range(2):
        place = block(piece, width)
        ahead.append(sum(1.5 * scale * before_ref[s, place, :] for s, scale in enumerate(scales)))
        factor.append(
            jnp.concatenate(
                [0.5 * scale * current_ref[s, place, :] for s, scale in enumerate(scales)], axis=1
            )
        )
    high, low = parts_of(jnp.concatenate(factor, axis=0), 2)
    split = halves(before)
    upper = jnp.concatenate([parts[0] for parts in split], axis=0)
    lower = jnp.concatenate([parts[1] for parts in split], axis=0)
    moved = product(high, upper) + product(high, lower) + product(low, upper)
    keep_ref[...] = ahead[0] - moved[:width]
    give_ref[...] = ahead[1] - moved[width:]


def finish(grams, shared, keep_ref, give_ref, before_ref, current_ref):
    before, current, scales = refit(grams, shared)
    for subject in range(2):
        before_ref[subject] = before[subject]
        current_ref[subject] = current[subject]
    shares(keep_ref, give_ref, before_ref, current_ref, before, scales)
    return scales


def refit_kernel(frames, packed_ref, shared_ref, *refs):
    grams = [parts_of(gram, 3) for gram in unpacked(packed_ref[...], frames)]
    finish(grams, shared_ref[...], *refs)


def unpack_kernel(frames, packed_ref, parts_ref):
    for subject, gram in enumerate(unpacked(packed_ref[...], frames)):
        for part, half in enumerate(parts_of(gram, 2)):
            parts_ref[subject, part] = half


def last_kernel(parts_ref, own_ref, near_ref, far_ref, both_ref, *refs):
    *refs, scales_ref, shared_ref = refs
    for piece, piece_ref in enumerate((own_ref, near_ref, far_ref, both_ref)):
        shared_ref[block(piece, piece_ref.shape[0]), :] = piece_ref[...]
    grams = [[parts_ref[subject, part] for part in range(2)] for subject in range(2)]
    scales = finish(grams, shared_ref[...], *refs)
    for subject in range(2):
        scales_ref[subject] = jnp.full(scales_ref.shape[1:], scales[subject], jnp.float32)


def project_kernel(before_ref, current_ref, scales_ref, out_ref):
    for subject in range(2):
        before = before_ref[subject]
        moved = against(parts_of(current_ref[subject], 2), parts_of(before, 2))
        projected = (1.5 * before - 0.5 * moved) * scales_ref[subject, 0:1, 0:1]
        out_ref[subject] = projected.T[0 : out_ref.shape[1], :]


def block(piece, width):
    core, side = lax.axis_index("core"), lax.axis_index("x") % 2
    core = 1 - core if piece % 2 else core
    side = 1 - side if piece // 2 else side
    return pl.ds(pl.multiple_of((2 * side + core) * width, width), width)


def call(kernel, name, out, args, scratch=()):
    return pl.pallas_call(
        kernel,
        in_specs=[VMEM] * len(args),
        out_specs=[VMEM] * len(out),
        out_shape=out,
        scratch_shapes=scratch,
        name=name,
    )(*(in_vmem(x) for x in args))


def whole_kernel(*refs):
    pieces, out_ref, whole_ref = refs[:4], refs[4], refs[5]
    for piece, piece_ref in enumerate(pieces):
        whole_ref[block(piece, piece_ref.shape[0]), :] = piece_ref[...]
    out_ref[...] = whole_ref[...].T[0 : out_ref.shape[0], :]


def in_vmem(x):
    return pltpu.with_memory_space_constraint(x, pltpu.VMEM)


def exchanged(pieces, axis):
    return lax.all_to_all(pieces, axis, 0, 0, tiled=True)


def to_everyone(shard, peers):
    return jnp.broadcast_to(shard[None], (peers, *shard.shape))


def swapped(x, core, across):
    cores, chips = lax.axis_size("core"), lax.axis_size("x")
    pairs = []
    for c in range(cores):
        for i in range(chips):
            to = (c ^ core) * chips + (i ^ across)
            pairs.append((c * chips + i, to))
    return lax.ppermute(x, ("core", "x"), pairs)


def all_summed(keep, give, dtype, scale, held):
    chip = keep + swapped(give, 1, 0)
    pieces = exchanged(to_everyone(chip, lax.axis_size("z")), "z")
    total = (jnp.sum(pieces, axis=0) * scale).astype(dtype)
    total, held = lax.optimization_barrier((total, held))
    return (total, swapped(total, 1, 0), swapped(total, 0, 1), swapped(total, 1, 1)), held


def local(data, shared_start):
    frames = data.shape[1]
    features = shared_start.shape[0]
    peers = lax.axis_size(("y", "x"))
    subjects = data.shape[0] * lax.axis_size(("z", "core"))
    size = padded(frames)
    packed, shared = packed_grams(data, shared_start.T, size)
    share = jnp.sum(exchanged(packed.reshape(peers, size // peers, size), ("y", "x")), axis=0)
    packed = exchanged(to_everyone(share, peers), ("y", "x")).reshape(size, size)
    blocks = [pltpu.VMEM((features // 4, size), jnp.float32)] * 2
    crosses = pltpu.VMEM((2, features, size), jnp.float32)
    squares = pltpu.VMEM((2, features, features), jnp.float32)
    keep, give = call(
        functools.partial(refit_kernel, frames), "refits", blocks, (packed, shared),
        [crosses, squares],
    )
    pieces, packed = all_summed(keep, give, jnp.bfloat16, 1.0 / subjects, packed)
    (parts,) = call(
        functools.partial(unpack_kernel, frames), "unpack",
        [pltpu.VMEM((2, 2, size, size), jnp.bfloat16)], (packed,),
    )
    keep, give, *state = call(
        last_kernel, "refits_last",
        [*blocks, crosses, squares, pltpu.VMEM((2, 8, LANES), jnp.float32)],
        (parts, *pieces), [pltpu.VMEM((features, size), jnp.bfloat16)],
    )
    pieces, state = all_summed(keep, give, jnp.float32, 1.0 / subjects, state)
    (projections,) = call(
        project_kernel, "project",
        [jax.ShapeDtypeStruct((2, frames, features), jnp.float32)], state,
    )
    (response,) = call(
        whole_kernel, "whole", [jax.ShapeDtypeStruct((frames, features), jnp.float32)], pieces,
        [pltpu.VMEM((features, size), jnp.float32)],
    )
    return (jnp.swapaxes(projections, 1, 2), response.T)


def solution(mesh):
    sizes = dict(mesh.shape)
    cores, across = 2, 4
    shape = (sizes["subj"] // cores, cores, sizes["vox"] // across, across)
    chips = Mesh(mesh.devices.reshape(shape), ("z", "core", "y", "x"))
    placed = (P(("z", "core"), None, ("y", "x")), P())
    return jax.shard_map(
        local,
        mesh=chips,
        in_specs=placed,
        out_specs=(P(("z", "core"), None, None), P()),
        check_vma=False,
    )
```

time: 83.7 us -> 82.2 us (0.982)
    pallas_call x3 -> x5, Pallas kernels: 5.12 us -> 4.86 us  [call(): pl.pallas_call(kernel, in_specs=[VMEM] * len(args), out_specs=[VMEM] * le...]
  transfers between devices with their start and end apart: 8 -> 8, of which waited for: 6 -> 5; matrix products, arithmetic and copies ran while one was open for 1% -> 0% of each run, Pallas kernels for 0% -> 2%
where the time goes in v5:
time: 82.2 us; the launch traced here: 81.9 us
  blocking collectives  59.3 us (72%)
  starting transfers between devices  9.78 us (12%)
  Pallas kernels  8.03 us (10%)
  waiting for transfers between devices  3.97 us (5%)
    all_to_all x4, blocking collectives, exchanged(): return lax.all_to_all(pieces, axis, 0, 0, tiled=True)  59.3 us
    ppermute x8, starting transfers between devices, swapped(): return lax.ppermute(x, ('core', 'x'), pairs)  9.78 us
    pallas_call x5, Pallas kernels, call(): pl.pallas_call(kernel, in_specs=[VMEM] * len(args), out_specs=[VMEM] * le...  4.86 us
    ppermute x8, waiting for transfers between devices, swapped(): return lax.ppermute(x, ('core', 'x'), pairs)  3.97 us
    pallas_call x1, Pallas kernels, packed_grams(): pl.pallas_call(gram_kernel, grid=(voxels // tile,), in_specs=[pl.BlockSpe...  3.17 us
  transfers between devices with their start and end apart: 8, of which 5 were waited for; matrix products, arithmetic and copies ran while one was open for 0% of the time, Pallas kernels for 2%

profile of v5, /device:TPU:1, one launch (start us, length us, event | category | flops | bytes accessed | tf_op | source)
XLA Modules:
  0.0 81.9 jit_solution(791821181147769510)
XLA Ops:
  0.6 3.2 %grams.1 = (f32[256,256]{1,0:T(8,128)S(1)}, bf16[128,256]{1,0:T(8,128)(2,1)S(1)}) custom-call(bf16[2,240,4096]{2,1,0:T(8,128)(2,1)} %data_ref.1, bf16[240,128]{1,0:T(8,128)(2,1)} %bitcast.10), custom_call_target="tpu_custom_call" | custom-call | tf_op jit(solution)/shard_map/grams/pallas_call | solution.py:56
  3.8 14.9 %all_to_all.20 = f32[16,16,256]{2,1,0:T(8,128)S(1)} all-to-all(f32[16,16,256]{2,1,0:T(8,128)S(1)} %bitcast.7), channel_id=1, replica_groups=mesh['z'=8,'core'=2,'y'=4,'x'=4] {'y','x'}, dimensions={0} | all-to-all | bytes 524288 | tf_op jit(solution)/shard_map/all_to_all | solution.py:229
  18.8 10.5 %all_to_all.21 = f32[16,16,256]{2,1,0:T(8,128)S(1)} all-to-all(f32[16,16,256]{2,1,0:T(8,128)S(1)} %broadcast_in_dim.6), channel_id=1, replica_groups=mesh['z'=8,'core'=2,'y'=4,'x'=4] {'y','x'}, dimensions={0} | all-to-all | bytes 524288 | tf_op jit(solution)/shard_map/all_to_all | solution.py:229
  29.2 1.5 %refits.1 = (f32[32,256]{1,0:T(8,128)S(1)}, f32[32,256]{1,0:T(8,128)S(1)}) custom-call(f32[256,256]{1,0:T(8,128)S(1)} %bitcast.5, bf16[128,256]{1,0:T(8,128)(2,1)S(1)} %get-tuple-element.18.shared_ref), custom_call_target="tpu_custom_call" | custom-call | tf_op jit(solution)/shard_map/refits/pallas_call | solution.py:207
  30.8 3.3 %collective-permute-start = (f32[32,256]{1,0:T(8,128)S(1)}, f32[32,256]{1,0:T(8,128)S(1)}, u32[]{:S(2)}, u32[]{:S(2)}) collective-permute-start(f32[32,256]{1,0:T(8,128)S(1)} %get-tuple-element.20), channel_id=1, source_target_pairs={{0,16},{1,17},{2,18},{3,19},{16,0},{17,1},{18,2},{19,3},{4,20},{5,... | collective-permute-start | bytes 98312 | tf_op jit(solution)/shard_map/ppermute | solution.py:243
  34.1 0.9 %collective-permute-done = f32[32,256]{1,0:T(8,128)S(1)} collective-permute-done((f32[32,256]{1,0:T(8,128)S(1)}, f32[32,256]{1,0:T(8,128)S(1)}, u32[]{:S(2)}, u32[]{:S(2)}) %collective-permute-start) | collective-permute-done | bytes 32800 | tf_op jit(solution)/shard_map/ppermute | solution.py:243
  35.0 19.2 %all_to_all.22 = f32[8,32,256]{2,1,0:T(8,128)S(1)} all-to-all(f32[8,32,256]{2,1,0:T(8,128)S(1)} %broadcast_in_dim.7), channel_id=1, replica_groups=mesh['z'=8,'core'=2,'y'=4,'x'=4] {'z'}, dimensions={0} | all-to-all | bytes 524288 | tf_op jit(solution)/shard_map/all_to_all | solution.py:229
  54.2 1.9 %collective-permute-start.3 = (bf16[32,256]{1,0:T(8,128)(2,1)S(1)}, bf16[32,256]{1,0:T(8,128)(2,1)S(1)}, u32[]{:S(2)}, u32[]{:S(2)}) collective-permute-start(bf16[32,256]{1,0:T(8,128)(2,1)S(1)} %multiply_convert_fusion.own_ref), channel_id=1, source_target_pairs={{0,17},{1,16},{2,19},{3,18},{16,1},{17,0},{18,3},{19,2},{4,21},{5,... | collective-permute-start | bytes 49160 | tf_op jit(solution)/shard_map/ppermute | solution.py:243
  56.1 1.2 %collective-permute-start.2 = (bf16[32,256]{1,0:T(8,128)(2,1)S(1)}, bf16[32,256]{1,0:T(8,128)(2,1)S(1)}, u32[]{:S(2)}, u32[]{:S(2)}) collective-permute-start(bf16[32,256]{1,0:T(8,128)(2,1)S(1)} %multiply_convert_fusion.own_ref), channel_id=1, source_target_pairs={{0,1},{1,0},{2,3},{3,2},{16,17},{17,16},{18,19},{19,18},{4,5},{5,4... | collective-permute-start | bytes 49160 | tf_op jit(solution)/shard_map/ppermute | solution.py:243
  57.3 0.0 collective-permute-start.1
  57.3 0.2 unpack.1.parts_ref
  57.5 0.0 collective-permute-done.3.both_ref
  57.5 1.2 %collective-permute-done.2.far_ref = bf16[32,256]{1,0:T(8,128)(2,1)S(1)} collective-permute-done((bf16[32,256]{1,0:T(8,128)(2,1)S(1)}, bf16[32,256]{1,0:T(8,128)(2,1)S(1)}, u32[]{:S(2)}, u32[]{:S(2)}) %collective-permute-start.2) | collective-permute-done | bytes 16416 | tf_op jit(solution)/shard_map/ppermute | solution.py:243
  58.7 0.0 collective-permute-done.1.near_ref
  58.7 1.3 %refits_last.1 = (f32[32,256]{1,0:T(8,128)S(1)}, f32[32,256]{1,0:T(8,128)S(1)}, f32[2,128,256]{2,1,0:T(8,128)S(1)}, f32[2,128,128]{2,1,0:T(8,128)S(1)}, f32[2,8,128]{2,1,0:T(8,128)S(1)}) custom-call(bf16[2,2,256,256]{3,2,1,0:T(8,128)(2,1)S(1)} %unpack.1.parts_ref, bf16[32,256]{1,0:T(8,128)(2,1)S(1)} %multiply_convert_fusion.own_ref, ...), custom_call_target="tpu_custom_call" | custom-call | tf_op jit(solution)/shard_map/refits_last/pallas_call | solution.py:207
  60.0 1.2 %collective-permute-start.4 = (f32[32,256]{1,0:T(8,128)S(1)}, f32[32,256]{1,0:T(8,128)S(1)}, u32[]{:S(2)}, u32[]{:S(2)}) collective-permute-start(f32[32,256]{1,0:T(8,128)S(1)} %get-tuple-element.24), channel_id=1, source_target_pairs={{0,16},{1,17},{2,18},{3,19},{16,0},{17,1},{18,2},{19,3},{4,20},{5,... | collective-permute-start | bytes 98312 | tf_op jit(solution)/shard_map/ppermute | solution.py:243
  61.2 0.9 %collective-permute-done.4 = f32[32,256]{1,0:T(8,128)S(1)} collective-permute-done((f32[32,256]{1,0:T(8,128)S(1)}, f32[32,256]{1,0:T(8,128)S(1)}, u32[]{:S(2)}, u32[]{:S(2)}) %collective-permute-start.4) | collective-permute-done | bytes 32800 | tf_op jit(solution)/shard_map/ppermute | solution.py:243
  62.1 14.8 %all_to_all.23 = f32[8,32,256]{2,1,0:T(8,128)S(1)} all-to-all(f32[8,32,256]{2,1,0:T(8,128)S(1)} %broadcast_in_dim.8), channel_id=1, replica_groups=mesh['z'=8,'core'=2,'y'=4,'x'=4] {'z'}, dimensions={0} | all-to-all | bytes 524288 | tf_op jit(solution)/shard_map/all_to_all | solution.py:229
  76.9 0.9 %collective-permute-start.7 = (f32[32,256]{1,0:T(8,128)S(1)}, f32[32,256]{1,0:T(8,128)S(1)}, u32[]{:S(2)}, u32[]{:S(2)}) collective-permute-start(f32[32,256]{1,0:T(8,128)S(1)} %broadcast_multiply_fusion.refs_0_), channel_id=1, source_target_pairs={{0,17},{1,16},{2,19},{3,18},{16,1},{17,0},{18,3},{19,2},{4,21},{5,... | collective-permute-start | bytes 98312 | tf_op jit(solution)/shard_map/ppermute | solution.py:243
  77.8 1.0 %collective-permute-start.6 = (f32[32,256]{1,0:T(8,128)S(1)}, f32[32,256]{1,0:T(8,128)S(1)}, u32[]{:S(2)}, u32[]{:S(2)}) collective-permute-start(f32[32,256]{1,0:T(8,128)S(1)} %broadcast_multiply_fusion.refs_0_), channel_id=1, source_target_pairs={{0,1},{1,0},{2,3},{3,2},{16,17},{17,16},{18,19},{19,18},{4,5},{5,4... | collective-permute-start | bytes 98312 | tf_op jit(solution)/shard_map/ppermute | solution.py:243
  78.8 0.3 collective-permute-start.5
  79.1 1.0 %project.1 = f32[2,240,128]{2,1,0:T(8,128)} custom-call(f32[2,128,256]{2,1,0:T(8,128)S(1)} %get-tuple-element.28.before_ref, f32[2,128,128]{2,1,0:T(8,128)S(1)} %get-tuple-element.29.current_ref, f32[2,8,128]{2,1,0:T(8,128)S(1)} %get-tuple-element.30.scales_ref), custom_call_target="tpu_custom_call" | custom-call | tf_op jit(solution)/shard_map/project/pallas_call | solution.py:207
  80.1 0.5 collective-permute-done.7.refs_3_
  80.7 0.5 collective-permute-done.6.refs_2_
  81.2 0.0 collective-permute-done.5.refs_1_
  81.2 0.8 whole.1
  (10 shorter events, 0.1 us)
Async XLA Ops:
  30.8 4.2 %collective-permute-start = (f32[32,256]{1,0:T(8,128)S(1)}, f32[32,256]{1,0:T(8,128)S(1)}, u32[]{:S(2)}, u32[]{:S(2)}) collective-permute-start(f32[32,256]{1,0:T(8,128)S(1)} %get-tuple-element.20), channel_id=1, source_target_pairs={{0,16},{1,17},{2,18},{3,19},{16,0},{17,1},{18,2},{19,3},{4,20},{5,... | collective-permute-start | bytes 98312 | tf_op jit(solution)/shard_map/ppermute | solution.py:243
  54.2 3.3 %collective-permute-start.3 = (bf16[32,256]{1,0:T(8,128)(2,1)S(1)}, bf16[32,256]{1,0:T(8,128)(2,1)S(1)}, u32[]{:S(2)}, u32[]{:S(2)}) collective-permute-start(bf16[32,256]{1,0:T(8,128)(2,1)S(1)} %multiply_convert_fusion.own_ref), channel_id=1, source_target_pairs={{0,17},{1,16},{2,19},{3,18},{16,1},{17,0},{18,3},{19,2},{4,21},{5,... | collective-permute-start | bytes 49160 | tf_op jit(solution)/shard_map/ppermute | solution.py:243
  56.1 2.6 %collective-permute-start.2 = (bf16[32,256]{1,0:T(8,128)(2,1)S(1)}, bf16[32,256]{1,0:T(8,128)(2,1)S(1)}, u32[]{:S(2)}, u32[]{:S(2)}) collective-permute-start(bf16[32,256]{1,0:T(8,128)(2,1)S(1)} %multiply_convert_fusion.own_ref), channel_id=1, source_target_pairs={{0,1},{1,0},{2,3},{3,2},{16,17},{17,16},{18,19},{19,18},{4,5},{5,4... | collective-permute-start | bytes 49160 | tf_op jit(solution)/shard_map/ppermute | solution.py:243
  57.3 1.4 %collective-permute-start.1 = (bf16[32,256]{1,0:T(8,128)(2,1)S(1)}, bf16[32,256]{1,0:T(8,128)(2,1)S(1)}, u32[]{:S(2)}, u32[]{:S(2)}) collective-permute-start(bf16[32,256]{1,0:T(8,128)(2,1)S(1)} %multiply_convert_fusion.own_ref), channel_id=1, source_target_pairs={{0,16},{1,17},{2,18},{3,19},{16,0},{17,1},{18,2},{19,3},{4,20},{5,... | collective-permute-start | bytes 49160 | tf_op jit(solution)/shard_map/ppermute | solution.py:243
  60.0 2.0 %collective-permute-start.4 = (f32[32,256]{1,0:T(8,128)S(1)}, f32[32,256]{1,0:T(8,128)S(1)}, u32[]{:S(2)}, u32[]{:S(2)}) collective-permute-start(f32[32,256]{1,0:T(8,128)S(1)} %get-tuple-element.24), channel_id=1, source_target_pairs={{0,16},{1,17},{2,18},{3,19},{16,0},{17,1},{18,2},{19,3},{4,20},{5,... | collective-permute-start | bytes 98312 | tf_op jit(solution)/shard_map/ppermute | solution.py:243
  76.9 3.8 %collective-permute-start.7 = (f32[32,256]{1,0:T(8,128)S(1)}, f32[32,256]{1,0:T(8,128)S(1)}, u32[]{:S(2)}, u32[]{:S(2)}) collective-permute-start(f32[32,256]{1,0:T(8,128)S(1)} %broadcast_multiply_fusion.refs_0_), channel_id=1, source_target_pairs={{0,17},{1,16},{2,19},{3,18},{16,1},{17,0},{18,3},{19,2},{4,21},{5,... | collective-permute-start | bytes 98312 | tf_op jit(solution)/shard_map/ppermute | solution.py:243
  77.8 3.4 %collective-permute-start.6 = (f32[32,256]{1,0:T(8,128)S(1)}, f32[32,256]{1,0:T(8,128)S(1)}, u32[]{:S(2)}, u32[]{:S(2)}) collective-permute-start(f32[32,256]{1,0:T(8,128)S(1)} %broadcast_multiply_fusion.refs_0_), channel_id=1, source_target_pairs={{0,1},{1,0},{2,3},{3,2},{16,17},{17,16},{18,19},{19,18},{4,5},{5,4... | collective-permute-start | bytes 98312 | tf_op jit(solution)/shard_map/ppermute | solution.py:243
  78.8 2.4 %collective-permute-start.5 = (f32[32,256]{1,0:T(8,128)S(1)}, f32[32,256]{1,0:T(8,128)S(1)}, u32[]{:S(2)}, u32[]{:S(2)}) collective-permute-start(f32[32,256]{1,0:T(8,128)S(1)} %broadcast_multiply_fusion.refs_0_), channel_id=1, source_target_pairs={{0,16},{1,17},{2,18},{3,19},{16,0},{17,1},{18,2},{19,3},{4,20},{5,... | collective-permute-start | bytes 98312 | tf_op jit(solution)/shard_map/ppermute | solution.py:243

commit v6 on v5

--- a/solution.py
+++ b/solution.py
@@ -23,40 +23,37 @@
 
 
 def gram_kernel(data_ref, start_ref, packed_ref, shared_ref, sums_ref):
-    step = pl.program_id(0)
     frames = data_ref.shape[1]
 
-    @pl.when(step == 0)
+    @pl.when(pl.program_id(0) == 0)
     def _():
-        sums_ref[...] = jnp.zeros_like(sums_ref)
         shared_ref[...] = jnp.zeros_like(shared_ref)
         shared_ref[:, 0:frames] = start_ref[...].T
-
-    for subject in range(2):
-        block = data_ref[subject]
-        sums_ref[subject] += lax.dot_general(
-            block, block, (((1,), (1,)), ((), ())), preferred_element_type=jnp.float32
+        packed_ref[...] = jnp.zeros_like(packed_ref)
+        for subject in range(2):
+            block = data_ref[subject]
+            sums_ref[subject] = product(block, block, ((1,), (1,)))
+
+    @pl.when(pl.program_id(0) == 1)
+    def _():
+        first, second = (
+            sums_ref[subject] + product(data_ref[subject], data_ref[subject], ((1,), (1,)))
+            for subject in range(2)
         )
-
-    @pl.when(step == pl.num_programs(0) - 1)
-    def _():
         rows, cols = positions(frames)
-        first, second = sums_ref[0], sums_ref[1]
-        mixed = jnp.where(rows >= cols, first, second)
-        diagonal = jnp.sum(jnp.where(rows == cols, second, 0.0), axis=1, keepdims=True)
-        packed_ref[...] = jnp.zeros_like(packed_ref)
-        packed_ref[0:frames, 0:frames] = mixed
-        packed_ref[0:frames, frames : frames + 1] = diagonal
+        packed_ref[0:frames, 0:frames] = jnp.where(rows >= cols, first, second)
+        packed_ref[0:frames, frames : frames + 1] = jnp.sum(
+            jnp.where(rows == cols, second, 0.0), axis=1, keepdims=True
+        )
 
 
 def packed_grams(data, start, size):
     subjects, frames, voxels = data.shape
     features = start.shape[1]
-    tile = 2048
     return pl.pallas_call(
         gram_kernel,
-        grid=(voxels // tile,),
-        in_specs=[pl.BlockSpec((subjects, frames, tile), lambda i: (0, 0, i)), VMEM],
+        grid=(2,),
+        in_specs=[pl.BlockSpec((subjects, frames, voxels // 2), lambda i: (0, 0, i)), VMEM],
         out_specs=[VMEM, VMEM],
         out_shape=[
             pltpu.VMEM((size, size), jnp.float32),
@@ -102,17 +99,18 @@
     )
 
 
-def refit(grams, shared):
+def refit(grams, shared, exact):
     crossed = [sum(product(shared, part) for part in parts) for parts in grams]
     wide = shared.astype(jnp.float32)
     squares = [jnp.sum(cross * wide) + 1e-06 for cross in crossed]
-    split = halves(crossed)
-    both = [product(shared, jnp.concatenate(parts, axis=0), ((1,), (1,))) for parts in split]
+    split = [parts_of(cross, 3 if exact else 2) for cross in crossed]
+    both = [product(shared, jnp.concatenate(parts[:2], axis=0), ((1,), (1,))) for parts in split]
     features = shared.shape[0]
-    current = [
-        (pair[:, :features] + pair[:, features:]) * (1.0 / square)
-        for pair, square in zip(both, squares)
-    ]
+    firsts = [pair[:, :features] + pair[:, features:] for pair in both]
+    if exact:
+        lows = [product(shared, parts[2], ((1,), (1,))) for parts in split]
+        firsts = [first + low for first, low in zip(firsts, lows)]
+    current = [first * (1.0 / square) for first, square in zip(firsts, squares)]
     taken, gain = None, 1.0
     for step in range(ITERS - 1):
         parts = halves(current)
@@ -133,7 +131,7 @@
 
 
 def against(a, b):
-    high, low = b
+    high, low = b[:2]
     stacked = jnp.concatenate([high, high], axis=0)
     return product(jnp.concatenate(a, axis=1), stacked) + product(a[0], low)
 
@@ -158,8 +156,8 @@
     give_ref[...] = ahead[1] - moved[width:]
 
 
-def finish(grams, shared, keep_ref, give_ref, before_ref, current_ref):
-    before, current, scales = refit(grams, shared)
+def finish(grams, shared, exact, keep_ref, give_ref, before_ref, current_ref):
+    before, current, scales = refit(grams, shared, exact)
     for subject in range(2):
         before_ref[subject] = before[subject]
         current_ref[subject] = current[subject]
@@ -169,21 +167,21 @@
 
 def refit_kernel(frames, packed_ref, shared_ref, *refs):
     grams = [parts_of(gram, 3) for gram in unpacked(packed_ref[...], frames)]
-    finish(grams, shared_ref[...], *refs)
+    finish(grams, shared_ref[...], True, *refs)
 
 
 def unpack_kernel(frames, packed_ref, parts_ref):
     for subject, gram in enumerate(unpacked(packed_ref[...], frames)):
-        for part, half in enumerate(parts_of(gram, 2)):
+        for part, half in enumerate(parts_of(gram, 3)):
             parts_ref[subject, part] = half
 
 
-def last_kernel(parts_ref, own_ref, near_ref, far_ref, both_ref, *refs):
+def last_kernel(parts_ref, own_ref, both_ref, near_ref, far_ref, *refs):
     *refs, scales_ref, shared_ref = refs
     for piece, piece_ref in enumerate((own_ref, near_ref, far_ref, both_ref)):
         shared_ref[block(piece, piece_ref.shape[0]), :] = piece_ref[...]
-    grams = [[parts_ref[subject, part] for part in range(2)] for subject in range(2)]
-    scales = finish(grams, shared_ref[...], *refs)
+    grams = [[parts_ref[subject, part] for part in range(3)] for subject in range(2)]
+    scales = finish(grams, shared_ref[...], False, *refs)
     for subject in range(2):
         scales_ref[subject] = jnp.full(scales_ref.shape[1:], scales[subject], jnp.float32)
 
@@ -214,9 +212,8 @@
     )(*(in_vmem(x) for x in args))
 
 
-def whole_kernel(*refs):
-    pieces, out_ref, whole_ref = refs[:4], refs[4], refs[5]
-    for piece, piece_ref in enumerate(pieces):
+def whole_kernel(own_ref, both_ref, near_ref, far_ref, out_ref, whole_ref):
+    for piece, piece_ref in enumerate((own_ref, near_ref, far_ref, both_ref)):
         whole_ref[block(piece, piece_ref.shape[0]), :] = piece_ref[...]
     out_ref[...] = whole_ref[...].T[0 : out_ref.shape[0], :]
 
@@ -248,7 +245,7 @@
     pieces = exchanged(to_everyone(chip, lax.axis_size("z")), "z")
     total = (jnp.sum(pieces, axis=0) * scale).astype(dtype)
     total, held = lax.optimization_barrier((total, held))
-    return (total, swapped(total, 1, 0), swapped(total, 0, 1), swapped(total, 1, 1)), held
+    return (total, swapped(total, 1, 1), swapped(total, 1, 0), swapped(total, 0, 1)), held
 
 
 def local(data, shared_start):
@@ -270,7 +267,7 @@
     pieces, packed = all_summed(keep, give, jnp.bfloat16, 1.0 / subjects, packed)
     (parts,) = call(
         functools.partial(unpack_kernel, frames), "unpack",
-        [pltpu.VMEM((2, 2, size, size), jnp.bfloat16)], (packed,),
+        [pltpu.VMEM((2, 3, size, size), jnp.bfloat16)], (packed,),
     )
     keep, give, *state = call(
         last_kernel, "refits_last",

time: 82.2 us -> 83.5 us (1.016)
  waiting for transfers between devices: 3.97 us -> 5.86 us
    ppermute x8, waiting for transfers between devices: 3.97 us -> 5.86 us  [swapped(): return lax.ppermute(x, ('core', 'x'), pairs)]
  transfers between devices with their start and end apart: 8 -> 8, of which waited for: 5 -> 4; matrix products, arithmetic and copies ran while one was open for 0% -> 0% of each run, Pallas kernels for 2% -> 2%
where the time goes in v6:
time: 83.5 us; the launch traced here: 83.3 us
  blocking collectives  59.3 us (71%)
  starting transfers between devices  9.12 us (11%)
  Pallas kernels  8.06 us (10%)
  waiting for transfers between devices  5.86 us (7%)
    all_to_all x4, blocking collectives, exchanged(): return lax.all_to_all(pieces, axis, 0, 0, tiled=True)  59.3 us
    ppermute x8, starting transfers between devices, swapped(): return lax.ppermute(x, ('core', 'x'), pairs)  9.12 us
    ppermute x8, waiting for transfers between devices, swapped(): return lax.ppermute(x, ('core', 'x'), pairs)  5.86 us
    pallas_call x5, Pallas kernels, call(): pl.pallas_call(kernel, in_specs=[VMEM] * len(args), out_specs=[VMEM] * le...  4.98 us
    pallas_call x1, Pallas kernels, packed_grams(): pl.pallas_call(gram_kernel, grid=(2,), in_specs=[pl.BlockSpec((subjects,...  3.08 us
  transfers between devices with their start and end apart: 8, of which 4 were waited for; matrix products, arithmetic and copies ran while one was open for 0% of the time, Pallas kernels for 2%

profile of v6, /device:TPU:1, one launch (start us, length us, event | category | flops | bytes accessed | tf_op | source)
XLA Modules:
  0.0 83.3 jit_solution(5843593702969940478)
XLA Ops:
  0.6 3.1 %grams.1 = (f32[256,256]{1,0:T(8,128)S(1)}, bf16[128,256]{1,0:T(8,128)(2,1)S(1)}) custom-call(bf16[2,240,4096]{2,1,0:T(8,128)(2,1)} %data_ref.1, bf16[240,128]{1,0:T(8,128)(2,1)} %bitcast.10), custom_call_target="tpu_custom_call" | custom-call | tf_op jit(solution)/shard_map/grams/pallas_call | solution.py:53
  3.7 14.9 %all_to_all.20 = f32[16,16,256]{2,1,0:T(8,128)S(1)} all-to-all(f32[16,16,256]{2,1,0:T(8,128)S(1)} %bitcast.7), channel_id=1, replica_groups=mesh['z'=8,'core'=2,'y'=4,'x'=4] {'y','x'}, dimensions={0} | all-to-all | bytes 524288 | tf_op jit(solution)/shard_map/all_to_all | solution.py:226
  18.7 10.5 %all_to_all.21 = f32[16,16,256]{2,1,0:T(8,128)S(1)} all-to-all(f32[16,16,256]{2,1,0:T(8,128)S(1)} %broadcast_in_dim.6), channel_id=1, replica_groups=mesh['z'=8,'core'=2,'y'=4,'x'=4] {'y','x'}, dimensions={0} | all-to-all | bytes 524288 | tf_op jit(solution)/shard_map/all_to_all | solution.py:226
  29.1 1.6 %refits.1 = (f32[32,256]{1,0:T(8,128)S(1)}, f32[32,256]{1,0:T(8,128)S(1)}) custom-call(f32[256,256]{1,0:T(8,128)S(1)} %bitcast.5, bf16[128,256]{1,0:T(8,128)(2,1)S(1)} %get-tuple-element.18.shared_ref), custom_call_target="tpu_custom_call" | custom-call | tf_op jit(solution)/shard_map/refits/pallas_call | solution.py:205
  30.7 3.3 %collective-permute-start = (f32[32,256]{1,0:T(8,128)S(1)}, f32[32,256]{1,0:T(8,128)S(1)}, u32[]{:S(2)}, u32[]{:S(2)}) collective-permute-start(f32[32,256]{1,0:T(8,128)S(1)} %get-tuple-element.20), channel_id=1, source_target_pairs={{0,16},{1,17},{2,18},{3,19},{16,0},{17,1},{18,2},{19,3},{4,20},{5,... | collective-permute-start | bytes 98312 | tf_op jit(solution)/shard_map/ppermute | solution.py:240
  34.1 0.9 %collective-permute-done = f32[32,256]{1,0:T(8,128)S(1)} collective-permute-done((f32[32,256]{1,0:T(8,128)S(1)}, f32[32,256]{1,0:T(8,128)S(1)}, u32[]{:S(2)}, u32[]{:S(2)}) %collective-permute-start) | collective-permute-done | bytes 32800 | tf_op jit(solution)/shard_map/ppermute | solution.py:240
  35.0 19.2 %all_to_all.22 = f32[8,32,256]{2,1,0:T(8,128)S(1)} all-to-all(f32[8,32,256]{2,1,0:T(8,128)S(1)} %broadcast_in_dim.7), channel_id=1, replica_groups=mesh['z'=8,'core'=2,'y'=4,'x'=4] {'z'}, dimensions={0} | all-to-all | bytes 524288 | tf_op jit(solution)/shard_map/all_to_all | solution.py:226
  54.2 0.4 collective-permute-start.3
  54.6 1.9 %collective-permute-start.2 = (bf16[32,256]{1,0:T(8,128)(2,1)S(1)}, bf16[32,256]{1,0:T(8,128)(2,1)S(1)}, u32[]{:S(2)}, u32[]{:S(2)}) collective-permute-start(bf16[32,256]{1,0:T(8,128)(2,1)S(1)} %multiply_convert_fusion.own_ref), channel_id=1, source_target_pairs={{0,16},{1,17},{2,18},{3,19},{16,0},{17,1},{18,2},{19,3},{4,20},{5,... | collective-permute-start | bytes 49160 | tf_op jit(solution)/shard_map/ppermute | solution.py:240
  56.5 1.1 %collective-permute-start.1 = (bf16[32,256]{1,0:T(8,128)(2,1)S(1)}, bf16[32,256]{1,0:T(8,128)(2,1)S(1)}, u32[]{:S(2)}, u32[]{:S(2)}) collective-permute-start(bf16[32,256]{1,0:T(8,128)(2,1)S(1)} %multiply_convert_fusion.own_ref), channel_id=1, source_target_pairs={{0,17},{1,16},{2,19},{3,18},{16,1},{17,0},{18,3},{19,2},{4,21},{5,... | collective-permute-start | bytes 49160 | tf_op jit(solution)/shard_map/ppermute | solution.py:240
  57.5 0.2 unpack.1.parts_ref
  57.8 0.0 collective-permute-done.3.far_ref
  57.8 0.0 collective-permute-done.2.near_ref
  57.8 1.8 %collective-permute-done.1.both_ref = bf16[32,256]{1,0:T(8,128)(2,1)S(1)} collective-permute-done((bf16[32,256]{1,0:T(8,128)(2,1)S(1)}, bf16[32,256]{1,0:T(8,128)(2,1)S(1)}, u32[]{:S(2)}, u32[]{:S(2)}) %collective-permute-start.1) | collective-permute-done | bytes 16416 | tf_op jit(solution)/shard_map/ppermute | solution.py:240
  59.6 1.4 %refits_last.1 = (f32[32,256]{1,0:T(8,128)S(1)}, f32[32,256]{1,0:T(8,128)S(1)}, f32[2,128,256]{2,1,0:T(8,128)S(1)}, f32[2,128,128]{2,1,0:T(8,128)S(1)}, f32[2,8,128]{2,1,0:T(8,128)S(1)}) custom-call(bf16[2,3,256,256]{3,2,1,0:T(8,128)(2,1)S(1)} %unpack.1.parts_ref, bf16[32,256]{1,0:T(8,128)(2,1)S(1)} %multiply_convert_fusion.own_ref, ...), custom_call_target="tpu_custom_call" | custom-call | tf_op jit(solution)/shard_map/refits_last/pallas_call | solution.py:205
  61.0 0.3 collective-permute-start.4
  61.3 1.0 %collective-permute-done.4 = f32[32,256]{1,0:T(8,128)S(1)} collective-permute-done((f32[32,256]{1,0:T(8,128)S(1)}, f32[32,256]{1,0:T(8,128)S(1)}, u32[]{:S(2)}, u32[]{:S(2)}) %collective-permute-start.4) | collective-permute-done | bytes 32800 | tf_op jit(solution)/shard_map/ppermute | solution.py:240
  62.3 14.8 %all_to_all.23 = f32[8,32,256]{2,1,0:T(8,128)S(1)} all-to-all(f32[8,32,256]{2,1,0:T(8,128)S(1)} %broadcast_in_dim.8), channel_id=1, replica_groups=mesh['z'=8,'core'=2,'y'=4,'x'=4] {'z'}, dimensions={0} | all-to-all | bytes 524288 | tf_op jit(solution)/shard_map/all_to_all | solution.py:226
  77.1 1.3 %collective-permute-start.7 = (f32[32,256]{1,0:T(8,128)S(1)}, f32[32,256]{1,0:T(8,128)S(1)}, u32[]{:S(2)}, u32[]{:S(2)}) collective-permute-start(f32[32,256]{1,0:T(8,128)S(1)} %broadcast_multiply_fusion.own_ref), channel_id=1, source_target_pairs={{0,1},{1,0},{2,3},{3,2},{16,17},{17,16},{18,19},{19,18},{4,5},{5,4... | collective-permute-start | bytes 98312 | tf_op jit(solution)/shard_map/ppermute | solution.py:240
  78.4 0.7 collective-permute-start.6
  79.2 0.2 collective-permute-start.5
  79.3 1.0 %project.1 = f32[2,240,128]{2,1,0:T(8,128)} custom-call(f32[2,128,256]{2,1,0:T(8,128)S(1)} %get-tuple-element.28.before_ref, f32[2,128,128]{2,1,0:T(8,128)S(1)} %get-tuple-element.29.current_ref, f32[2,8,128]{2,1,0:T(8,128)S(1)} %get-tuple-element.30.scales_ref), custom_call_target="tpu_custom_call" | custom-call | tf_op jit(solution)/shard_map/project/pallas_call | solution.py:205
  80.4 0.0 collective-permute-done.7.far_ref
  80.4 0.0 collective-permute-done.6.near_ref
  80.4 2.1 %collective-permute-done.5.both_ref = f32[32,256]{1,0:T(8,128)S(1)} collective-permute-done((f32[32,256]{1,0:T(8,128)S(1)}, f32[32,256]{1,0:T(8,128)S(1)}, u32[]{:S(2)}, u32[]{:S(2)}) %collective-permute-start.5) | collective-permute-done | bytes 32800 | tf_op jit(solution)/shard_map/ppermute | solution.py:240
  82.5 0.8 whole.1
  (10 shorter events, 0.1 us)
Async XLA Ops:
  30.7 4.2 %collective-permute-start = (f32[32,256]{1,0:T(8,128)S(1)}, f32[32,256]{1,0:T(8,128)S(1)}, u32[]{:S(2)}, u32[]{:S(2)}) collective-permute-start(f32[32,256]{1,0:T(8,128)S(1)} %get-tuple-element.20), channel_id=1, source_target_pairs={{0,16},{1,17},{2,18},{3,19},{16,0},{17,1},{18,2},{19,3},{4,20},{5,... | collective-permute-start | bytes 98312 | tf_op jit(solution)/shard_map/ppermute | solution.py:240
  54.2 3.6 %collective-permute-start.3 = (bf16[32,256]{1,0:T(8,128)(2,1)S(1)}, bf16[32,256]{1,0:T(8,128)(2,1)S(1)}, u32[]{:S(2)}, u32[]{:S(2)}) collective-permute-start(bf16[32,256]{1,0:T(8,128)(2,1)S(1)} %multiply_convert_fusion.own_ref), channel_id=1, source_target_pairs={{0,1},{1,0},{2,3},{3,2},{16,17},{17,16},{18,19},{19,18},{4,5},{5,4... | collective-permute-start | bytes 49160 | tf_op jit(solution)/shard_map/ppermute | solution.py:240
  54.6 3.2 %collective-permute-start.2 = (bf16[32,256]{1,0:T(8,128)(2,1)S(1)}, bf16[32,256]{1,0:T(8,128)(2,1)S(1)}, u32[]{:S(2)}, u32[]{:S(2)}) collective-permute-start(bf16[32,256]{1,0:T(8,128)(2,1)S(1)} %multiply_convert_fusion.own_ref), channel_id=1, source_target_pairs={{0,16},{1,17},{2,18},{3,19},{16,0},{17,1},{18,2},{19,3},{4,20},{5,... | collective-permute-start | bytes 49160 | tf_op jit(solution)/shard_map/ppermute | solution.py:240
  56.5 3.2 %collective-permute-start.1 = (bf16[32,256]{1,0:T(8,128)(2,1)S(1)}, bf16[32,256]{1,0:T(8,128)(2,1)S(1)}, u32[]{:S(2)}, u32[]{:S(2)}) collective-permute-start(bf16[32,256]{1,0:T(8,128)(2,1)S(1)} %multiply_convert_fusion.own_ref), channel_id=1, source_target_pairs={{0,17},{1,16},{2,19},{3,18},{16,1},{17,0},{18,3},{19,2},{4,21},{5,... | collective-permute-start | bytes 49160 | tf_op jit(solution)/shard_map/ppermute | solution.py:240
  61.0 1.3 %collective-permute-start.4 = (f32[32,256]{1,0:T(8,128)S(1)}, f32[32,256]{1,0:T(8,128)S(1)}, u32[]{:S(2)}, u32[]{:S(2)}) collective-permute-start(f32[32,256]{1,0:T(8,128)S(1)} %get-tuple-element.24), channel_id=1, source_target_pairs={{0,16},{1,17},{2,18},{3,19},{16,0},{17,1},{18,2},{19,3},{4,20},{5,... | collective-permute-start | bytes 98312 | tf_op jit(solution)/shard_map/ppermute | solution.py:240
  77.1 3.2 %collective-permute-start.7 = (f32[32,256]{1,0:T(8,128)S(1)}, f32[32,256]{1,0:T(8,128)S(1)}, u32[]{:S(2)}, u32[]{:S(2)}) collective-permute-start(f32[32,256]{1,0:T(8,128)S(1)} %broadcast_multiply_fusion.own_ref), channel_id=1, source_target_pairs={{0,1},{1,0},{2,3},{3,2},{16,17},{17,16},{18,19},{19,18},{4,5},{5,4... | collective-permute-start | bytes 98312 | tf_op jit(solution)/shard_map/ppermute | solution.py:240
  78.4 1.9 %collective-permute-start.6 = (f32[32,256]{1,0:T(8,128)S(1)}, f32[32,256]{1,0:T(8,128)S(1)}, u32[]{:S(2)}, u32[]{:S(2)}) collective-permute-start(f32[32,256]{1,0:T(8,128)S(1)} %broadcast_multiply_fusion.own_ref), channel_id=1, source_target_pairs={{0,16},{1,17},{2,18},{3,19},{16,0},{17,1},{18,2},{19,3},{4,20},{5,... | collective-permute-start | bytes 98312 | tf_op jit(solution)/shard_map/ppermute | solution.py:240
  79.2 3.3 %collective-permute-start.5 = (f32[32,256]{1,0:T(8,128)S(1)}, f32[32,256]{1,0:T(8,128)S(1)}, u32[]{:S(2)}, u32[]{:S(2)}) collective-permute-start(f32[32,256]{1,0:T(8,128)S(1)} %broadcast_multiply_fusion.own_ref), channel_id=1, source_target_pairs={{0,17},{1,16},{2,19},{3,18},{16,1},{17,0},{18,3},{19,2},{4,21},{5,... | collective-permute-start | bytes 98312 | tf_op jit(solution)/shard_map/ppermute | solution.py:240

commit v7 on v6

--- a/solution.py
+++ b/solution.py
@@ -176,7 +176,7 @@
             parts_ref[subject, part] = half
 
 
-def last_kernel(parts_ref, own_ref, both_ref, near_ref, far_ref, *refs):
+def last_kernel(parts_ref, own_ref, near_ref, far_ref, both_ref, *refs):
     *refs, scales_ref, shared_ref = refs
     for piece, piece_ref in enumerate((own_ref, near_ref, far_ref, both_ref)):
         shared_ref[block(piece, piece_ref.shape[0]), :] = piece_ref[...]
@@ -212,7 +212,7 @@
     )(*(in_vmem(x) for x in args))
 
 
-def whole_kernel(own_ref, both_ref, near_ref, far_ref, out_ref, whole_ref):
+def whole_kernel(own_ref, near_ref, far_ref, both_ref, out_ref, whole_ref):
     for piece, piece_ref in enumerate((own_ref, near_ref, far_ref, both_ref)):
         whole_ref[block(piece, piece_ref.shape[0]), :] = piece_ref[...]
     out_ref[...] = whole_ref[...].T[0 : out_ref.shape[0], :]
@@ -240,12 +240,24 @@
     return lax.ppermute(x, ("core", "x"), pairs)
 
 
+def along(x, mask):
+    chips = lax.axis_size("z")
+    return lax.ppermute(x, "z", [(chip, chip ^ mask) for chip in range(chips)])
+
+
+def four_kernel(own_ref, near_ref, far_ref, next_ref, out_ref):
+    out_ref[...] = (own_ref[...] + near_ref[...]) + (far_ref[...] + next_ref[...])
+
+
 def all_summed(keep, give, dtype, scale, held):
-    chip = keep + swapped(give, 1, 0)
-    pieces = exchanged(to_everyone(chip, lax.axis_size("z")), "z")
-    total = (jnp.sum(pieces, axis=0) * scale).astype(dtype)
+    total = keep + swapped(give, 1, 0)
+    (total,) = call(
+        four_kernel, "four", [pltpu.VMEM(keep.shape, jnp.float32)],
+        (total, along(total, 1), along(total, 6), along(total, 7)),
+    )
+    total = ((total + along(total, 2)) * scale).astype(dtype)
     total, held = lax.optimization_barrier((total, held))
-    return (total, swapped(total, 1, 1), swapped(total, 1, 0), swapped(total, 0, 1)), held
+    return (total, swapped(total, 1, 0), swapped(total, 0, 1), swapped(total, 1, 1)), held
 
 
 def local(data, shared_start):

time: 83.5 us -> 77.6 us (0.929)
  blocking collectives: 59.3 us -> 25.4 us
  starting transfers between devices: 9.12 us -> 28.8 us
  waiting for transfers between devices: 5.86 us -> 14.4 us
    all_to_all x4 -> x2, blocking collectives: 59.3 us -> 25.4 us  [exchanged(): return lax.all_to_all(pieces, axis, 0, 0, tiled=True)]
    ppermute x0 -> x8, starting transfers between devices: none -> 15.5 us  [along(): return lax.ppermute(x, 'z', [(chip, chip ^ mask) for chip in range(chips)])]
    ppermute x0 -> x8, waiting for transfers between devices: none -> 10.4 us  [along(): return lax.ppermute(x, 'z', [(chip, chip ^ mask) for chip in range(chips)])]
    ppermute x8, starting transfers between devices: 9.12 us -> 13.3 us  [swapped(): return lax.ppermute(x, ('core', 'x'), pairs)]
    ppermute x8, waiting for transfers between devices: 5.86 us -> 3.99 us  [swapped(): return lax.ppermute(x, ('core', 'x'), pairs)]
    pallas_call x5 -> x7, Pallas kernels: 4.98 us -> 5 us  [call(): pl.pallas_call(kernel, in_specs=[VMEM] * len(args), out_specs=[VMEM] * le...]
  transfers between devices with their start and end apart: 8 -> 16, of which waited for: 4 -> 9; matrix products, arithmetic and copies ran while one was open for 0% -> 0% of each run, Pallas kernels for 2% -> 2%
where the time goes in v7:
time: 77.6 us; the launch traced here: 77.5 us
  starting transfers between devices  28.8 us (37%)
  blocking collectives  25.4 us (33%)
  waiting for transfers between devices  14.4 us (19%)
  Pallas kernels  8.09 us (10%)
    all_to_all x2, blocking collectives, exchanged(): return lax.all_to_all(pieces, axis, 0, 0, tiled=True)  25.4 us
    ppermute x8, starting transfers between devices, along(): return lax.ppermute(x, 'z', [(chip, chip ^ mask) for chip in range(chips)])  15.5 us
    ppermute x8, starting transfers between devices, swapped(): return lax.ppermute(x, ('core', 'x'), pairs)  13.3 us
    ppermute x8, waiting for transfers between devices, along(): return lax.ppermute(x, 'z', [(chip, chip ^ mask) for chip in range(chips)])  10.4 us
    pallas_call x7, Pallas kernels, call(): pl.pallas_call(kernel, in_specs=[VMEM] * len(args), out_specs=[VMEM] * le...  5 us
    ppermute x8, waiting for transfers between devices, swapped(): return lax.ppermute(x, ('core', 'x'), pairs)  3.99 us
    pallas_call x1, Pallas kernels, packed_grams(): pl.pallas_call(gram_kernel, grid=(2,), in_specs=[pl.BlockSpec((subjects,...  3.08 us
  transfers between devices with their start and end apart: 16, of which 9 were waited for; matrix products, arithmetic and copies ran while one was open for 0% of the time, Pallas kernels for 2%

profile of v7, /device:TPU:1, one launch (start us, length us, event | category | flops | bytes accessed | tf_op | source)
XLA Modules:
  0.0 77.5 jit_solution(9853925602298329909)
XLA Ops:
  0.6 3.1 %grams.1 = (f32[256,256]{1,0:T(8,128)S(1)}, bf16[128,256]{1,0:T(8,128)(2,1)S(1)}) custom-call(bf16[2,240,4096]{2,1,0:T(8,128)(2,1)} %data_ref.1, bf16[240,128]{1,0:T(8,128)(2,1)} %bitcast.10), custom_call_target="tpu_custom_call" | custom-call | tf_op jit(solution)/shard_map/grams/pallas_call | solution.py:53
  3.7 14.9 %all_to_all.10 = f32[16,16,256]{2,1,0:T(8,128)S(1)} all-to-all(f32[16,16,256]{2,1,0:T(8,128)S(1)} %bitcast.7), channel_id=1, replica_groups=mesh['z'=8,'core'=2,'y'=4,'x'=4] {'y','x'}, dimensions={0} | all-to-all | bytes 524288 | tf_op jit(solution)/shard_map/all_to_all | solution.py:226
  18.7 10.5 %all_to_all.11 = f32[16,16,256]{2,1,0:T(8,128)S(1)} all-to-all(f32[16,16,256]{2,1,0:T(8,128)S(1)} %broadcast_in_dim.2), channel_id=1, replica_groups=mesh['z'=8,'core'=2,'y'=4,'x'=4] {'y','x'}, dimensions={0} | all-to-all | bytes 524288 | tf_op jit(solution)/shard_map/all_to_all | solution.py:226
  29.1 1.6 %refits.1 = (f32[32,256]{1,0:T(8,128)S(1)}, f32[32,256]{1,0:T(8,128)S(1)}) custom-call(f32[256,256]{1,0:T(8,128)S(1)} %bitcast.5, bf16[128,256]{1,0:T(8,128)(2,1)S(1)} %get-tuple-element.18.shared_ref), custom_call_target="tpu_custom_call" | custom-call | tf_op jit(solution)/shard_map/refits/pallas_call | solution.py:205
  30.7 3.3 %collective-permute-start = (f32[32,256]{1,0:T(8,128)S(1)}, f32[32,256]{1,0:T(8,128)S(1)}, u32[]{:S(2)}, u32[]{:S(2)}) collective-permute-start(f32[32,256]{1,0:T(8,128)S(1)} %get-tuple-element.20), channel_id=1, source_target_pairs={{0,16},{1,17},{2,18},{3,19},{16,0},{17,1},{18,2},{19,3},{4,20},{5,... | collective-permute-start | bytes 98312 | tf_op jit(solution)/shard_map/ppermute | solution.py:240
  34.1 0.9 %collective-permute-done = f32[32,256]{1,0:T(8,128)S(1)} collective-permute-done((f32[32,256]{1,0:T(8,128)S(1)}, f32[32,256]{1,0:T(8,128)S(1)}, u32[]{:S(2)}, u32[]{:S(2)}) %collective-permute-start) | collective-permute-done | bytes 32800 | tf_op jit(solution)/shard_map/ppermute | solution.py:240
  34.9 5.6 %collective-permute-start.3 = (f32[32,256]{1,0:T(8,128)S(1)}, f32[32,256]{1,0:T(8,128)S(1)}, u32[]{:S(2)}, u32[]{:S(2)}) collective-permute-start(f32[32,256]{1,0:T(8,128)S(1)} %add.12.own_ref), channel_id=1, source_target_pairs={{0,224},{32,192},{64,160},{96,128},{128,96},{160,64},{192,32},{224... | collective-permute-start | bytes 98312 | tf_op jit(solution)/shard_map/ppermute | solution.py:245
  40.5 0.5 collective-permute-start.2
  41.0 1.1 %collective-permute-start.1 = (f32[32,256]{1,0:T(8,128)S(1)}, f32[32,256]{1,0:T(8,128)S(1)}, u32[]{:S(2)}, u32[]{:S(2)}) collective-permute-start(f32[32,256]{1,0:T(8,128)S(1)} %add.12.own_ref), channel_id=1, source_target_pairs={{0,32},{32,0},{64,96},{96,64},{128,160},{160,128},{192,224},{224,1... | collective-permute-start | bytes 98312 | tf_op jit(solution)/shard_map/ppermute | solution.py:245
  42.1 3.2 %collective-permute-done.2.far_ref = f32[32,256]{1,0:T(8,128)S(1)} collective-permute-done((f32[32,256]{1,0:T(8,128)S(1)}, f32[32,256]{1,0:T(8,128)S(1)}, u32[]{:S(2)}, u32[]{:S(2)}) %collective-permute-start.2) | collective-permute-done | bytes 32800 | tf_op jit(solution)/shard_map/ppermute | solution.py:245
  45.4 0.0 collective-permute-done.1.near_ref
  45.4 2.2 %collective-permute-start.4 = (f32[32,256]{1,0:T(8,128)S(1)}, f32[32,256]{1,0:T(8,128)S(1)}, u32[]{:S(2)}, u32[]{:S(2)}) collective-permute-start(f32[32,256]{1,0:T(8,128)S(1)} %four.2), channel_id=1, source_target_pairs={{0,64},{32,96},{64,0},{96,32},{128,192},{160,224},{192,128},{224,1... | collective-permute-start | bytes 98312 | tf_op jit(solution)/shard_map/ppermute | solution.py:245
  47.6 1.6 %collective-permute-done.4 = f32[32,256]{1,0:T(8,128)S(1)} collective-permute-done((f32[32,256]{1,0:T(8,128)S(1)}, f32[32,256]{1,0:T(8,128)S(1)}, u32[]{:S(2)}, u32[]{:S(2)}) %collective-permute-start.4) | collective-permute-done | bytes 32800 | tf_op jit(solution)/shard_map/ppermute | solution.py:245
  49.2 3.2 %collective-permute-start.7 = (bf16[32,256]{1,0:T(8,128)(2,1)S(1)}, bf16[32,256]{1,0:T(8,128)(2,1)S(1)}, u32[]{:S(2)}, u32[]{:S(2)}) collective-permute-start(bf16[32,256]{1,0:T(8,128)(2,1)S(1)} %multiply_convert_fusion.own_ref), channel_id=1, source_target_pairs={{0,17},{1,16},{2,19},{3,18},{16,1},{17,0},{18,3},{19,2},{4,21},{5,... | collective-permute-start | bytes 49160 | tf_op jit(solution)/shard_map/ppermute | solution.py:240
  52.4 1.2 %collective-permute-start.6 = (bf16[32,256]{1,0:T(8,128)(2,1)S(1)}, bf16[32,256]{1,0:T(8,128)(2,1)S(1)}, u32[]{:S(2)}, u32[]{:S(2)}) collective-permute-start(bf16[32,256]{1,0:T(8,128)(2,1)S(1)} %multiply_convert_fusion.own_ref), channel_id=1, source_target_pairs={{0,1},{1,0},{2,3},{3,2},{16,17},{17,16},{18,19},{19,18},{4,5},{5,4... | collective-permute-start | bytes 49160 | tf_op jit(solution)/shard_map/ppermute | solution.py:240
  53.5 0.0 collective-permute-start.5
  53.5 0.2 unpack.1.parts_ref
  53.8 1.2 %collective-permute-done.6.far_ref = bf16[32,256]{1,0:T(8,128)(2,1)S(1)} collective-permute-done((bf16[32,256]{1,0:T(8,128)(2,1)S(1)}, bf16[32,256]{1,0:T(8,128)(2,1)S(1)}, u32[]{:S(2)}, u32[]{:S(2)}) %collective-permute-start.6) | collective-permute-done | bytes 16416 | tf_op jit(solution)/shard_map/ppermute | solution.py:240
  55.0 1.4 %refits_last.1 = (f32[32,256]{1,0:T(8,128)S(1)}, f32[32,256]{1,0:T(8,128)S(1)}, f32[2,128,256]{2,1,0:T(8,128)S(1)}, f32[2,128,128]{2,1,0:T(8,128)S(1)}, f32[2,8,128]{2,1,0:T(8,128)S(1)}) custom-call(bf16[2,3,256,256]{3,2,1,0:T(8,128)(2,1)S(1)} %unpack.1.parts_ref, bf16[32,256]{1,0:T(8,128)(2,1)S(1)} %multiply_convert_fusion.own_ref, ...), custom_call_target="tpu_custom_call" | custom-call | tf_op jit(solution)/shard_map/refits_last/pallas_call | solution.py:205
  56.3 1.2 %collective-permute-start.8 = (f32[32,256]{1,0:T(8,128)S(1)}, f32[32,256]{1,0:T(8,128)S(1)}, u32[]{:S(2)}, u32[]{:S(2)}) collective-permute-start(f32[32,256]{1,0:T(8,128)S(1)} %get-tuple-element.24), channel_id=1, source_target_pairs={{0,16},{1,17},{2,18},{3,19},{16,0},{17,1},{18,2},{19,3},{4,20},{5,... | collective-permute-start | bytes 98312 | tf_op jit(solution)/shard_map/ppermute | solution.py:240
  57.5 0.9 %collective-permute-done.8 = f32[32,256]{1,0:T(8,128)S(1)} collective-permute-done((f32[32,256]{1,0:T(8,128)S(1)}, f32[32,256]{1,0:T(8,128)S(1)}, u32[]{:S(2)}, u32[]{:S(2)}) %collective-permute-start.8) | collective-permute-done | bytes 32800 | tf_op jit(solution)/shard_map/ppermute | solution.py:240
  58.4 2.2 %collective-permute-start.11 = (f32[32,256]{1,0:T(8,128)S(1)}, f32[32,256]{1,0:T(8,128)S(1)}, u32[]{:S(2)}, u32[]{:S(2)}) collective-permute-start(f32[32,256]{1,0:T(8,128)S(1)} %add.14.own_ref), channel_id=1, source_target_pairs={{0,224},{32,192},{64,160},{96,128},{128,96},{160,64},{192,32},{224... | collective-permute-start | bytes 98312 | tf_op jit(solution)/shard_map/ppermute | solution.py:245
  60.5 2.7 %collective-permute-start.10 = (f32[32,256]{1,0:T(8,128)S(1)}, f32[32,256]{1,0:T(8,128)S(1)}, u32[]{:S(2)}, u32[]{:S(2)}) collective-permute-start(f32[32,256]{1,0:T(8,128)S(1)} %add.14.own_ref), channel_id=1, source_target_pairs={{0,192},{32,224},{64,128},{96,160},{128,64},{160,96},{192,0},{224,... | collective-permute-start | bytes 98312 | tf_op jit(solution)/shard_map/ppermute | solution.py:245
  63.3 2.5 %collective-permute-done.10.far_ref = f32[32,256]{1,0:T(8,128)S(1)} collective-permute-done((f32[32,256]{1,0:T(8,128)S(1)}, f32[32,256]{1,0:T(8,128)S(1)}, u32[]{:S(2)}, u32[]{:S(2)}) %collective-permute-start.10) | collective-permute-done | bytes 32800 | tf_op jit(solution)/shard_map/ppermute | solution.py:245
  65.7 0.6 collective-permute-done.9.near_ref
  66.3 1.2 %collective-permute-start.12 = (f32[32,256]{1,0:T(8,128)S(1)}, f32[32,256]{1,0:T(8,128)S(1)}, u32[]{:S(2)}, u32[]{:S(2)}) collective-permute-start(f32[32,256]{1,0:T(8,128)S(1)} %four.3), channel_id=1, source_target_pairs={{0,64},{32,96},{64,0},{96,32},{128,192},{160,224},{192,128},{224,1... | collective-permute-start | bytes 98312 | tf_op jit(solution)/shard_map/ppermute | solution.py:245
  67.6 2.5 %collective-permute-done.12 = f32[32,256]{1,0:T(8,128)S(1)} collective-permute-done((f32[32,256]{1,0:T(8,128)S(1)}, f32[32,256]{1,0:T(8,128)S(1)}, u32[]{:S(2)}, u32[]{:S(2)}) %collective-permute-start.12) | collective-permute-done | bytes 32800 | tf_op jit(solution)/shard_map/ppermute | solution.py:245
  70.1 3.4 %collective-permute-start.15 = (f32[32,256]{1,0:T(8,128)S(1)}, f32[32,256]{1,0:T(8,128)S(1)}, u32[]{:S(2)}, u32[]{:S(2)}) collective-permute-start(f32[32,256]{1,0:T(8,128)S(1)} %add_multiply_fusion.own_ref), channel_id=1, source_target_pairs={{0,17},{1,16},{2,19},{3,18},{16,1},{17,0},{18,3},{19,2},{4,21},{5,... | collective-permute-start | bytes 98312 | tf_op jit(solution)/shard_map/ppermute | solution.py:240
  73.5 1.0 %collective-permute-start.14 = (f32[32,256]{1,0:T(8,128)S(1)}, f32[32,256]{1,0:T(8,128)S(1)}, u32[]{:S(2)}, u32[]{:S(2)}) collective-permute-start(f32[32,256]{1,0:T(8,128)S(1)} %add_multiply_fusion.own_ref), channel_id=1, source_target_pairs={{0,1},{1,0},{2,3},{3,2},{16,17},{17,16},{18,19},{19,18},{4,5},{5,4... | collective-permute-start | bytes 98312 | tf_op jit(solution)/shard_map/ppermute | solution.py:240
  74.6 1.0 %project.1 = f32[2,240,128]{2,1,0:T(8,128)} custom-call(f32[2,128,256]{2,1,0:T(8,128)S(1)} %get-tuple-element.28.before_ref, f32[2,128,128]{2,1,0:T(8,128)S(1)} %get-tuple-element.29.current_ref, f32[2,8,128]{2,1,0:T(8,128)S(1)} %get-tuple-element.30.scales_ref), custom_call_target="tpu_custom_call" | custom-call | tf_op jit(solution)/shard_map/project/pallas_call | solution.py:205
  75.6 1.1 %collective-permute-done.14.far_ref = f32[32,256]{1,0:T(8,128)S(1)} collective-permute-done((f32[32,256]{1,0:T(8,128)S(1)}, f32[32,256]{1,0:T(8,128)S(1)}, u32[]{:S(2)}, u32[]{:S(2)}) %collective-permute-start.14) | collective-permute-done | bytes 32800 | tf_op jit(solution)/shard_map/ppermute | solution.py:240
  76.7 0.8 whole.1
  (16 shorter events, 0.1 us)
Async XLA Ops:
  30.7 4.2 %collective-permute-start = (f32[32,256]{1,0:T(8,128)S(1)}, f32[32,256]{1,0:T(8,128)S(1)}, u32[]{:S(2)}, u32[]{:S(2)}) collective-permute-start(f32[32,256]{1,0:T(8,128)S(1)} %get-tuple-element.20), channel_id=1, source_target_pairs={{0,16},{1,17},{2,18},{3,19},{16,0},{17,1},{18,2},{19,3},{4,20},{5,... | collective-permute-start | bytes 98312 | tf_op jit(solution)/shard_map/ppermute | solution.py:240
  34.9 7.2 %collective-permute-start.3 = (f32[32,256]{1,0:T(8,128)S(1)}, f32[32,256]{1,0:T(8,128)S(1)}, u32[]{:S(2)}, u32[]{:S(2)}) collective-permute-start(f32[32,256]{1,0:T(8,128)S(1)} %add.12.own_ref), channel_id=1, source_target_pairs={{0,224},{32,192},{64,160},{96,128},{128,96},{160,64},{192,32},{224... | collective-permute-start | bytes 98312 | tf_op jit(solution)/shard_map/ppermute | solution.py:245
  40.5 4.9 %collective-permute-start.2 = (f32[32,256]{1,0:T(8,128)S(1)}, f32[32,256]{1,0:T(8,128)S(1)}, u32[]{:S(2)}, u32[]{:S(2)}) collective-permute-start(f32[32,256]{1,0:T(8,128)S(1)} %add.12.own_ref), channel_id=1, source_target_pairs={{0,192},{32,224},{64,128},{96,160},{128,64},{160,96},{192,0},{224,... | collective-permute-start | bytes 98312 | tf_op jit(solution)/shard_map/ppermute | solution.py:245
  41.0 4.3 %collective-permute-start.1 = (f32[32,256]{1,0:T(8,128)S(1)}, f32[32,256]{1,0:T(8,128)S(1)}, u32[]{:S(2)}, u32[]{:S(2)}) collective-permute-start(f32[32,256]{1,0:T(8,128)S(1)} %add.12.own_ref), channel_id=1, source_target_pairs={{0,32},{32,0},{64,96},{96,64},{128,160},{160,128},{192,224},{224,1... | collective-permute-start | bytes 98312 | tf_op jit(solution)/shard_map/ppermute | solution.py:245
  45.4 3.8 %collective-permute-start.4 = (f32[32,256]{1,0:T(8,128)S(1)}, f32[32,256]{1,0:T(8,128)S(1)}, u32[]{:S(2)}, u32[]{:S(2)}) collective-permute-start(f32[32,256]{1,0:T(8,128)S(1)} %four.2), channel_id=1, source_target_pairs={{0,64},{32,96},{64,0},{96,32},{128,192},{160,224},{192,128},{224,1... | collective-permute-start | bytes 98312 | tf_op jit(solution)/shard_map/ppermute | solution.py:245
  49.2 4.6 %collective-permute-start.7 = (bf16[32,256]{1,0:T(8,128)(2,1)S(1)}, bf16[32,256]{1,0:T(8,128)(2,1)S(1)}, u32[]{:S(2)}, u32[]{:S(2)}) collective-permute-start(bf16[32,256]{1,0:T(8,128)(2,1)S(1)} %multiply_convert_fusion.own_ref), channel_id=1, source_target_pairs={{0,17},{1,16},{2,19},{3,18},{16,1},{17,0},{18,3},{19,2},{4,21},{5,... | collective-permute-start | bytes 49160 | tf_op jit(solution)/shard_map/ppermute | solution.py:240
  52.4 2.6 %collective-permute-start.6 = (bf16[32,256]{1,0:T(8,128)(2,1)S(1)}, bf16[32,256]{1,0:T(8,128)(2,1)S(1)}, u32[]{:S(2)}, u32[]{:S(2)}) collective-permute-start(bf16[32,256]{1,0:T(8,128)(2,1)S(1)} %multiply_convert_fusion.own_ref), channel_id=1, source_target_pairs={{0,1},{1,0},{2,3},{3,2},{16,17},{17,16},{18,19},{19,18},{4,5},{5,4... | collective-permute-start | bytes 49160 | tf_op jit(solution)/shard_map/ppermute | solution.py:240
  53.5 1.4 %collective-permute-start.5 = (bf16[32,256]{1,0:T(8,128)(2,1)S(1)}, bf16[32,256]{1,0:T(8,128)(2,1)S(1)}, u32[]{:S(2)}, u32[]{:S(2)}) collective-permute-start(bf16[32,256]{1,0:T(8,128)(2,1)S(1)} %multiply_convert_fusion.own_ref), channel_id=1, source_target_pairs={{0,16},{1,17},{2,18},{3,19},{16,0},{17,1},{18,2},{19,3},{4,20},{5,... | collective-permute-start | bytes 49160 | tf_op jit(solution)/shard_map/ppermute | solution.py:240
  56.3 2.0 %collective-permute-start.8 = (f32[32,256]{1,0:T(8,128)S(1)}, f32[32,256]{1,0:T(8,128)S(1)}, u32[]{:S(2)}, u32[]{:S(2)}) collective-permute-start(f32[32,256]{1,0:T(8,128)S(1)} %get-tuple-element.24), channel_id=1, source_target_pairs={{0,16},{1,17},{2,18},{3,19},{16,0},{17,1},{18,2},{19,3},{4,20},{5,... | collective-permute-start | bytes 98312 | tf_op jit(solution)/shard_map/ppermute | solution.py:240
  58.4 4.9 %collective-permute-start.11 = (f32[32,256]{1,0:T(8,128)S(1)}, f32[32,256]{1,0:T(8,128)S(1)}, u32[]{:S(2)}, u32[]{:S(2)}) collective-permute-start(f32[32,256]{1,0:T(8,128)S(1)} %add.14.own_ref), channel_id=1, source_target_pairs={{0,224},{32,192},{64,160},{96,128},{128,96},{160,64},{192,32},{224... | collective-permute-start | bytes 98312 | tf_op jit(solution)/shard_map/ppermute | solution.py:245
  60.5 5.2 %collective-permute-start.10 = (f32[32,256]{1,0:T(8,128)S(1)}, f32[32,256]{1,0:T(8,128)S(1)}, u32[]{:S(2)}, u32[]{:S(2)}) collective-permute-start(f32[32,256]{1,0:T(8,128)S(1)} %add.14.own_ref), channel_id=1, source_target_pairs={{0,192},{32,224},{64,128},{96,160},{128,64},{160,96},{192,0},{224,... | collective-permute-start | bytes 98312 | tf_op jit(solution)/shard_map/ppermute | solution.py:245
  63.3 3.1 %collective-permute-start.9 = (f32[32,256]{1,0:T(8,128)S(1)}, f32[32,256]{1,0:T(8,128)S(1)}, u32[]{:S(2)}, u32[]{:S(2)}) collective-permute-start(f32[32,256]{1,0:T(8,128)S(1)} %add.14.own_ref), channel_id=1, source_target_pairs={{0,32},{32,0},{64,96},{96,64},{128,160},{160,128},{192,224},{224,1... | collective-permute-start | bytes 98312 | tf_op jit(solution)/shard_map/ppermute | solution.py:245
  66.3 3.8 %collective-permute-start.12 = (f32[32,256]{1,0:T(8,128)S(1)}, f32[32,256]{1,0:T(8,128)S(1)}, u32[]{:S(2)}, u32[]{:S(2)}) collective-permute-start(f32[32,256]{1,0:T(8,128)S(1)} %four.3), channel_id=1, source_target_pairs={{0,64},{32,96},{64,0},{96,32},{128,192},{160,224},{192,128},{224,1... | collective-permute-start | bytes 98312 | tf_op jit(solution)/shard_map/ppermute | solution.py:245
  70.1 5.5 %collective-permute-start.15 = (f32[32,256]{1,0:T(8,128)S(1)}, f32[32,256]{1,0:T(8,128)S(1)}, u32[]{:S(2)}, u32[]{:S(2)}) collective-permute-start(f32[32,256]{1,0:T(8,128)S(1)} %add_multiply_fusion.own_ref), channel_id=1, source_target_pairs={{0,17},{1,16},{2,19},{3,18},{16,1},{17,0},{18,3},{19,2},{4,21},{5,... | collective-permute-start | bytes 98312 | tf_op jit(solution)/shard_map/ppermute | solution.py:240
  73.5 3.2 %collective-permute-start.14 = (f32[32,256]{1,0:T(8,128)S(1)}, f32[32,256]{1,0:T(8,128)S(1)}, u32[]{:S(2)}, u32[]{:S(2)}) collective-permute-start(f32[32,256]{1,0:T(8,128)S(1)} %add_multiply_fusion.own_ref), channel_id=1, source_target_pairs={{0,1},{1,0},{2,3},{3,2},{16,17},{17,16},{18,19},{19,18},{4,5},{5,4... | collective-permute-start | bytes 98312 | tf_op jit(solution)/shard_map/ppermute | solution.py:240
  74.6 2.1 %collective-permute-start.13 = (f32[32,256]{1,0:T(8,128)S(1)}, f32[32,256]{1,0:T(8,128)S(1)}, u32[]{:S(2)}, u32[]{:S(2)}) collective-permute-start(f32[32,256]{1,0:T(8,128)S(1)} %add_multiply_fusion.own_ref), channel_id=1, source_target_pairs={{0,16},{1,17},{2,18},{3,19},{16,0},{17,1},{18,2},{19,3},{4,20},{5,... | collective-permute-start | bytes 98312 | tf_op jit(solution)/shard_map/ppermute | solution.py:240

commit v8 on v7

--- a/solution.py
+++ b/solution.py
@@ -245,7 +245,7 @@
     return lax.ppermute(x, "z", [(chip, chip ^ mask) for chip in range(chips)])
 
 
-def four_kernel(own_ref, near_ref, far_ref, next_ref, out_ref):
+def four_kernel(own_ref, near_ref, next_ref, far_ref, out_ref):
     out_ref[...] = (own_ref[...] + near_ref[...]) + (far_ref[...] + next_ref[...])
 
 
@@ -253,7 +253,7 @@
     total = keep + swapped(give, 1, 0)
     (total,) = call(
         four_kernel, "four", [pltpu.VMEM(keep.shape, jnp.float32)],
-        (total, along(total, 1), along(total, 6), along(total, 7)),
+        (total, along(total, 1), along(total, 7), along(total, 6)),
     )
     total = ((total + along(total, 2)) * scale).astype(dtype)
     total, held = lax.optimization_barrier((total, held))

time: 77.6 us -> 76.8 us (0.990)
  waiting for transfers between devices: 14.4 us -> 13.4 us
    ppermute x8, starting transfers between devices: 15.5 us -> 16.4 us  [along(): return lax.ppermute(x, 'z', [(chip, chip ^ mask) for chip in range(chips)])]
    ppermute x8, waiting for transfers between devices: 10.4 us -> 9.56 us  [along(): return lax.ppermute(x, 'z', [(chip, chip ^ mask) for chip in range(chips)])]
  transfers between devices with their start and end apart: 16 -> 16, of which waited for: 9 -> 11; matrix products, arithmetic and copies ran while one was open for 0% -> 0% of each run, Pallas kernels for 2% -> 2%
where the time goes in v8:
time: 76.8 us; the launch traced here: 76.7 us
  starting transfers between devices  29 us (38%)
  blocking collectives  25.4 us (33%)
  waiting for transfers between devices  13.4 us (17%)
  Pallas kernels  8.09 us (11%)
    all_to_all x2, blocking collectives, exchanged(): return lax.all_to_all(pieces, axis, 0, 0, tiled=True)  25.4 us
    ppermute x8, starting transfers between devices, along(): return lax.ppermute(x, 'z', [(chip, chip ^ mask) for chip in range(chips)])  16.4 us
    ppermute x8, starting transfers between devices, swapped(): return lax.ppermute(x, ('core', 'x'), pairs)  12.6 us
    ppermute x8, waiting for transfers between devices, along(): return lax.ppermute(x, 'z', [(chip, chip ^ mask) for chip in range(chips)])  9.56 us
    pallas_call x7, Pallas kernels, call(): pl.pallas_call(kernel, in_specs=[VMEM] * len(args), out_specs=[VMEM] * le...  5 us
    ppermute x8, waiting for transfers between devices, swapped(): return lax.ppermute(x, ('core', 'x'), pairs)  3.83 us
    pallas_call x1, Pallas kernels, packed_grams(): pl.pallas_call(gram_kernel, grid=(2,), in_specs=[pl.BlockSpec((subjects,...  3.08 us
  transfers between devices with their start and end apart: 16, of which 11 were waited for; matrix products, arithmetic and copies ran while one was open for 0% of the time, Pallas kernels for 2%

profile of v8, /device:TPU:1, one launch (start us, length us, event | category | flops | bytes accessed | tf_op | source)
XLA Modules:
  0.0 76.7 jit_solution(678646136534146540)
XLA Ops:
  0.6 3.1 %grams.1 = (f32[256,256]{1,0:T(8,128)S(1)}, bf16[128,256]{1,0:T(8,128)(2,1)S(1)}) custom-call(bf16[2,240,4096]{2,1,0:T(8,128)(2,1)} %data_ref.1, bf16[240,128]{1,0:T(8,128)(2,1)} %bitcast.10), custom_call_target="tpu_custom_call" | custom-call | tf_op jit(solution)/shard_map/grams/pallas_call | solution.py:53
  3.7 14.9 %all_to_all.10 = f32[16,16,256]{2,1,0:T(8,128)S(1)} all-to-all(f32[16,16,256]{2,1,0:T(8,128)S(1)} %bitcast.7), channel_id=1, replica_groups=mesh['z'=8,'core'=2,'y'=4,'x'=4] {'y','x'}, dimensions={0} | all-to-all | bytes 524288 | tf_op jit(solution)/shard_map/all_to_all | solution.py:226
  18.7 10.5 %all_to_all.11 = f32[16,16,256]{2,1,0:T(8,128)S(1)} all-to-all(f32[16,16,256]{2,1,0:T(8,128)S(1)} %broadcast_in_dim.2), channel_id=1, replica_groups=mesh['z'=8,'core'=2,'y'=4,'x'=4] {'y','x'}, dimensions={0} | all-to-all | bytes 524288 | tf_op jit(solution)/shard_map/all_to_all | solution.py:226
  29.1 1.6 %refits.1 = (f32[32,256]{1,0:T(8,128)S(1)}, f32[32,256]{1,0:T(8,128)S(1)}) custom-call(f32[256,256]{1,0:T(8,128)S(1)} %bitcast.5, bf16[128,256]{1,0:T(8,128)(2,1)S(1)} %get-tuple-element.18.shared_ref), custom_call_target="tpu_custom_call" | custom-call | tf_op jit(solution)/shard_map/refits/pallas_call | solution.py:205
  30.7 3.3 %collective-permute-start = (f32[32,256]{1,0:T(8,128)S(1)}, f32[32,256]{1,0:T(8,128)S(1)}, u32[]{:S(2)}, u32[]{:S(2)}) collective-permute-start(f32[32,256]{1,0:T(8,128)S(1)} %get-tuple-element.20), channel_id=1, source_target_pairs={{0,16},{1,17},{2,18},{3,19},{16,0},{17,1},{18,2},{19,3},{4,20},{5,... | collective-permute-start | bytes 98312 | tf_op jit(solution)/shard_map/ppermute | solution.py:240
  34.1 0.9 %collective-permute-done = f32[32,256]{1,0:T(8,128)S(1)} collective-permute-done((f32[32,256]{1,0:T(8,128)S(1)}, f32[32,256]{1,0:T(8,128)S(1)}, u32[]{:S(2)}, u32[]{:S(2)}) %collective-permute-start) | collective-permute-done | bytes 32800 | tf_op jit(solution)/shard_map/ppermute | solution.py:240
  34.9 6.0 %collective-permute-start.3 = (f32[32,256]{1,0:T(8,128)S(1)}, f32[32,256]{1,0:T(8,128)S(1)}, u32[]{:S(2)}, u32[]{:S(2)}) collective-permute-start(f32[32,256]{1,0:T(8,128)S(1)} %add.12.own_ref), channel_id=1, source_target_pairs={{0,192},{32,224},{64,128},{96,160},{128,64},{160,96},{192,0},{224,... | collective-permute-start | bytes 98312 | tf_op jit(solution)/shard_map/ppermute | solution.py:245
  41.0 1.3 %collective-permute-start.1 = (f32[32,256]{1,0:T(8,128)S(1)}, f32[32,256]{1,0:T(8,128)S(1)}, u32[]{:S(2)}, u32[]{:S(2)}) collective-permute-start(f32[32,256]{1,0:T(8,128)S(1)} %add.12.own_ref), channel_id=1, source_target_pairs={{0,32},{32,0},{64,96},{96,64},{128,160},{160,128},{192,224},{224,1... | collective-permute-start | bytes 98312 | tf_op jit(solution)/shard_map/ppermute | solution.py:245
  42.2 0.1 collective-permute-done.3.far_ref
  42.3 2.6 %collective-permute-done.2.next_ref = f32[32,256]{1,0:T(8,128)S(1)} collective-permute-done((f32[32,256]{1,0:T(8,128)S(1)}, f32[32,256]{1,0:T(8,128)S(1)}, u32[]{:S(2)}, u32[]{:S(2)}) %collective-permute-start.2) | collective-permute-done | bytes 32800 | tf_op jit(solution)/shard_map/ppermute | solution.py:245
  45.0 3.1 %collective-permute-start.4 = (f32[32,256]{1,0:T(8,128)S(1)}, f32[32,256]{1,0:T(8,128)S(1)}, u32[]{:S(2)}, u32[]{:S(2)}) collective-permute-start(f32[32,256]{1,0:T(8,128)S(1)} %four.2), channel_id=1, source_target_pairs={{0,64},{32,96},{64,0},{96,32},{128,192},{160,224},{192,128},{224,1... | collective-permute-start | bytes 98312 | tf_op jit(solution)/shard_map/ppermute | solution.py:245
  48.1 1.3 %collective-permute-done.4 = f32[32,256]{1,0:T(8,128)S(1)} collective-permute-done((f32[32,256]{1,0:T(8,128)S(1)}, f32[32,256]{1,0:T(8,128)S(1)}, u32[]{:S(2)}, u32[]{:S(2)}) %collective-permute-start.4) | collective-permute-done | bytes 32800 | tf_op jit(solution)/shard_map/ppermute | solution.py:245
  49.4 2.9 %collective-permute-start.7 = (bf16[32,256]{1,0:T(8,128)(2,1)S(1)}, bf16[32,256]{1,0:T(8,128)(2,1)S(1)}, u32[]{:S(2)}, u32[]{:S(2)}) collective-permute-start(bf16[32,256]{1,0:T(8,128)(2,1)S(1)} %multiply_convert_fusion.own_ref), channel_id=1, source_target_pairs={{0,17},{1,16},{2,19},{3,18},{16,1},{17,0},{18,3},{19,2},{4,21},{5,... | collective-permute-start | bytes 49160 | tf_op jit(solution)/shard_map/ppermute | solution.py:240
  52.3 1.2 %collective-permute-start.6 = (bf16[32,256]{1,0:T(8,128)(2,1)S(1)}, bf16[32,256]{1,0:T(8,128)(2,1)S(1)}, u32[]{:S(2)}, u32[]{:S(2)}) collective-permute-start(bf16[32,256]{1,0:T(8,128)(2,1)S(1)} %multiply_convert_fusion.own_ref), channel_id=1, source_target_pairs={{0,1},{1,0},{2,3},{3,2},{16,17},{17,16},{18,19},{19,18},{4,5},{5,4... | collective-permute-start | bytes 49160 | tf_op jit(solution)/shard_map/ppermute | solution.py:240
  53.5 0.2 unpack.1.parts_ref
  53.8 1.2 %collective-permute-done.6.far_ref = bf16[32,256]{1,0:T(8,128)(2,1)S(1)} collective-permute-done((bf16[32,256]{1,0:T(8,128)(2,1)S(1)}, bf16[32,256]{1,0:T(8,128)(2,1)S(1)}, u32[]{:S(2)}, u32[]{:S(2)}) %collective-permute-start.6) | collective-permute-done | bytes 16416 | tf_op jit(solution)/shard_map/ppermute | solution.py:240
  55.0 1.4 %refits_last.1 = (f32[32,256]{1,0:T(8,128)S(1)}, f32[32,256]{1,0:T(8,128)S(1)}, f32[2,128,256]{2,1,0:T(8,128)S(1)}, f32[2,128,128]{2,1,0:T(8,128)S(1)}, f32[2,8,128]{2,1,0:T(8,128)S(1)}) custom-call(bf16[2,3,256,256]{3,2,1,0:T(8,128)(2,1)S(1)} %unpack.1.parts_ref, bf16[32,256]{1,0:T(8,128)(2,1)S(1)} %multiply_convert_fusion.own_ref, ...), custom_call_target="tpu_custom_call" | custom-call | tf_op jit(solution)/shard_map/refits_last/pallas_call | solution.py:205
  56.3 1.2 %collective-permute-start.8 = (f32[32,256]{1,0:T(8,128)S(1)}, f32[32,256]{1,0:T(8,128)S(1)}, u32[]{:S(2)}, u32[]{:S(2)}) collective-permute-start(f32[32,256]{1,0:T(8,128)S(1)} %get-tuple-element.24), channel_id=1, source_target_pairs={{0,16},{1,17},{2,18},{3,19},{16,0},{17,1},{18,2},{19,3},{4,20},{5,... | collective-permute-start | bytes 98312 | tf_op jit(solution)/shard_map/ppermute | solution.py:240
  57.5 0.9 %collective-permute-done.8 = f32[32,256]{1,0:T(8,128)S(1)} collective-permute-done((f32[32,256]{1,0:T(8,128)S(1)}, f32[32,256]{1,0:T(8,128)S(1)}, u32[]{:S(2)}, u32[]{:S(2)}) %collective-permute-start.8) | collective-permute-done | bytes 32800 | tf_op jit(solution)/shard_map/ppermute | solution.py:240
  58.4 2.6 %collective-permute-start.11 = (f32[32,256]{1,0:T(8,128)S(1)}, f32[32,256]{1,0:T(8,128)S(1)}, u32[]{:S(2)}, u32[]{:S(2)}) collective-permute-start(f32[32,256]{1,0:T(8,128)S(1)} %add.14.own_ref), channel_id=1, source_target_pairs={{0,192},{32,224},{64,128},{96,160},{128,64},{160,96},{192,0},{224,... | collective-permute-start | bytes 98312 | tf_op jit(solution)/shard_map/ppermute | solution.py:245
  61.0 1.8 %collective-permute-start.10 = (f32[32,256]{1,0:T(8,128)S(1)}, f32[32,256]{1,0:T(8,128)S(1)}, u32[]{:S(2)}, u32[]{:S(2)}) collective-permute-start(f32[32,256]{1,0:T(8,128)S(1)} %add.14.own_ref), channel_id=1, source_target_pairs={{0,224},{32,192},{64,160},{96,128},{128,96},{160,64},{192,32},{224... | collective-permute-start | bytes 98312 | tf_op jit(solution)/shard_map/ppermute | solution.py:245
  62.8 0.3 collective-permute-start.9
  63.1 0.1 collective-permute-done.11.far_ref
  63.2 2.1 %collective-permute-done.10.next_ref = f32[32,256]{1,0:T(8,128)S(1)} collective-permute-done((f32[32,256]{1,0:T(8,128)S(1)}, f32[32,256]{1,0:T(8,128)S(1)}, u32[]{:S(2)}, u32[]{:S(2)}) %collective-permute-start.10) | collective-permute-done | bytes 32800 | tf_op jit(solution)/shard_map/ppermute | solution.py:245
  65.3 0.9 %collective-permute-done.9.near_ref = f32[32,256]{1,0:T(8,128)S(1)} collective-permute-done((f32[32,256]{1,0:T(8,128)S(1)}, f32[32,256]{1,0:T(8,128)S(1)}, u32[]{:S(2)}, u32[]{:S(2)}) %collective-permute-start.9) | collective-permute-done | bytes 32800 | tf_op jit(solution)/shard_map/ppermute | solution.py:245
  66.2 1.2 %collective-permute-start.12 = (f32[32,256]{1,0:T(8,128)S(1)}, f32[32,256]{1,0:T(8,128)S(1)}, u32[]{:S(2)}, u32[]{:S(2)}) collective-permute-start(f32[32,256]{1,0:T(8,128)S(1)} %four.3), channel_id=1, source_target_pairs={{0,64},{32,96},{64,0},{96,32},{128,192},{160,224},{192,128},{224,1... | collective-permute-start | bytes 98312 | tf_op jit(solution)/shard_map/ppermute | solution.py:245
  67.4 2.5 %collective-permute-done.12 = f32[32,256]{1,0:T(8,128)S(1)} collective-permute-done((f32[32,256]{1,0:T(8,128)S(1)}, f32[32,256]{1,0:T(8,128)S(1)}, u32[]{:S(2)}, u32[]{:S(2)}) %collective-permute-start.12) | collective-permute-done | bytes 32800 | tf_op jit(solution)/shard_map/ppermute | solution.py:245
  69.9 2.8 %collective-permute-start.15 = (f32[32,256]{1,0:T(8,128)S(1)}, f32[32,256]{1,0:T(8,128)S(1)}, u32[]{:S(2)}, u32[]{:S(2)}) collective-permute-start(f32[32,256]{1,0:T(8,128)S(1)} %add_multiply_fusion.own_ref), channel_id=1, source_target_pairs={{0,17},{1,16},{2,19},{3,18},{16,1},{17,0},{18,3},{19,2},{4,21},{5,... | collective-permute-start | bytes 98312 | tf_op jit(solution)/shard_map/ppermute | solution.py:240
  72.7 1.2 %collective-permute-start.14 = (f32[32,256]{1,0:T(8,128)S(1)}, f32[32,256]{1,0:T(8,128)S(1)}, u32[]{:S(2)}, u32[]{:S(2)}) collective-permute-start(f32[32,256]{1,0:T(8,128)S(1)} %add_multiply_fusion.own_ref), channel_id=1, source_target_pairs={{0,1},{1,0},{2,3},{3,2},{16,17},{17,16},{18,19},{19,18},{4,5},{5,4... | collective-permute-start | bytes 98312 | tf_op jit(solution)/shard_map/ppermute | solution.py:240
  73.9 1.0 %project.1 = f32[2,240,128]{2,1,0:T(8,128)} custom-call(f32[2,128,256]{2,1,0:T(8,128)S(1)} %get-tuple-element.28.before_ref, f32[2,128,128]{2,1,0:T(8,128)S(1)} %get-tuple-element.29.current_ref, f32[2,8,128]{2,1,0:T(8,128)S(1)} %get-tuple-element.30.scales_ref), custom_call_target="tpu_custom_call" | custom-call | tf_op jit(solution)/shard_map/project/pallas_call | solution.py:205
  75.0 0.9 %collective-permute-done.14.far_ref = f32[32,256]{1,0:T(8,128)S(1)} collective-permute-done((f32[32,256]{1,0:T(8,128)S(1)}, f32[32,256]{1,0:T(8,128)S(1)}, u32[]{:S(2)}, u32[]{:S(2)}) %collective-permute-start.14) | collective-permute-done | bytes 32800 | tf_op jit(solution)/shard_map/ppermute | solution.py:240
  75.9 0.8 whole.1
  (16 shorter events, 0.1 us)
Async XLA Ops:
  30.7 4.2 %collective-permute-start = (f32[32,256]{1,0:T(8,128)S(1)}, f32[32,256]{1,0:T(8,128)S(1)}, u32[]{:S(2)}, u32[]{:S(2)}) collective-permute-start(f32[32,256]{1,0:T(8,128)S(1)} %get-tuple-element.20), channel_id=1, source_target_pairs={{0,16},{1,17},{2,18},{3,19},{16,0},{17,1},{18,2},{19,3},{4,20},{5,... | collective-permute-start | bytes 98312 | tf_op jit(solution)/shard_map/ppermute | solution.py:240
  34.9 7.4 %collective-permute-start.3 = (f32[32,256]{1,0:T(8,128)S(1)}, f32[32,256]{1,0:T(8,128)S(1)}, u32[]{:S(2)}, u32[]{:S(2)}) collective-permute-start(f32[32,256]{1,0:T(8,128)S(1)} %add.12.own_ref), channel_id=1, source_target_pairs={{0,192},{32,224},{64,128},{96,160},{128,64},{160,96},{192,0},{224,... | collective-permute-start | bytes 98312 | tf_op jit(solution)/shard_map/ppermute | solution.py:245
  41.0 4.0 %collective-permute-start.2 = (f32[32,256]{1,0:T(8,128)S(1)}, f32[32,256]{1,0:T(8,128)S(1)}, u32[]{:S(2)}, u32[]{:S(2)}) collective-permute-start(f32[32,256]{1,0:T(8,128)S(1)} %add.12.own_ref), channel_id=1, source_target_pairs={{0,224},{32,192},{64,160},{96,128},{128,96},{160,64},{192,32},{224... | collective-permute-start | bytes 98312 | tf_op jit(solution)/shard_map/ppermute | solution.py:245
  41.0 4.0 %collective-permute-start.1 = (f32[32,256]{1,0:T(8,128)S(1)}, f32[32,256]{1,0:T(8,128)S(1)}, u32[]{:S(2)}, u32[]{:S(2)}) collective-permute-start(f32[32,256]{1,0:T(8,128)S(1)} %add.12.own_ref), channel_id=1, source_target_pairs={{0,32},{32,0},{64,96},{96,64},{128,160},{160,128},{192,224},{224,1... | collective-permute-start | bytes 98312 | tf_op jit(solution)/shard_map/ppermute | solution.py:245
  45.0 4.5 %collective-permute-start.4 = (f32[32,256]{1,0:T(8,128)S(1)}, f32[32,256]{1,0:T(8,128)S(1)}, u32[]{:S(2)}, u32[]{:S(2)}) collective-permute-start(f32[32,256]{1,0:T(8,128)S(1)} %four.2), channel_id=1, source_target_pairs={{0,64},{32,96},{64,0},{96,32},{128,192},{160,224},{192,128},{224,1... | collective-permute-start | bytes 98312 | tf_op jit(solution)/shard_map/ppermute | solution.py:245
  49.4 4.4 %collective-permute-start.7 = (bf16[32,256]{1,0:T(8,128)(2,1)S(1)}, bf16[32,256]{1,0:T(8,128)(2,1)S(1)}, u32[]{:S(2)}, u32[]{:S(2)}) collective-permute-start(bf16[32,256]{1,0:T(8,128)(2,1)S(1)} %multiply_convert_fusion.own_ref), channel_id=1, source_target_pairs={{0,17},{1,16},{2,19},{3,18},{16,1},{17,0},{18,3},{19,2},{4,21},{5,... | collective-permute-start | bytes 49160 | tf_op jit(solution)/shard_map/ppermute | solution.py:240
  52.3 2.6 %collective-permute-start.6 = (bf16[32,256]{1,0:T(8,128)(2,1)S(1)}, bf16[32,256]{1,0:T(8,128)(2,1)S(1)}, u32[]{:S(2)}, u32[]{:S(2)}) collective-permute-start(bf16[32,256]{1,0:T(8,128)(2,1)S(1)} %multiply_convert_fusion.own_ref), channel_id=1, source_target_pairs={{0,1},{1,0},{2,3},{3,2},{16,17},{17,16},{18,19},{19,18},{4,5},{5,4... | collective-permute-start | bytes 49160 | tf_op jit(solution)/shard_map/ppermute | solution.py:240
  53.5 1.4 %collective-permute-start.5 = (bf16[32,256]{1,0:T(8,128)(2,1)S(1)}, bf16[32,256]{1,0:T(8,128)(2,1)S(1)}, u32[]{:S(2)}, u32[]{:S(2)}) collective-permute-start(bf16[32,256]{1,0:T(8,128)(2,1)S(1)} %multiply_convert_fusion.own_ref), channel_id=1, source_target_pairs={{0,16},{1,17},{2,18},{3,19},{16,0},{17,1},{18,2},{19,3},{4,20},{5,... | collective-permute-start | bytes 49160 | tf_op jit(solution)/shard_map/ppermute | solution.py:240
  56.3 2.0 %collective-permute-start.8 = (f32[32,256]{1,0:T(8,128)S(1)}, f32[32,256]{1,0:T(8,128)S(1)}, u32[]{:S(2)}, u32[]{:S(2)}) collective-permute-start(f32[32,256]{1,0:T(8,128)S(1)} %get-tuple-element.24), channel_id=1, source_target_pairs={{0,16},{1,17},{2,18},{3,19},{16,0},{17,1},{18,2},{19,3},{4,20},{5,... | collective-permute-start | bytes 98312 | tf_op jit(solution)/shard_map/ppermute | solution.py:240
  58.4 4.9 %collective-permute-start.11 = (f32[32,256]{1,0:T(8,128)S(1)}, f32[32,256]{1,0:T(8,128)S(1)}, u32[]{:S(2)}, u32[]{:S(2)}) collective-permute-start(f32[32,256]{1,0:T(8,128)S(1)} %add.14.own_ref), channel_id=1, source_target_pairs={{0,192},{32,224},{64,128},{96,160},{128,64},{160,96},{192,0},{224,... | collective-permute-start | bytes 98312 | tf_op jit(solution)/shard_map/ppermute | solution.py:245
  61.0 4.3 %collective-permute-start.10 = (f32[32,256]{1,0:T(8,128)S(1)}, f32[32,256]{1,0:T(8,128)S(1)}, u32[]{:S(2)}, u32[]{:S(2)}) collective-permute-start(f32[32,256]{1,0:T(8,128)S(1)} %add.14.own_ref), channel_id=1, source_target_pairs={{0,224},{32,192},{64,160},{96,128},{128,96},{160,64},{192,32},{224... | collective-permute-start | bytes 98312 | tf_op jit(solution)/shard_map/ppermute | solution.py:245
  62.8 3.3 %collective-permute-start.9 = (f32[32,256]{1,0:T(8,128)S(1)}, f32[32,256]{1,0:T(8,128)S(1)}, u32[]{:S(2)}, u32[]{:S(2)}) collective-permute-start(f32[32,256]{1,0:T(8,128)S(1)} %add.14.own_ref), channel_id=1, source_target_pairs={{0,32},{32,0},{64,96},{96,64},{128,160},{160,128},{192,224},{224,1... | collective-permute-start | bytes 98312 | tf_op jit(solution)/shard_map/ppermute | solution.py:245
  66.2 3.8 %collective-permute-start.12 = (f32[32,256]{1,0:T(8,128)S(1)}, f32[32,256]{1,0:T(8,128)S(1)}, u32[]{:S(2)}, u32[]{:S(2)}) collective-permute-start(f32[32,256]{1,0:T(8,128)S(1)} %four.3), channel_id=1, source_target_pairs={{0,64},{32,96},{64,0},{96,32},{128,192},{160,224},{192,128},{224,1... | collective-permute-start | bytes 98312 | tf_op jit(solution)/shard_map/ppermute | solution.py:245
  69.9 5.0 %collective-permute-start.15 = (f32[32,256]{1,0:T(8,128)S(1)}, f32[32,256]{1,0:T(8,128)S(1)}, u32[]{:S(2)}, u32[]{:S(2)}) collective-permute-start(f32[32,256]{1,0:T(8,128)S(1)} %add_multiply_fusion.own_ref), channel_id=1, source_target_pairs={{0,17},{1,16},{2,19},{3,18},{16,1},{17,0},{18,3},{19,2},{4,21},{5,... | collective-permute-start | bytes 98312 | tf_op jit(solution)/shard_map/ppermute | solution.py:240
  72.7 3.1 %collective-permute-start.14 = (f32[32,256]{1,0:T(8,128)S(1)}, f32[32,256]{1,0:T(8,128)S(1)}, u32[]{:S(2)}, u32[]{:S(2)}) collective-permute-start(f32[32,256]{1,0:T(8,128)S(1)} %add_multiply_fusion.own_ref), channel_id=1, source_target_pairs={{0,1},{1,0},{2,3},{3,2},{16,17},{17,16},{18,19},{19,18},{4,5},{5,4... | collective-permute-start | bytes 98312 | tf_op jit(solution)/shard_map/ppermute | solution.py:240
  73.9 2.0 %collective-permute-start.13 = (f32[32,256]{1,0:T(8,128)S(1)}, f32[32,256]{1,0:T(8,128)S(1)}, u32[]{:S(2)}, u32[]{:S(2)}) collective-permute-start(f32[32,256]{1,0:T(8,128)S(1)} %add_multiply_fusion.own_ref), channel_id=1, source_target_pairs={{0,16},{1,17},{2,18},{3,19},{16,0},{17,1},{18,2},{19,3},{4,20},{5,... | collective-permute-start | bytes 98312 | tf_op jit(solution)/shard_map/ppermute | solution.py:240

commit v9 on v8

--- a/solution.py
+++ b/solution.py
@@ -176,9 +176,9 @@
             parts_ref[subject, part] = half
 
 
-def last_kernel(parts_ref, own_ref, near_ref, far_ref, both_ref, *refs):
+def last_kernel(parts_ref, own_ref, near_ref, *refs):
     *refs, scales_ref, shared_ref = refs
-    for piece, piece_ref in enumerate((own_ref, near_ref, far_ref, both_ref)):
+    for piece, piece_ref in enumerate((own_ref, near_ref)):
         shared_ref[block(piece, piece_ref.shape[0]), :] = piece_ref[...]
     grams = [[parts_ref[subject, part] for part in range(3)] for subject in range(2)]
     scales = finish(grams, shared_ref[...], False, *refs)
@@ -195,10 +195,9 @@
 
 
 def block(piece, width):
-    core, side = lax.axis_index("core"), lax.axis_index("x") % 2
-    core = 1 - core if piece % 2 else core
-    side = 1 - side if piece // 2 else side
-    return pl.ds(pl.multiple_of((2 * side + core) * width, width), width)
+    core = lax.axis_index("core")
+    core = 1 - core if piece else core
+    return pl.ds(pl.multiple_of(core * width, width), width)
 
 
 def call(kernel, name, out, args, scratch=()):
@@ -212,8 +211,8 @@
     )(*(in_vmem(x) for x in args))
 
 
-def whole_kernel(own_ref, near_ref, far_ref, both_ref, out_ref, whole_ref):
-    for piece, piece_ref in enumerate((own_ref, near_ref, far_ref, both_ref)):
+def whole_kernel(own_ref, near_ref, out_ref, whole_ref):
+    for piece, piece_ref in enumerate((own_ref, near_ref)):
         whole_ref[block(piece, piece_ref.shape[0]), :] = piece_ref[...]
     out_ref[...] = whole_ref[...].T[0 : out_ref.shape[0], :]
 
@@ -230,14 +229,8 @@
     return jnp.broadcast_to(shard[None], (peers, *shard.shape))
 
 
-def swapped(x, core, across):
-    cores, chips = lax.axis_size("core"), lax.axis_size("x")
-    pairs = []
-    for c in range(cores):
-        for i in range(chips):
-            to = (c ^ core) * chips + (i ^ across)
-            pairs.append((c * chips + i, to))
-    return lax.ppermute(x, ("core", "x"), pairs)
+def swapped(x):
+    return lax.ppermute(x, "core", [(0, 1), (1, 0)])
 
 
 def along(x, mask):
@@ -250,14 +243,14 @@
 
 
 def all_summed(keep, give, dtype, scale, held):
-    total = keep + swapped(give, 1, 0)
+    total = keep + swapped(give)
     (total,) = call(
         four_kernel, "four", [pltpu.VMEM(keep.shape, jnp.float32)],
         (total, along(total, 1), along(total, 7), along(total, 6)),
     )
     total = ((total + along(total, 2)) * scale).astype(dtype)
     total, held = lax.optimization_barrier((total, held))
-    return (total, swapped(total, 1, 0), swapped(total, 0, 1), swapped(total, 1, 1)), held
+    return (total, swapped(total)), held
 
 
 def local(data, shared_start):
@@ -269,7 +262,7 @@
     packed, shared = packed_grams(data, shared_start.T, size)
     share = jnp.sum(exchanged(packed.reshape(peers, size // peers, size), ("y", "x")), axis=0)
     packed = exchanged(to_everyone(share, peers), ("y", "x")).reshape(size, size)
-    blocks = [pltpu.VMEM((features // 4, size), jnp.float32)] * 2
+    blocks = [pltpu.VMEM((features // 2, size), jnp.float32)] * 2
     crosses = pltpu.VMEM((2, features, size), jnp.float32)
     squares = pltpu.VMEM((2, features, features), jnp.float32)
     keep, give = call(

time: 76.8 us -> 75.6 us (0.984)
  starting transfers between devices: 29 us -> 26.1 us
  waiting for transfers between devices: 13.4 us -> 14.9 us
    ppermute x8 -> x4, starting transfers between devices: 12.6 us -> 9.41 us  [swapped(): return lax.ppermute(x, 'core', [(0, 1), (1, 0)])]
    ppermute x8, waiting for transfers between devices: 9.56 us -> 12.4 us  [along(): return lax.ppermute(x, 'z', [(chip, chip ^ mask) for chip in range(chips)])]
    ppermute x8 -> x4, waiting for transfers between devices: 3.83 us -> 2.43 us  [swapped(): return lax.ppermute(x, 'core', [(0, 1), (1, 0)])]
  transfers between devices with their start and end apart: 16 -> 12, of which waited for: 11 -> 10; matrix products, arithmetic and copies ran while one was open for 0% -> 0% of each run, Pallas kernels for 2% -> 2%
where the time goes in v9:
time: 75.6 us; the launch traced here: 75.4 us
  starting transfers between devices  26.1 us (35%)
  blocking collectives  25.4 us (34%)
  waiting for transfers between devices  14.9 us (20%)
  Pallas kernels  8.3 us (11%)
    all_to_all x2, blocking collectives, exchanged(): return lax.all_to_all(pieces, axis, 0, 0, tiled=True)  25.4 us
    ppermute x8, starting transfers between devices, along(): return lax.ppermute(x, 'z', [(chip, chip ^ mask) for chip in range(chips)])  16.7 us
    ppermute x8, waiting for transfers between devices, along(): return lax.ppermute(x, 'z', [(chip, chip ^ mask) for chip in range(chips)])  12.4 us
    ppermute x4, starting transfers between devices, swapped(): return lax.ppermute(x, 'core', [(0, 1), (1, 0)])  9.41 us
    pallas_call x7, Pallas kernels, call(): pl.pallas_call(kernel, in_specs=[VMEM] * len(args), out_specs=[VMEM] * le...  5.21 us
    pallas_call x1, Pallas kernels, packed_grams(): pl.pallas_call(gram_kernel, grid=(2,), in_specs=[pl.BlockSpec((subjects,...  3.08 us
    ppermute x4, waiting for transfers between devices, swapped(): return lax.ppermute(x, 'core', [(0, 1), (1, 0)])  2.43 us
  transfers between devices with their start and end apart: 12, of which 10 were waited for; matrix products, arithmetic and copies ran while one was open for 0% of the time, Pallas kernels for 2%

profile of v9, /device:TPU:1, one launch (start us, length us, event | category | flops | bytes accessed | tf_op | source)
XLA Modules:
  0.0 75.4 jit_solution(2165830272822081929)
XLA Ops:
  0.6 3.1 %grams.1 = (f32[256,256]{1,0:T(8,128)S(1)}, bf16[128,256]{1,0:T(8,128)(2,1)S(1)}) custom-call(bf16[2,240,4096]{2,1,0:T(8,128)(2,1)} %data_ref.1, bf16[240,128]{1,0:T(8,128)(2,1)} %bitcast.10), custom_call_target="tpu_custom_call" | custom-call | tf_op jit(solution)/shard_map/grams/pallas_call | solution.py:53
  3.7 14.9 %all_to_all.10 = f32[16,16,256]{2,1,0:T(8,128)S(1)} all-to-all(f32[16,16,256]{2,1,0:T(8,128)S(1)} %bitcast.7), channel_id=1, replica_groups=mesh['z'=8,'core'=2,'y'=4,'x'=4] {'y','x'}, dimensions={0} | all-to-all | bytes 524288 | tf_op jit(solution)/shard_map/all_to_all | solution.py:225
  18.7 10.5 %all_to_all.11 = f32[16,16,256]{2,1,0:T(8,128)S(1)} all-to-all(f32[16,16,256]{2,1,0:T(8,128)S(1)} %broadcast_in_dim.2), channel_id=1, replica_groups=mesh['z'=8,'core'=2,'y'=4,'x'=4] {'y','x'}, dimensions={0} | all-to-all | bytes 524288 | tf_op jit(solution)/shard_map/all_to_all | solution.py:225
  29.1 1.7 %refits.1 = (f32[64,256]{1,0:T(8,128)S(1)}, f32[64,256]{1,0:T(8,128)S(1)}) custom-call(f32[256,256]{1,0:T(8,128)S(1)} %bitcast.5, bf16[128,256]{1,0:T(8,128)(2,1)S(1)} %get-tuple-element.18.shared_ref), custom_call_target="tpu_custom_call" | custom-call | tf_op jit(solution)/shard_map/refits/pallas_call | solution.py:204
  30.9 3.3 %collective-permute-start = (f32[64,256]{1,0:T(8,128)S(1)}, f32[64,256]{1,0:T(8,128)S(1)}, u32[]{:S(2)}, u32[]{:S(2)}) collective-permute-start(f32[64,256]{1,0:T(8,128)S(1)} %get-tuple-element.20), channel_id=1, source_target_pairs={{0,16},{16,0},{1,17},{17,1},{2,18},{18,2},{3,19},{19,3},{4,20},{20... | collective-permute-start | bytes 196616 | tf_op jit(solution)/shard_map/ppermute | solution.py:233
  34.2 0.9 %collective-permute-done = f32[64,256]{1,0:T(8,128)S(1)} collective-permute-done((f32[64,256]{1,0:T(8,128)S(1)}, f32[64,256]{1,0:T(8,128)S(1)}, u32[]{:S(2)}, u32[]{:S(2)}) %collective-permute-start) | collective-permute-done | bytes 65568 | tf_op jit(solution)/shard_map/ppermute | solution.py:233
  35.1 6.1 %collective-permute-start.3 = (f32[64,256]{1,0:T(8,128)S(1)}, f32[64,256]{1,0:T(8,128)S(1)}, u32[]{:S(2)}, u32[]{:S(2)}) collective-permute-start(f32[64,256]{1,0:T(8,128)S(1)} %add.12.own_ref), channel_id=1, source_target_pairs={{0,192},{32,224},{64,128},{96,160},{128,64},{160,96},{192,0},{224,... | collective-permute-start | bytes 196616 | tf_op jit(solution)/shard_map/ppermute | solution.py:238
  41.2 0.0 collective-permute-start.2
  41.2 1.3 %collective-permute-start.1 = (f32[64,256]{1,0:T(8,128)S(1)}, f32[64,256]{1,0:T(8,128)S(1)}, u32[]{:S(2)}, u32[]{:S(2)}) collective-permute-start(f32[64,256]{1,0:T(8,128)S(1)} %add.12.own_ref), channel_id=1, source_target_pairs={{0,32},{32,0},{64,96},{96,64},{128,160},{160,128},{192,224},{224,1... | collective-permute-start | bytes 196616 | tf_op jit(solution)/shard_map/ppermute | solution.py:238
  42.5 0.8 %collective-permute-done.3.far_ref = f32[64,256]{1,0:T(8,128)S(1)} collective-permute-done((f32[64,256]{1,0:T(8,128)S(1)}, f32[64,256]{1,0:T(8,128)S(1)}, u32[]{:S(2)}, u32[]{:S(2)}) %collective-permute-start.3) | collective-permute-done | bytes 65568 | tf_op jit(solution)/shard_map/ppermute | solution.py:238
  43.3 3.3 %collective-permute-done.2.next_ref = f32[64,256]{1,0:T(8,128)S(1)} collective-permute-done((f32[64,256]{1,0:T(8,128)S(1)}, f32[64,256]{1,0:T(8,128)S(1)}, u32[]{:S(2)}, u32[]{:S(2)}) %collective-permute-start.2) | collective-permute-done | bytes 65568 | tf_op jit(solution)/shard_map/ppermute | solution.py:238
  46.6 0.0 collective-permute-done.1.near_ref
  46.7 2.1 %collective-permute-start.4 = (f32[64,256]{1,0:T(8,128)S(1)}, f32[64,256]{1,0:T(8,128)S(1)}, u32[]{:S(2)}, u32[]{:S(2)}) collective-permute-start(f32[64,256]{1,0:T(8,128)S(1)} %four.2), channel_id=1, source_target_pairs={{0,64},{32,96},{64,0},{96,32},{128,192},{160,224},{192,128},{224,1... | collective-permute-start | bytes 196616 | tf_op jit(solution)/shard_map/ppermute | solution.py:238
  48.7 2.0 %collective-permute-done.4 = f32[64,256]{1,0:T(8,128)S(1)} collective-permute-done((f32[64,256]{1,0:T(8,128)S(1)}, f32[64,256]{1,0:T(8,128)S(1)}, u32[]{:S(2)}, u32[]{:S(2)}) %collective-permute-start.4) | collective-permute-done | bytes 65568 | tf_op jit(solution)/shard_map/ppermute | solution.py:238
  50.8 2.7 %collective-permute-start.5 = (bf16[64,256]{1,0:T(8,128)(2,1)S(1)}, bf16[64,256]{1,0:T(8,128)(2,1)S(1)}, u32[]{:S(2)}, u32[]{:S(2)}) collective-permute-start(bf16[64,256]{1,0:T(8,128)(2,1)S(1)} %multiply_convert_fusion.own_ref), channel_id=1, source_target_pairs={{0,16},{16,0},{1,17},{17,1},{2,18},{18,2},{3,19},{19,3},{4,20},{20... | collective-permute-start | bytes 98312 | tf_op jit(solution)/shard_map/ppermute | solution.py:233
  53.5 0.2 unpack.1.parts_ref
  53.7 0.6 collective-permute-done.5.near_ref
  54.4 1.5 %refits_last.1 = (f32[64,256]{1,0:T(8,128)S(1)}, f32[64,256]{1,0:T(8,128)S(1)}, f32[2,128,256]{2,1,0:T(8,128)S(1)}, f32[2,128,128]{2,1,0:T(8,128)S(1)}, f32[2,8,128]{2,1,0:T(8,128)S(1)}) custom-call(bf16[2,3,256,256]{3,2,1,0:T(8,128)(2,1)S(1)} %unpack.1.parts_ref, bf16[64,256]{1,0:T(8,128)(2,1)S(1)} %multiply_convert_fusion.own_ref, ...), custom_call_target="tpu_custom_call" | custom-call | tf_op jit(solution)/shard_map/refits_last/pallas_call | solution.py:204
  55.8 0.4 collective-permute-start.6
  56.3 0.9 %collective-permute-done.6 = f32[64,256]{1,0:T(8,128)S(1)} collective-permute-done((f32[64,256]{1,0:T(8,128)S(1)}, f32[64,256]{1,0:T(8,128)S(1)}, u32[]{:S(2)}, u32[]{:S(2)}) %collective-permute-start.6) | collective-permute-done | bytes 65568 | tf_op jit(solution)/shard_map/ppermute | solution.py:233
  57.2 3.7 %collective-permute-start.9 = (f32[64,256]{1,0:T(8,128)S(1)}, f32[64,256]{1,0:T(8,128)S(1)}, u32[]{:S(2)}, u32[]{:S(2)}) collective-permute-start(f32[64,256]{1,0:T(8,128)S(1)} %add.14.own_ref), channel_id=1, source_target_pairs={{0,192},{32,224},{64,128},{96,160},{128,64},{160,96},{192,0},{224,... | collective-permute-start | bytes 196616 | tf_op jit(solution)/shard_map/ppermute | solution.py:238
  60.8 0.8 %collective-permute-start.8 = (f32[64,256]{1,0:T(8,128)S(1)}, f32[64,256]{1,0:T(8,128)S(1)}, u32[]{:S(2)}, u32[]{:S(2)}) collective-permute-start(f32[64,256]{1,0:T(8,128)S(1)} %add.14.own_ref), channel_id=1, source_target_pairs={{0,224},{32,192},{64,160},{96,128},{128,96},{160,64},{192,32},{224... | collective-permute-start | bytes 196616 | tf_op jit(solution)/shard_map/ppermute | solution.py:238
  61.7 0.5 collective-permute-start.7
  62.2 0.3 collective-permute-done.9.far_ref
  62.5 3.9 %collective-permute-done.8.next_ref = f32[64,256]{1,0:T(8,128)S(1)} collective-permute-done((f32[64,256]{1,0:T(8,128)S(1)}, f32[64,256]{1,0:T(8,128)S(1)}, u32[]{:S(2)}, u32[]{:S(2)}) %collective-permute-start.8) | collective-permute-done | bytes 65568 | tf_op jit(solution)/shard_map/ppermute | solution.py:238
  66.4 0.2 collective-permute-done.7.near_ref
  66.6 2.3 %collective-permute-start.10 = (f32[64,256]{1,0:T(8,128)S(1)}, f32[64,256]{1,0:T(8,128)S(1)}, u32[]{:S(2)}, u32[]{:S(2)}) collective-permute-start(f32[64,256]{1,0:T(8,128)S(1)} %four.3), channel_id=1, source_target_pairs={{0,64},{32,96},{64,0},{96,32},{128,192},{160,224},{192,128},{224,1... | collective-permute-start | bytes 196616 | tf_op jit(solution)/shard_map/ppermute | solution.py:238
  68.8 1.8 %collective-permute-done.10 = f32[64,256]{1,0:T(8,128)S(1)} collective-permute-done((f32[64,256]{1,0:T(8,128)S(1)}, f32[64,256]{1,0:T(8,128)S(1)}, u32[]{:S(2)}, u32[]{:S(2)}) %collective-permute-start.10) | collective-permute-done | bytes 65568 | tf_op jit(solution)/shard_map/ppermute | solution.py:238
  70.7 2.9 %collective-permute-start.11 = (f32[64,256]{1,0:T(8,128)S(1)}, f32[64,256]{1,0:T(8,128)S(1)}, u32[]{:S(2)}, u32[]{:S(2)}) collective-permute-start(f32[64,256]{1,0:T(8,128)S(1)} %add_multiply_fusion.own_ref), channel_id=1, source_target_pairs={{0,16},{16,0},{1,17},{17,1},{2,18},{18,2},{3,19},{19,3},{4,20},{20... | collective-permute-start | bytes 196616 | tf_op jit(solution)/shard_map/ppermute | solution.py:233
  73.6 1.0 %project.1 = f32[2,240,128]{2,1,0:T(8,128)} custom-call(f32[2,128,256]{2,1,0:T(8,128)S(1)} %get-tuple-element.28.before_ref, f32[2,128,128]{2,1,0:T(8,128)S(1)} %get-tuple-element.29.current_ref, f32[2,8,128]{2,1,0:T(8,128)S(1)} %get-tuple-element.30.scales_ref), custom_call_target="tpu_custom_call" | custom-call | tf_op jit(solution)/shard_map/project/pallas_call | solution.py:204
  74.6 0.0 collective-permute-done.11.near_ref
  74.6 0.8 %whole.1 = f32[240,128]{1,0:T(8,128)} custom-call(f32[64,256]{1,0:T(8,128)S(1)} %add_multiply_fusion.own_ref, f32[64,256]{1,0:T(8,128)S(1)} %collective-permute-done.11.near_ref), custom_call_target="tpu_custom_call" | custom-call | tf_op jit(solution)/shard_map/whole/pallas_call | solution.py:204
  (8 shorter events, 0.1 us)
Async XLA Ops:
  30.9 4.2 %collective-permute-start = (f32[64,256]{1,0:T(8,128)S(1)}, f32[64,256]{1,0:T(8,128)S(1)}, u32[]{:S(2)}, u32[]{:S(2)}) collective-permute-start(f32[64,256]{1,0:T(8,128)S(1)} %get-tuple-element.20), channel_id=1, source_target_pairs={{0,16},{16,0},{1,17},{17,1},{2,18},{18,2},{3,19},{19,3},{4,20},{20... | collective-permute-start | bytes 196616 | tf_op jit(solution)/shard_map/ppermute | solution.py:233
  35.1 8.2 %collective-permute-start.3 = (f32[64,256]{1,0:T(8,128)S(1)}, f32[64,256]{1,0:T(8,128)S(1)}, u32[]{:S(2)}, u32[]{:S(2)}) collective-permute-start(f32[64,256]{1,0:T(8,128)S(1)} %add.12.own_ref), channel_id=1, source_target_pairs={{0,192},{32,224},{64,128},{96,160},{128,64},{160,96},{192,0},{224,... | collective-permute-start | bytes 196616 | tf_op jit(solution)/shard_map/ppermute | solution.py:238
  41.2 5.4 %collective-permute-start.2 = (f32[64,256]{1,0:T(8,128)S(1)}, f32[64,256]{1,0:T(8,128)S(1)}, u32[]{:S(2)}, u32[]{:S(2)}) collective-permute-start(f32[64,256]{1,0:T(8,128)S(1)} %add.12.own_ref), channel_id=1, source_target_pairs={{0,224},{32,192},{64,160},{96,128},{128,96},{160,64},{192,32},{224... | collective-permute-start | bytes 196616 | tf_op jit(solution)/shard_map/ppermute | solution.py:238
  41.2 5.4 %collective-permute-start.1 = (f32[64,256]{1,0:T(8,128)S(1)}, f32[64,256]{1,0:T(8,128)S(1)}, u32[]{:S(2)}, u32[]{:S(2)}) collective-permute-start(f32[64,256]{1,0:T(8,128)S(1)} %add.12.own_ref), channel_id=1, source_target_pairs={{0,32},{32,0},{64,96},{96,64},{128,160},{160,128},{192,224},{224,1... | collective-permute-start | bytes 196616 | tf_op jit(solution)/shard_map/ppermute | solution.py:238
  46.7 4.1 %collective-permute-start.4 = (f32[64,256]{1,0:T(8,128)S(1)}, f32[64,256]{1,0:T(8,128)S(1)}, u32[]{:S(2)}, u32[]{:S(2)}) collective-permute-start(f32[64,256]{1,0:T(8,128)S(1)} %four.2), channel_id=1, source_target_pairs={{0,64},{32,96},{64,0},{96,32},{128,192},{160,224},{192,128},{224,1... | collective-permute-start | bytes 196616 | tf_op jit(solution)/shard_map/ppermute | solution.py:238
  50.8 3.6 %collective-permute-start.5 = (bf16[64,256]{1,0:T(8,128)(2,1)S(1)}, bf16[64,256]{1,0:T(8,128)(2,1)S(1)}, u32[]{:S(2)}, u32[]{:S(2)}) collective-permute-start(bf16[64,256]{1,0:T(8,128)(2,1)S(1)} %multiply_convert_fusion.own_ref), channel_id=1, source_target_pairs={{0,16},{16,0},{1,17},{17,1},{2,18},{18,2},{3,19},{19,3},{4,20},{20... | collective-permute-start | bytes 98312 | tf_op jit(solution)/shard_map/ppermute | solution.py:233
  55.8 1.3 %collective-permute-start.6 = (f32[64,256]{1,0:T(8,128)S(1)}, f32[64,256]{1,0:T(8,128)S(1)}, u32[]{:S(2)}, u32[]{:S(2)}) collective-permute-start(f32[64,256]{1,0:T(8,128)S(1)} %get-tuple-element.24), channel_id=1, source_target_pairs={{0,16},{16,0},{1,17},{17,1},{2,18},{18,2},{3,19},{19,3},{4,20},{20... | collective-permute-start | bytes 196616 | tf_op jit(solution)/shard_map/ppermute | solution.py:233
  57.2 5.3 %collective-permute-start.9 = (f32[64,256]{1,0:T(8,128)S(1)}, f32[64,256]{1,0:T(8,128)S(1)}, u32[]{:S(2)}, u32[]{:S(2)}) collective-permute-start(f32[64,256]{1,0:T(8,128)S(1)} %add.14.own_ref), channel_id=1, source_target_pairs={{0,192},{32,224},{64,128},{96,160},{128,64},{160,96},{192,0},{224,... | collective-permute-start | bytes 196616 | tf_op jit(solution)/shard_map/ppermute | solution.py:238
  60.8 5.6 %collective-permute-start.8 = (f32[64,256]{1,0:T(8,128)S(1)}, f32[64,256]{1,0:T(8,128)S(1)}, u32[]{:S(2)}, u32[]{:S(2)}) collective-permute-start(f32[64,256]{1,0:T(8,128)S(1)} %add.14.own_ref), channel_id=1, source_target_pairs={{0,224},{32,192},{64,160},{96,128},{128,96},{160,64},{192,32},{224... | collective-permute-start | bytes 196616 | tf_op jit(solution)/shard_map/ppermute | solution.py:238
  61.7 4.9 %collective-permute-start.7 = (f32[64,256]{1,0:T(8,128)S(1)}, f32[64,256]{1,0:T(8,128)S(1)}, u32[]{:S(2)}, u32[]{:S(2)}) collective-permute-start(f32[64,256]{1,0:T(8,128)S(1)} %add.14.own_ref), channel_id=1, source_target_pairs={{0,32},{32,0},{64,96},{96,64},{128,160},{160,128},{192,224},{224,1... | collective-permute-start | bytes 196616 | tf_op jit(solution)/shard_map/ppermute | solution.py:238
  66.6 4.1 %collective-permute-start.10 = (f32[64,256]{1,0:T(8,128)S(1)}, f32[64,256]{1,0:T(8,128)S(1)}, u32[]{:S(2)}, u32[]{:S(2)}) collective-permute-start(f32[64,256]{1,0:T(8,128)S(1)} %four.3), channel_id=1, source_target_pairs={{0,64},{32,96},{64,0},{96,32},{128,192},{160,224},{192,128},{224,1... | collective-permute-start | bytes 196616 | tf_op jit(solution)/shard_map/ppermute | solution.py:238
  70.7 4.0 %collective-permute-start.11 = (f32[64,256]{1,0:T(8,128)S(1)}, f32[64,256]{1,0:T(8,128)S(1)}, u32[]{:S(2)}, u32[]{:S(2)}) collective-permute-start(f32[64,256]{1,0:T(8,128)S(1)} %add_multiply_fusion.own_ref), channel_id=1, source_target_pairs={{0,16},{16,0},{1,17},{17,1},{2,18},{18,2},{3,19},{19,3},{4,20},{20... | collective-permute-start | bytes 196616 | tf_op jit(solution)/shard_map/ppermute | solution.py:233

commit v10 on v9

--- a/solution.py
+++ b/solution.py
@@ -238,7 +238,7 @@
     return lax.ppermute(x, "z", [(chip, chip ^ mask) for chip in range(chips)])
 
 
-def four_kernel(own_ref, near_ref, next_ref, far_ref, out_ref):
+def four_kernel(own_ref, near_ref, far_ref, next_ref, out_ref):
     out_ref[...] = (own_ref[...] + near_ref[...]) + (far_ref[...] + next_ref[...])
 
 
@@ -246,7 +246,7 @@
     total = keep + swapped(give)
     (total,) = call(
         four_kernel, "four", [pltpu.VMEM(keep.shape, jnp.float32)],
-        (total, along(total, 1), along(total, 7), along(total, 6)),
+        (total, along(total, 1), along(total, 6), along(total, 7)),
     )
     total = ((total + along(total, 2)) * scale).astype(dtype)
     total, held = lax.optimization_barrier((total, held))

time: 75.6 us -> 76.6 us (1.013)
  starting transfers between devices: 26.1 us -> 27.5 us
    ppermute x8, starting transfers between devices: 16.7 us -> 17.5 us  [along(): return lax.ppermute(x, 'z', [(chip, chip ^ mask) for chip in range(chips)])]
  transfers between devices with their start and end apart: 12 -> 12, of which waited for: 10 -> 11; matrix products, arithmetic and copies ran while one was open for 0% -> 0% of each run, Pallas kernels for 2% -> 2%
where the time goes in v10:
time: 76.6 us; the launch traced here: 76.4 us
  starting transfers between devices  27.5 us (36%)
  blocking collectives  25.4 us (33%)
  waiting for transfers between devices  14.5 us (19%)
  Pallas kernels  8.3 us (11%)
    all_to_all x2, blocking collectives, exchanged(): return lax.all_to_all(pieces, axis, 0, 0, tiled=True)  25.4 us
    ppermute x8, starting transfers between devices, along(): return lax.ppermute(x, 'z', [(chip, chip ^ mask) for chip in range(chips)])  17.5 us
    ppermute x8, waiting for transfers between devices, along(): return lax.ppermute(x, 'z', [(chip, chip ^ mask) for chip in range(chips)])  12 us
    ppermute x4, starting transfers between devices, swapped(): return lax.ppermute(x, 'core', [(0, 1), (1, 0)])  10 us
    pallas_call x7, Pallas kernels, call(): pl.pallas_call(kernel, in_specs=[VMEM] * len(args), out_specs=[VMEM] * le...  5.21 us
    pallas_call x1, Pallas kernels, packed_grams(): pl.pallas_call(gram_kernel, grid=(2,), in_specs=[pl.BlockSpec((subjects,...  3.08 us
    ppermute x4, waiting for transfers between devices, swapped(): return lax.ppermute(x, 'core', [(0, 1), (1, 0)])  2.43 us
  transfers between devices with their start and end apart: 12, of which 11 were waited for; matrix products, arithmetic and copies ran while one was open for 0% of the time, Pallas kernels for 2%

profile of v10, /device:TPU:1, one launch (start us, length us, event | category | flops | bytes accessed | tf_op | source)
XLA Modules:
  0.0 76.4 jit_solution(5754946036274414860)
XLA Ops:
  0.6 3.1 %grams.1 = (f32[256,256]{1,0:T(8,128)S(1)}, bf16[128,256]{1,0:T(8,128)(2,1)S(1)}) custom-call(bf16[2,240,4096]{2,1,0:T(8,128)(2,1)} %data_ref.1, bf16[240,128]{1,0:T(8,128)(2,1)} %bitcast.10), custom_call_target="tpu_custom_call" | custom-call | tf_op jit(solution)/shard_map/grams/pallas_call | solution.py:53
  3.7 14.9 %all_to_all.10 = f32[16,16,256]{2,1,0:T(8,128)S(1)} all-to-all(f32[16,16,256]{2,1,0:T(8,128)S(1)} %bitcast.7), channel_id=1, replica_groups=mesh['z'=8,'core'=2,'y'=4,'x'=4] {'y','x'}, dimensions={0} | all-to-all | bytes 524288 | tf_op jit(solution)/shard_map/all_to_all | solution.py:225
  18.7 10.5 %all_to_all.11 = f32[16,16,256]{2,1,0:T(8,128)S(1)} all-to-all(f32[16,16,256]{2,1,0:T(8,128)S(1)} %broadcast_in_dim.2), channel_id=1, replica_groups=mesh['z'=8,'core'=2,'y'=4,'x'=4] {'y','x'}, dimensions={0} | all-to-all | bytes 524288 | tf_op jit(solution)/shard_map/all_to_all | solution.py:225
  29.1 1.7 %refits.1 = (f32[64,256]{1,0:T(8,128)S(1)}, f32[64,256]{1,0:T(8,128)S(1)}) custom-call(f32[256,256]{1,0:T(8,128)S(1)} %bitcast.5, bf16[128,256]{1,0:T(8,128)(2,1)S(1)} %get-tuple-element.18.shared_ref), custom_call_target="tpu_custom_call" | custom-call | tf_op jit(solution)/shard_map/refits/pallas_call | solution.py:204
  30.9 3.3 %collective-permute-start = (f32[64,256]{1,0:T(8,128)S(1)}, f32[64,256]{1,0:T(8,128)S(1)}, u32[]{:S(2)}, u32[]{:S(2)}) collective-permute-start(f32[64,256]{1,0:T(8,128)S(1)} %get-tuple-element.20), channel_id=1, source_target_pairs={{0,16},{16,0},{1,17},{17,1},{2,18},{18,2},{3,19},{19,3},{4,20},{20... | collective-permute-start | bytes 196616 | tf_op jit(solution)/shard_map/ppermute | solution.py:233
  34.2 0.9 %collective-permute-done = f32[64,256]{1,0:T(8,128)S(1)} collective-permute-done((f32[64,256]{1,0:T(8,128)S(1)}, f32[64,256]{1,0:T(8,128)S(1)}, u32[]{:S(2)}, u32[]{:S(2)}) %collective-permute-start) | collective-permute-done | bytes 65568 | tf_op jit(solution)/shard_map/ppermute | solution.py:233
  35.1 5.7 %collective-permute-start.3 = (f32[64,256]{1,0:T(8,128)S(1)}, f32[64,256]{1,0:T(8,128)S(1)}, u32[]{:S(2)}, u32[]{:S(2)}) collective-permute-start(f32[64,256]{1,0:T(8,128)S(1)} %add.12.own_ref), channel_id=1, source_target_pairs={{0,224},{32,192},{64,160},{96,128},{128,96},{160,64},{192,32},{224... | collective-permute-start | bytes 196616 | tf_op jit(solution)/shard_map/ppermute | solution.py:238
  40.8 0.5 collective-permute-start.2
  41.3 1.1 %collective-permute-start.1 = (f32[64,256]{1,0:T(8,128)S(1)}, f32[64,256]{1,0:T(8,128)S(1)}, u32[]{:S(2)}, u32[]{:S(2)}) collective-permute-start(f32[64,256]{1,0:T(8,128)S(1)} %add.12.own_ref), channel_id=1, source_target_pairs={{0,32},{32,0},{64,96},{96,64},{128,160},{160,128},{192,224},{224,1... | collective-permute-start | bytes 196616 | tf_op jit(solution)/shard_map/ppermute | solution.py:238
  42.4 1.9 %collective-permute-done.3.next_ref = f32[64,256]{1,0:T(8,128)S(1)} collective-permute-done((f32[64,256]{1,0:T(8,128)S(1)}, f32[64,256]{1,0:T(8,128)S(1)}, u32[]{:S(2)}, u32[]{:S(2)}) %collective-permute-start.3) | collective-permute-done | bytes 65568 | tf_op jit(solution)/shard_map/ppermute | solution.py:238
  44.3 1.7 %collective-permute-done.2.far_ref = f32[64,256]{1,0:T(8,128)S(1)} collective-permute-done((f32[64,256]{1,0:T(8,128)S(1)}, f32[64,256]{1,0:T(8,128)S(1)}, u32[]{:S(2)}, u32[]{:S(2)}) %collective-permute-start.2) | collective-permute-done | bytes 65568 | tf_op jit(solution)/shard_map/ppermute | solution.py:238
  46.0 1.1 %collective-permute-done.1.near_ref = f32[64,256]{1,0:T(8,128)S(1)} collective-permute-done((f32[64,256]{1,0:T(8,128)S(1)}, f32[64,256]{1,0:T(8,128)S(1)}, u32[]{:S(2)}, u32[]{:S(2)}) %collective-permute-start.1) | collective-permute-done | bytes 65568 | tf_op jit(solution)/shard_map/ppermute | solution.py:238
  47.1 2.6 %collective-permute-start.4 = (f32[64,256]{1,0:T(8,128)S(1)}, f32[64,256]{1,0:T(8,128)S(1)}, u32[]{:S(2)}, u32[]{:S(2)}) collective-permute-start(f32[64,256]{1,0:T(8,128)S(1)} %four.2), channel_id=1, source_target_pairs={{0,64},{32,96},{64,0},{96,32},{128,192},{160,224},{192,128},{224,1... | collective-permute-start | bytes 196616 | tf_op jit(solution)/shard_map/ppermute | solution.py:238
  49.7 1.7 %collective-permute-done.4 = f32[64,256]{1,0:T(8,128)S(1)} collective-permute-done((f32[64,256]{1,0:T(8,128)S(1)}, f32[64,256]{1,0:T(8,128)S(1)}, u32[]{:S(2)}, u32[]{:S(2)}) %collective-permute-start.4) | collective-permute-done | bytes 65568 | tf_op jit(solution)/shard_map/ppermute | solution.py:238
  51.4 3.0 %collective-permute-start.5 = (bf16[64,256]{1,0:T(8,128)(2,1)S(1)}, bf16[64,256]{1,0:T(8,128)(2,1)S(1)}, u32[]{:S(2)}, u32[]{:S(2)}) collective-permute-start(bf16[64,256]{1,0:T(8,128)(2,1)S(1)} %multiply_convert_fusion.own_ref), channel_id=1, source_target_pairs={{0,16},{16,0},{1,17},{17,1},{2,18},{18,2},{3,19},{19,3},{4,20},{20... | collective-permute-start | bytes 98312 | tf_op jit(solution)/shard_map/ppermute | solution.py:233
  54.4 0.2 unpack.1.parts_ref
  54.6 0.6 collective-permute-done.5.near_ref
  55.2 1.5 %refits_last.1 = (f32[64,256]{1,0:T(8,128)S(1)}, f32[64,256]{1,0:T(8,128)S(1)}, f32[2,128,256]{2,1,0:T(8,128)S(1)}, f32[2,128,128]{2,1,0:T(8,128)S(1)}, f32[2,8,128]{2,1,0:T(8,128)S(1)}) custom-call(bf16[2,3,256,256]{3,2,1,0:T(8,128)(2,1)S(1)} %unpack.1.parts_ref, bf16[64,256]{1,0:T(8,128)(2,1)S(1)} %multiply_convert_fusion.own_ref, ...), custom_call_target="tpu_custom_call" | custom-call | tf_op jit(solution)/shard_map/refits_last/pallas_call | solution.py:204
  56.7 0.4 collective-permute-start.6
  57.1 0.9 %collective-permute-done.6 = f32[64,256]{1,0:T(8,128)S(1)} collective-permute-done((f32[64,256]{1,0:T(8,128)S(1)}, f32[64,256]{1,0:T(8,128)S(1)}, u32[]{:S(2)}, u32[]{:S(2)}) %collective-permute-start.6) | collective-permute-done | bytes 65568 | tf_op jit(solution)/shard_map/ppermute | solution.py:233
  58.0 1.2 %collective-permute-start.9 = (f32[64,256]{1,0:T(8,128)S(1)}, f32[64,256]{1,0:T(8,128)S(1)}, u32[]{:S(2)}, u32[]{:S(2)}) collective-permute-start(f32[64,256]{1,0:T(8,128)S(1)} %add.14.own_ref), channel_id=1, source_target_pairs={{0,224},{32,192},{64,160},{96,128},{128,96},{160,64},{192,32},{224... | collective-permute-start | bytes 196616 | tf_op jit(solution)/shard_map/ppermute | solution.py:238
  59.2 3.2 %collective-permute-start.8 = (f32[64,256]{1,0:T(8,128)S(1)}, f32[64,256]{1,0:T(8,128)S(1)}, u32[]{:S(2)}, u32[]{:S(2)}) collective-permute-start(f32[64,256]{1,0:T(8,128)S(1)} %add.14.own_ref), channel_id=1, source_target_pairs={{0,192},{32,224},{64,128},{96,160},{128,64},{160,96},{192,0},{224,... | collective-permute-start | bytes 196616 | tf_op jit(solution)/shard_map/ppermute | solution.py:238
  62.4 0.0 collective-permute-start.7
  62.4 0.1 collective-permute-done.9.next_ref
  62.5 3.6 %collective-permute-done.8.far_ref = f32[64,256]{1,0:T(8,128)S(1)} collective-permute-done((f32[64,256]{1,0:T(8,128)S(1)}, f32[64,256]{1,0:T(8,128)S(1)}, u32[]{:S(2)}, u32[]{:S(2)}) %collective-permute-start.8) | collective-permute-done | bytes 65568 | tf_op jit(solution)/shard_map/ppermute | solution.py:238
  66.1 0.3 collective-permute-done.7.near_ref
  66.5 3.2 %collective-permute-start.10 = (f32[64,256]{1,0:T(8,128)S(1)}, f32[64,256]{1,0:T(8,128)S(1)}, u32[]{:S(2)}, u32[]{:S(2)}) collective-permute-start(f32[64,256]{1,0:T(8,128)S(1)} %four.3), channel_id=1, source_target_pairs={{0,64},{32,96},{64,0},{96,32},{128,192},{160,224},{192,128},{224,1... | collective-permute-start | bytes 196616 | tf_op jit(solution)/shard_map/ppermute | solution.py:238
  69.7 1.7 %collective-permute-done.10 = f32[64,256]{1,0:T(8,128)S(1)} collective-permute-done((f32[64,256]{1,0:T(8,128)S(1)}, f32[64,256]{1,0:T(8,128)S(1)}, u32[]{:S(2)}, u32[]{:S(2)}) %collective-permute-start.10) | collective-permute-done | bytes 65568 | tf_op jit(solution)/shard_map/ppermute | solution.py:238
  71.3 3.3 %collective-permute-start.11 = (f32[64,256]{1,0:T(8,128)S(1)}, f32[64,256]{1,0:T(8,128)S(1)}, u32[]{:S(2)}, u32[]{:S(2)}) collective-permute-start(f32[64,256]{1,0:T(8,128)S(1)} %add_multiply_fusion.own_ref), channel_id=1, source_target_pairs={{0,16},{16,0},{1,17},{17,1},{2,18},{18,2},{3,19},{19,3},{4,20},{20... | collective-permute-start | bytes 196616 | tf_op jit(solution)/shard_map/ppermute | solution.py:233
  74.6 1.0 %project.1 = f32[2,240,128]{2,1,0:T(8,128)} custom-call(f32[2,128,256]{2,1,0:T(8,128)S(1)} %get-tuple-element.28.before_ref, f32[2,128,128]{2,1,0:T(8,128)S(1)} %get-tuple-element.29.current_ref, f32[2,8,128]{2,1,0:T(8,128)S(1)} %get-tuple-element.30.scales_ref), custom_call_target="tpu_custom_call" | custom-call | tf_op jit(solution)/shard_map/project/pallas_call | solution.py:204
  75.6 0.0 collective-permute-done.11.near_ref
  75.6 0.8 %whole.1 = f32[240,128]{1,0:T(8,128)} custom-call(f32[64,256]{1,0:T(8,128)S(1)} %add_multiply_fusion.own_ref, f32[64,256]{1,0:T(8,128)S(1)} %collective-permute-done.11.near_ref), custom_call_target="tpu_custom_call" | custom-call | tf_op jit(solution)/shard_map/whole/pallas_call | solution.py:204
  (8 shorter events, 0.1 us)
Async XLA Ops:
  30.9 4.2 %collective-permute-start = (f32[64,256]{1,0:T(8,128)S(1)}, f32[64,256]{1,0:T(8,128)S(1)}, u32[]{:S(2)}, u32[]{:S(2)}) collective-permute-start(f32[64,256]{1,0:T(8,128)S(1)} %get-tuple-element.20), channel_id=1, source_target_pairs={{0,16},{16,0},{1,17},{17,1},{2,18},{18,2},{3,19},{19,3},{4,20},{20... | collective-permute-start | bytes 196616 | tf_op jit(solution)/shard_map/ppermute | solution.py:233
  35.1 9.2 %collective-permute-start.3 = (f32[64,256]{1,0:T(8,128)S(1)}, f32[64,256]{1,0:T(8,128)S(1)}, u32[]{:S(2)}, u32[]{:S(2)}) collective-permute-start(f32[64,256]{1,0:T(8,128)S(1)} %add.12.own_ref), channel_id=1, source_target_pairs={{0,224},{32,192},{64,160},{96,128},{128,96},{160,64},{192,32},{224... | collective-permute-start | bytes 196616 | tf_op jit(solution)/shard_map/ppermute | solution.py:238
  40.8 5.2 %collective-permute-start.2 = (f32[64,256]{1,0:T(8,128)S(1)}, f32[64,256]{1,0:T(8,128)S(1)}, u32[]{:S(2)}, u32[]{:S(2)}) collective-permute-start(f32[64,256]{1,0:T(8,128)S(1)} %add.12.own_ref), channel_id=1, source_target_pairs={{0,192},{32,224},{64,128},{96,160},{128,64},{160,96},{192,0},{224,... | collective-permute-start | bytes 196616 | tf_op jit(solution)/shard_map/ppermute | solution.py:238
  41.3 5.8 %collective-permute-start.1 = (f32[64,256]{1,0:T(8,128)S(1)}, f32[64,256]{1,0:T(8,128)S(1)}, u32[]{:S(2)}, u32[]{:S(2)}) collective-permute-start(f32[64,256]{1,0:T(8,128)S(1)} %add.12.own_ref), channel_id=1, source_target_pairs={{0,32},{32,0},{64,96},{96,64},{128,160},{160,128},{192,224},{224,1... | collective-permute-start | bytes 196616 | tf_op jit(solution)/shard_map/ppermute | solution.py:238
  47.1 4.3 %collective-permute-start.4 = (f32[64,256]{1,0:T(8,128)S(1)}, f32[64,256]{1,0:T(8,128)S(1)}, u32[]{:S(2)}, u32[]{:S(2)}) collective-permute-start(f32[64,256]{1,0:T(8,128)S(1)} %four.2), channel_id=1, source_target_pairs={{0,64},{32,96},{64,0},{96,32},{128,192},{160,224},{192,128},{224,1... | collective-permute-start | bytes 196616 | tf_op jit(solution)/shard_map/ppermute | solution.py:238
  51.4 3.8 %collective-permute-start.5 = (bf16[64,256]{1,0:T(8,128)(2,1)S(1)}, bf16[64,256]{1,0:T(8,128)(2,1)S(1)}, u32[]{:S(2)}, u32[]{:S(2)}) collective-permute-start(bf16[64,256]{1,0:T(8,128)(2,1)S(1)} %multiply_convert_fusion.own_ref), channel_id=1, source_target_pairs={{0,16},{16,0},{1,17},{17,1},{2,18},{18,2},{3,19},{19,3},{4,20},{20... | collective-permute-start | bytes 98312 | tf_op jit(solution)/shard_map/ppermute | solution.py:233
  56.7 1.3 %collective-permute-start.6 = (f32[64,256]{1,0:T(8,128)S(1)}, f32[64,256]{1,0:T(8,128)S(1)}, u32[]{:S(2)}, u32[]{:S(2)}) collective-permute-start(f32[64,256]{1,0:T(8,128)S(1)} %get-tuple-element.24), channel_id=1, source_target_pairs={{0,16},{16,0},{1,17},{17,1},{2,18},{18,2},{3,19},{19,3},{4,20},{20... | collective-permute-start | bytes 196616 | tf_op jit(solution)/shard_map/ppermute | solution.py:233
  58.0 4.4 %collective-permute-start.9 = (f32[64,256]{1,0:T(8,128)S(1)}, f32[64,256]{1,0:T(8,128)S(1)}, u32[]{:S(2)}, u32[]{:S(2)}) collective-permute-start(f32[64,256]{1,0:T(8,128)S(1)} %add.14.own_ref), channel_id=1, source_target_pairs={{0,224},{32,192},{64,160},{96,128},{128,96},{160,64},{192,32},{224... | collective-permute-start | bytes 196616 | tf_op jit(solution)/shard_map/ppermute | solution.py:238
  59.2 6.9 %collective-permute-start.8 = (f32[64,256]{1,0:T(8,128)S(1)}, f32[64,256]{1,0:T(8,128)S(1)}, u32[]{:S(2)}, u32[]{:S(2)}) collective-permute-start(f32[64,256]{1,0:T(8,128)S(1)} %add.14.own_ref), channel_id=1, source_target_pairs={{0,192},{32,224},{64,128},{96,160},{128,64},{160,96},{192,0},{224,... | collective-permute-start | bytes 196616 | tf_op jit(solution)/shard_map/ppermute | solution.py:238
  62.4 4.1 %collective-permute-start.7 = (f32[64,256]{1,0:T(8,128)S(1)}, f32[64,256]{1,0:T(8,128)S(1)}, u32[]{:S(2)}, u32[]{:S(2)}) collective-permute-start(f32[64,256]{1,0:T(8,128)S(1)} %add.14.own_ref), channel_id=1, source_target_pairs={{0,32},{32,0},{64,96},{96,64},{128,160},{160,128},{192,224},{224,1... | collective-permute-start | bytes 196616 | tf_op jit(solution)/shard_map/ppermute | solution.py:238
  66.5 4.9 %collective-permute-start.10 = (f32[64,256]{1,0:T(8,128)S(1)}, f32[64,256]{1,0:T(8,128)S(1)}, u32[]{:S(2)}, u32[]{:S(2)}) collective-permute-start(f32[64,256]{1,0:T(8,128)S(1)} %four.3), channel_id=1, source_target_pairs={{0,64},{32,96},{64,0},{96,32},{128,192},{160,224},{192,128},{224,1... | collective-permute-start | bytes 196616 | tf_op jit(solution)/shard_map/ppermute | solution.py:238
  71.3 4.3 %collective-permute-start.11 = (f32[64,256]{1,0:T(8,128)S(1)}, f32[64,256]{1,0:T(8,128)S(1)}, u32[]{:S(2)}, u32[]{:S(2)}) collective-permute-start(f32[64,256]{1,0:T(8,128)S(1)} %add_multiply_fusion.own_ref), channel_id=1, source_target_pairs={{0,16},{16,0},{1,17},{17,1},{2,18},{18,2},{3,19},{19,3},{4,20},{20... | collective-permute-start | bytes 196616 | tf_op jit(solution)/shard_map/ppermute | solution.py:233
